TPU v7x, 32 devices: a whole 2x2x4 slice. The times are simulated.
32 devices in a mesh: dp: 8 (over z, x), head: 4 (over y, core).
Axes of the slice: x: 2, y: 2, z: 4, core: 2. Of those that a mesh axis runs over, the one named last changes fastest.
Arguments:
- tokens: bfloat16 [48, 512, 768], P('dp'), may hold values from -6 to 6
- query_weight: bfloat16 [768, 768], P('dp', 'head'), may hold values from -0.21875 to 0.21875
- query_bias: float32 [768], P('head'), may hold values from -3 to 3
- key_weight: bfloat16 [768, 768], P('dp', 'head'), may hold values from -0.21875 to 0.21875
- value_weight: bfloat16 [768, 768], P('dp', 'head'), may hold values from -0.21875 to 0.21875
- value_bias: float32 [768], P('head'), may hold values from -0.3125 to 0.3125
- out_weight: bfloat16 [768, 768], P('head', 'dp'), may hold values from -2.5 to 2.5
- out_bias: float32 [768], replicated, may hold values from -1.75 to 1.75
- first_gain: float32 [768], replicated, may hold values from 0.25 to 1.75
- first_shift: float32 [768], replicated, may hold values from -1.75 to 1.75
- up_weight: bfloat16 [768, 3072], P('dp', 'head'), may hold values from -0.21875 to 0.21875
- up_bias: float32 [3072], P('head'), may hold values from -1.75 to 1.75
- down_weight: bfloat16 [3072, 768], P('head', 'dp'), may hold values from -0.109375 to 0.109375
- down_bias: float32 [768], replicated, may hold values from -1.75 to 1.75
- second_gain: float32 [768], replicated, may hold values from 0.25 to 1.75
- second_shift: float32 [768], replicated, may hold values from -1.75 to 1.75
- block_order: int32 [12], P('head'), may hold values from 0 to 1, as said below
- masked_rows: int32 [48, 128], P('dp'), may hold values from -1 to 511, as said below
- out_grad: bfloat16 [48, 128, 768], P('dp'), may hold values from -6 to 6
Outputs:
- out_y: bfloat16 [48, 512, 768], P('dp', 'head')
- grad_x: bfloat16 [48, 512, 768], P('dp', 'head')
- grad_query_weight: float32 [768, 768], P('dp', 'head')
- grad_query_bias: float32 [768], replicated
- grad_key_weight: float32 [768, 768], P('dp', 'head')
- grad_value_weight: float32 [768, 768], P('dp', 'head')
- grad_value_bias: float32 [768], replicated
- grad_out_weight: float32 [768, 768], P('head', 'dp')
- grad_out_bias: float32 [768], replicated
- grad_first_gain: float32 [768], replicated
- grad_first_shift: float32 [768], replicated
- grad_up_weight: float32 [768, 3072], P('dp', 'head')
- grad_up_bias: float32 [3072], replicated
- grad_down_weight: float32 [3072, 768], P('head', 'dp')
- grad_down_bias: float32 [768], replicated
- grad_second_gain: float32 [768], replicated
- grad_second_shift: float32 [768], replicated
Inputs may be any that keep to these rules, and one draw needn't show every extreme that they name: `block_order`: exactly 6 entries are 1, the others 0. `masked_rows`: each row lists distinct positions of its query block in any order, -1 marking an empty slot. Of each aligned run of 128 positions of a block at least one and at most 32 are listed, and some run lists exactly 32.
All inputs are finite; a program needn't handle non-finite values.
Results may differ from a plain program's by a relative error of at most 0.015.
The roundings to bfloat16 on the way count: a program that leaves them out, or rounds other values in their place, can miss the bound.
Values may be sent and summed in bfloat16 or wider, within the bound.
A program may use at most 128 MiB of HBM per device.

v0:
```python
import jax
import jax.numpy as jnp
from jax import lax
from jax.sharding import PartitionSpec as P

HEADS = 12
HD = 64
FF = 3072


EPSILON = 1e-12


def from_behind(block, axis, distance):
    devices = range(lax.axis_size(axis))
    route = [((i - distance) % len(devices), i) for i in devices]
    return lax.ppermute(block, axis, route)


def normalize(row_sums, norm_gain, norm_shift):
    centered = row_sums - jnp.mean(row_sums, axis=-1, keepdims=True)
    inverse = lax.rsqrt(jnp.mean(centered * centered, axis=-1, keepdims=True) + EPSILON)
    normed = centered * inverse
    return (normed * norm_gain + norm_shift, normed, inverse)


def norm_back(incoming, normed, inverse, norm_gain):
    scaled = incoming * norm_gain
    return inverse * (
        scaled
        - jnp.mean(scaled, axis=-1, keepdims=True)
        - normed * jnp.mean(scaled * normed, axis=-1, keepdims=True)
    )


def gelu_exact(inputs_in):
    return jax.nn.gelu(inputs_in, approximate=False)


def matmul(operand, weights):
    return jnp.dot(operand, weights, preferred_element_type=jnp.float32)


def matmul_by_rows(operand, right_side):
    return lax.dot_general(
        operand, right_side, (((0,), (0,)), ((), ())), preferred_element_type=jnp.float32
    )


def matmul_by_cols(operand, weights):
    return lax.dot_general(
        operand, weights, (((1,), (1,)), ((), ())), preferred_element_type=jnp.float32
    )


def take_one(lookup, indices):
    return lookup[indices]


def take_rows(lookup, indices):
    return jax.vmap(take_one)(lookup, indices)


def per_device(
    tokens,
    query_weight,
    query_bias,
    key_weight,
    value_weight,
    value_bias,
    out_weight,
    out_bias,
    first_gain,
    first_shift,
    up_weight,
    up_bias,
    down_weight,
    down_bias,
    second_gain,
    second_shift,
    block_order,
    masked_rows,
    out_grad,
):
    block_count, block_rows, model_width = tokens.shape
    head_parts = lax.axis_size("head")
    row_share = block_rows // head_parts
    head_index = lax.axis_index("head")
    slot_count = masked_rows.shape[1]
    partner = lax.axis_size("dp") // 2
    w_query, w_key, w_value, w_out, w_up, w_down = (
        lax.all_gather(query_weight, "dp", axis=0, tiled=True),
        lax.all_gather(key_weight, "dp", axis=0, tiled=True),
        lax.all_gather(value_weight, "dp", axis=0, tiled=True),
        lax.all_gather(out_weight, "dp", axis=1, tiled=True),
        lax.all_gather(up_weight, "dp", axis=0, tiled=True),
        lax.all_gather(down_weight, "dp", axis=1, tiled=True),
    )
    local_width = w_query.shape[1]
    heads_here = local_width // HD
    score_scale = HD ** (-0.5)
    flattened = tokens.reshape(block_count * block_rows, model_width)
    head_shape = (block_count, block_rows, heads_here, HD)
    queries = (
        (matmul(flattened, w_query) + query_bias)
        .astype(jnp.bfloat16)
        .reshape(block_count, block_rows, local_width)
    )
    key_near = (
        matmul(flattened, w_key).astype(jnp.bfloat16).reshape(block_count, block_rows, local_width)
    )
    value_near = (
        (matmul(flattened, w_value) + value_bias)
        .astype(jnp.bfloat16)
        .reshape(block_count, block_rows, local_width)
    )
    key_far, value_far = from_behind((key_near, value_near), "dp", partner)
    swapped = (block_order == 1)[None, None, :, None]
    keys_used = jnp.where(swapped, key_far.reshape(head_shape), key_near.reshape(head_shape))
    values_used = jnp.where(swapped, value_far.reshape(head_shape), value_near.reshape(head_shape))

    def attend(block_items):
        query_rows, key_rows, value_rows = block_items
        scores = (
            jnp.einsum("qhd,khd->hqk", query_rows, key_rows, preferred_element_type=jnp.float32)
            * score_scale
        )
        highest = jnp.max(scores, axis=-1, keepdims=True)
        raised = jnp.exp(scores - highest)
        totals = jnp.sum(raised, axis=-1, keepdims=True)
        probs_low = (raised / totals).astype(jnp.bfloat16)
        mixed = jnp.einsum(
            "hqk,khd->qhd", probs_low, value_rows, preferred_element_type=jnp.float32
        )
        return (mixed.astype(jnp.bfloat16), jnp.transpose((highest + jnp.log(totals))[:, :, 0]))

    attention_heads, log_totals = lax.map(
        attend, (queries.reshape(head_shape), keys_used, values_used)
    )
    attention = attention_heads.reshape(block_count, block_rows, local_width)
    branch_term = matmul(attention.reshape(-1, local_width), w_out).reshape(
        block_count, block_rows, model_width
    )
    branch_out = lax.psum_scatter(branch_term, "head", scatter_dimension=1, tiled=True)
    own_tokens = lax.dynamic_slice_in_dim(tokens, head_index * row_share, row_share, 1).astype(
        jnp.float32
    )
    hidden, normed_one, inverse_one = normalize(
        own_tokens + branch_out + out_bias, first_gain, first_shift
    )
    hidden_low = lax.all_gather(hidden.astype(jnp.bfloat16), "head", axis=1, tiled=True)
    pre_gelu = matmul(hidden_low.reshape(-1, model_width), w_up) + up_bias
    activated = gelu_exact(pre_gelu).astype(jnp.bfloat16)
    feed_term = matmul(activated, w_down).reshape(block_count, block_rows, model_width)
    feed_out = lax.psum_scatter(feed_term, "head", scatter_dimension=1, tiled=True) + down_bias
    result, normed_two, inverse_two = normalize(hidden + feed_out, second_gain, second_shift)
    out_y = result.astype(jnp.bfloat16)
    positions = jnp.arange(block_rows, dtype=jnp.int32)
    matches = masked_rows[:, None, :] == positions[None, :, None]
    is_listed = jnp.any(matches, axis=2)
    entry_index = jnp.sum(
        jnp.where(matches, jnp.arange(slot_count, dtype=jnp.int32)[None, None, :], 0), axis=2
    )
    own_listed = lax.dynamic_slice_in_dim(is_listed, head_index * row_share, row_share, 1)
    own_entry = lax.dynamic_slice_in_dim(entry_index, head_index * row_share, row_share, 1)
    grad_y = jnp.where(
        own_listed[..., None], take_rows(out_grad, own_entry).astype(jnp.float32), 0.0
    )
    d_second = norm_back(grad_y, normed_two, inverse_two, second_gain)
    g_second_gain = jnp.sum(grad_y * normed_two, axis=(0, 1))
    g_second_shift = jnp.sum(grad_y, axis=(0, 1))
    d_feed = d_second.astype(jnp.bfloat16)
    g_down_bias = jnp.sum(d_feed.astype(jnp.float32), axis=(0, 1))
    d_feed_all = lax.all_gather(d_feed, "head", axis=1, tiled=True)
    rows_count = d_feed_all.shape[1]
    hidden_width = w_up.shape[1]
    pre_used = pre_gelu.reshape(block_count, block_rows, hidden_width).reshape(-1, hidden_width)
    activated_used = activated.reshape(block_count, block_rows, hidden_width).reshape(
        -1, hidden_width
    )
    hidden_used = hidden_low.reshape(-1, model_width)
    d_feed_flat = d_feed_all.reshape(-1, model_width)
    d_activated = matmul_by_cols(d_feed_flat, w_down)
    unused_value, gelu_backward = jax.vjp(gelu_exact, pre_used)
    d_pre = gelu_backward(d_activated)[0].astype(jnp.bfloat16)
    g_down = matmul_by_rows(activated_used, d_feed_flat)
    g_up = matmul_by_rows(hidden_used, d_pre)
    g_up_bias = jnp.sum(d_pre.astype(jnp.float32), axis=0)
    d_hidden_term = matmul_by_cols(d_pre, w_up).reshape(block_count, rows_count, model_width)
    d_hidden_own = lax.psum_scatter(d_hidden_term, "head", scatter_dimension=1, tiled=True)
    d_hidden = d_second + d_hidden_own
    g_first_gain = jnp.sum(d_hidden * normed_one, axis=(0, 1))
    g_first_shift = jnp.sum(d_hidden, axis=(0, 1))
    d_first = norm_back(d_hidden, normed_one, inverse_one, first_gain)
    d_branch = d_first.astype(jnp.bfloat16)
    g_out_bias = jnp.sum(d_branch.astype(jnp.float32), axis=(0, 1))
    d_branch_all = lax.all_gather(d_branch, "head", axis=1, tiled=True)
    d_branch_flat = d_branch_all.reshape(-1, model_width)
    attention_used = attention.reshape(-1, local_width)
    g_out = matmul_by_rows(attention_used, d_branch_flat)
    d_attention = (
        matmul_by_cols(d_branch_flat, w_out)
        .astype(jnp.bfloat16)
        .reshape(block_count, rows_count, heads_here, HD)
    )
    queries_used = queries.reshape(block_count, rows_count, heads_here, HD)

    def attend_back(block_items):
        query_rows, key_rows, value_rows, grad_rows, log_rows = block_items
        scores = (
            jnp.einsum("qhd,khd->hqk", query_rows, key_rows, preferred_element_type=jnp.float32)
            * score_scale
        )
        probs = jnp.exp(scores - jnp.transpose(log_rows)[:, :, None])
        d_probs = jnp.einsum(
            "qhd,khd->hqk", grad_rows, value_rows, preferred_element_type=jnp.float32
        )
        d_scores = (probs * (d_probs - jnp.sum(d_probs * probs, axis=-1, keepdims=True))).astype(
            jnp.bfloat16
        )
        d_query_rows = (
            jnp.einsum("hqk,khd->qhd", d_scores, key_rows, preferred_element_type=jnp.float32)
            * score_scale
        ).astype(jnp.bfloat16)
        d_key_rows = (
            jnp.einsum("hqk,qhd->khd", d_scores, query_rows, preferred_element_type=jnp.float32)
            * score_scale
        ).astype(jnp.bfloat16)
        d_value_rows = jnp.einsum(
            "hqk,qhd->khd",
            probs.astype(jnp.bfloat16),
            grad_rows,
            preferred_element_type=jnp.float32,
        ).astype(jnp.bfloat16)
        return (d_query_rows, d_key_rows, d_value_rows)

    d_queries, d_keys_used, d_values_used = lax.map(
        attend_back, (queries_used, keys_used, values_used, d_attention, log_totals)
    )
    far_keys, far_values = from_behind(
        (jnp.where(swapped, d_keys_used, 0), jnp.where(swapped, d_values_used, 0)), "dp", partner
    )
    d_keys = (jnp.where(swapped, 0, d_keys_used) + far_keys).reshape(
        block_count, block_rows, local_width
    )
    d_values = (jnp.where(swapped, 0, d_values_used) + far_values).reshape(
        block_count, block_rows, local_width
    )
    d_queries_rows = d_queries.reshape(block_count, rows_count, local_width)
    stacked = jnp.concatenate((d_queries_rows, d_keys, d_values), axis=2)
    joined_weights = jnp.concatenate((w_query, w_key, w_value), axis=1)
    input_term = matmul_by_cols(stacked.reshape(-1, 3 * local_width), joined_weights).reshape(
        block_count, block_rows, model_width
    )
    input_own = lax.psum_scatter(input_term, "head", scatter_dimension=1, tiled=True)
    grad_x = (input_own + d_first).astype(jnp.bfloat16)
    tokens_used = tokens.reshape(-1, model_width)
    g_query = matmul_by_rows(tokens_used, d_queries_rows.reshape(-1, local_width))
    g_key = matmul_by_rows(flattened, d_keys.reshape(-1, local_width))
    g_value = matmul_by_rows(flattened, d_values.reshape(-1, local_width))
    g_query_bias = jnp.sum(d_queries_rows.astype(jnp.float32), axis=(0, 1))
    g_value_bias = jnp.sum(d_values.astype(jnp.float32), axis=(0, 1))
    s_query, s_key, s_value, s_out, s_up, s_down = (
        lax.psum_scatter(g_query, "dp", scatter_dimension=0, tiled=True),
        lax.psum_scatter(g_key, "dp", scatter_dimension=0, tiled=True),
        lax.psum_scatter(g_value, "dp", scatter_dimension=0, tiled=True),
        lax.psum_scatter(g_out, "dp", scatter_dimension=1, tiled=True),
        lax.psum_scatter(g_up, "dp", scatter_dimension=0, tiled=True),
        lax.psum_scatter(g_down, "dp", scatter_dimension=1, tiled=True),
    )

    def widen(piece, full_length):
        return lax.dynamic_update_slice_in_dim(
            jnp.zeros((full_length,), jnp.float32), piece, head_index * piece.shape[0], 0
        )

    (
        v_query_bias,
        v_value_bias,
        v_out_bias,
        v_first_gain,
        v_first_shift,
        v_up_bias,
        v_down_bias,
        v_second_gain,
        v_second_shift,
    ) = lax.psum(
        (
            widen(g_query_bias, HEADS * HD),
            widen(g_value_bias, HEADS * HD),
            g_out_bias,
            g_first_gain,
            g_first_shift,
            widen(g_up_bias, FF),
            g_down_bias,
            g_second_gain,
            g_second_shift,
        ),
        ("dp", "head"),
    )
    return (
        out_y,
        grad_x,
        s_query,
        v_query_bias,
        s_key,
        s_value,
        v_value_bias,
        s_out,
        v_out_bias,
        v_first_gain,
        v_first_shift,
        s_up,
        v_up_bias,
        s_down,
        v_down_bias,
        v_second_gain,
        v_second_shift,
    )


def solution(mesh):
    in_specs = (
        P("dp", None, None),
        P("dp", "head"),
        P("head"),
        P("dp", "head"),
        P("dp", "head"),
        P("head"),
        P("head", "dp"),
        P(),
        P(),
        P(),
        P("dp", "head"),
        P("head"),
        P("head", "dp"),
        P(),
        P(),
        P(),
        P("head"),
        P("dp", None),
        P("dp", None, None),
    )
    out_specs = (
        P("dp", "head", None),
        P("dp", "head", None),
        P("dp", "head"),
        P(),
        P("dp", "head"),
        P("dp", "head"),
        P(),
        P("head", "dp"),
        P(),
        P(),
        P(),
        P("dp", "head"),
        P(),
        P("head", "dp"),
        P(),
        P(),
        P(),
    )
    return jax.shard_map(
        per_device, mesh=mesh, in_specs=in_specs, out_specs=out_specs, check_vma=False
    )
```

profile of v0, /device:TPU:0, one launch (start us, length us, event | category | flops | bytes accessed | tf_op | source)
XLA Modules:
  0.0 1372.7 jit_solution(13289600110082354804)
XLA Ops:
  8.1 33.1 %all_gather.27 = bf16[768,192]{1,0:T(8,128)(2,1)S(1)} all-gather(bf16[96,192]{1,0:T(8,128)(2,1)} %param.27), channel_id=1, replica_groups=mesh['dp'=8,'head'=4] {'dp'}, dimensions={0}, use_global_device_ids=true | all-gather | bytes 331776 | tf_op jit(solution)/shard_map/all_gather | solution.py:94
  41.2 4.2 fusion.63
  46.6 69.0 %all_gather.29 = bf16[768,192]{1,0:T(8,128)(2,1)S(1)} all-gather(bf16[96,192]{1,0:T(8,128)(2,1)S(1)} %copy-done.19), channel_id=1, replica_groups=mesh['dp'=8,'head'=4] {'dp'}, dimensions={0}, use_global_device_ids=true | all-gather | bytes 331776 | tf_op jit(solution)/shard_map/all_gather | solution.py:93
  123.0 62.4 %all_gather.28 = bf16[768,192]{1,0:T(8,128)(2,1)S(1)} all-gather(bf16[96,192]{1,0:T(8,128)(2,1)S(1)} %copy-done.20), channel_id=1, replica_groups=mesh['dp'=8,'head'=4] {'dp'}, dimensions={0}, use_global_device_ids=true | all-gather | bytes 331776 | tf_op jit(solution)/shard_map/all_gather | solution.py:92
  185.4 4.2 fusion.64
  193.8 33.2 %all_gather.30 = bf16[192,768]{0,1:T(8,128)(2,1)} all-gather(bf16[192,96]{0,1:T(8,128)(2,1)S(1)} %copy.133), channel_id=1, replica_groups=mesh['dp'=8,'head'=4] {'dp'}, dimensions={1}, use_global_device_ids=true | all-gather | bytes 331776 | tf_op jit(solution)/shard_map/all_gather | solution.py:95
  234.5 24.9 %while.26 = (s32[]{:T(128)}, bf16[6,512,3,64]{1,3,2,0:T(8,128)(2,1)}, f32[6,512,3]{1,2,0:T(4,128)}, bf16[6,512,3,64]{1,3,2,0:T(8,128)(2,1)}, bf16[6,512,3,64]{1,...) while((s32[]{:T(128)}, bf16[6,512,3,64]{1,3,2,0:T(8,128)(2,1)}, ...), condition=%wide.region_3.4_spmd, body=%wide.region_0.3_spmd.sunk | while | flops 208501248 | bytes 10277453 | solution.py:137
  240.4 2.4 fusion.159
  259.4 7.3 fusion.91
  267.4 78.0 %reduce-scatter.19.cloned.1.call-done = f32[6,128,768]{2,1,0:T(8,128)} async-done(((f32[6,512,768]{2,1,0:T(8,128)}), f32[6,128,768]{2,1,0:T(8,128)}) %reduce-scatter.19.cloned.1.call-update) | async-done | bytes 2359312 | tf_op jit(solution)/shard_map/reduce_scatter | solution.py:144
  350.9 36.5 %all-gather.6.cloned.1.call-done = bf16[6,512,768]{2,1,0:T(8,128)(2,1)} async-done(((bf16[6,128,768]{2,1,0:T(8,128)(2,1)}), bf16[6,512,768]{2,1,0:T(8,128)(2,1)}) %all-gather.6.cloned.1.call-update) | async-done | bytes 4718608 | tf_op jit(solution)/shard_map/all_gather | solution.py:151
  387.4 26.9 %multiply_convert_fusion.1 = (bf16[3072,768]{1,0:T(8,128)(2,1)}, f32[3072,768]{1,0:T(8,128)}, f32[3072,768]{1,0:T(8,128)}) fusion(f32[768]{0:T(1024)S(1)} %copy-done.34, bf16[3072,768]{1,0:T(8,128)(2,1)} %bitcast.243, bf16[768,768]{1,0:T(8,128)(2,1)} %all-gather.8.cloned.1.call-done), kind=kOutput, calls=%fused_computation.65 | convolution fusion | flops 3779592192 | bytes 29494272 | tf_op jit(solution)/shard_map/dot_general | solution.py:41
  414.2 16.6 %all-gather.10.cloned.1.call-done = bf16[768,768]{0,1:T(8,128)(2,1)} async-done(((bf16[768,96]{0,1:T(8,128)(2,1)}), bf16[768,768]{0,1:T(8,128)(2,1)}) %all-gather.10.cloned.1.call-update) | async-done | bytes 1179664 | tf_op jit(solution)/shard_map/all_gather | solution.py:97
  430.8 10.3 fusion.107
  442.3 8.7 gather_fusion
  452.7 64.5 %reduce-scatter.21.cloned.1.call-done = f32[6,128,768]{2,1,0:T(8,128)} async-done(((f32[6,512,768]{2,1,0:T(8,128)}), f32[6,128,768]{2,1,0:T(8,128)}) %reduce-scatter.21.cloned.1.call-update) | async-done | bytes 2359312 | tf_op jit(solution)/shard_map/reduce_scatter | solution.py:155
  517.3 2.4 fusion.104
  523.8 2.4 convert_reduce_fusion.2
  526.4 37.5 %all-gather.12.cloned.1.call-done = bf16[6,512,768]{2,1,0:T(8,128)(2,1)} async-done(((bf16[6,128,768]{2,1,0:T(8,128)(2,1)}), bf16[6,512,768]{2,1,0:T(8,128)(2,1)}) %all-gather.12.cloned.1.call-update) | async-done | bytes 4718608 | tf_op jit(solution)/shard_map/all_gather | solution.py:174
  563.9 13.6 convert_reduce_fusion
  577.5 6.4 fusion.108
  584.0 77.9 %reduce-scatter.23.cloned.1.call-done = f32[6,128,768]{2,1,0:T(8,128)} async-done(((f32[6,512,768]{2,1,0:T(8,128)}), f32[6,128,768]{2,1,0:T(8,128)}) %reduce-scatter.23.cloned.1.call-update) | async-done | bytes 2359312 | tf_op jit(solution)/shard_map/reduce_scatter | solution.py:190
  661.9 5.7 multiply_reduce_fusion.2
  670.2 37.2 %all-gather.14.cloned.1.call-done = bf16[6,512,768]{2,1,0:T(8,128)(2,1)} async-done(((bf16[6,128,768]{2,1,0:T(8,128)(2,1)}), bf16[6,512,768]{2,1,0:T(8,128)(2,1)}) %all-gather.14.cloned.1.call-update) | async-done | bytes 4718608 | tf_op jit(solution)/shard_map/all_gather | solution.py:197
  707.4 4.1 convolution_convert_fusion
  713.8 2.8 copy.140
  719.0 65.1 %while.27 = (s32[]{:T(128)}, bf16[6,512,3,64]{1,3,2,0:T(8,128)(2,1)S(1)}, bf16[6,512,3,64]{1,3,2,0:T(8,128)(2,1)}, bf16[6,512,3,64]{1,3,2,0:T(8,128)(2,1)}, bf16...) while((s32[]{:T(128)}, ...), condition=%wide.region_19.20_spmd, body=%wide.region_17.19_spmd.sunk | while | flops 513243648 | bytes 25607272 | solution.py:237
  786.5 2.5 collective-permute-start.2
  789.0 51.9 %collective-permute-done.2 = bf16[6,512,3,64]{1,3,2,0:T(8,128)(2,1)S(1)} collective-permute-done((bf16[6,512,3,64]{1,3,2,0:T(8,128)(2,1)S(1)}, bf16[6,512,3,64]{1,3,2,0:T(8,128)(2,1)S(1)}, u32[]{:S(2)}, u32[]{:S(2)}) %collective-permute-start.2) | collective-permute-done | bytes 1179680 | tf_op jit(solution)/shard_map/ppermute | solution.py:17
  840.9 4.6 fusion.82
  849.3 2.8 convolution_bitcast_fusion
  859.9 47.1 %collective-permute-done.3 = bf16[6,512,3,64]{1,3,2,0:T(8,128)(2,1)} collective-permute-done((bf16[6,512,3,64]{1,3,2,0:T(8,128)(2,1)}, bf16[6,512,3,64]{1,3,2,0:T(8,128)(2,1)}, u32[]{:S(2)}, u32[]{:S(2)}) %collective-permute-start.3) | collective-permute-done | bytes 1179680 | tf_op jit(solution)/shard_map/ppermute | solution.py:17
  907.0 4.4 convert_reduce_fusion.1
  913.1 6.3 fusion.65
  919.5 9.1 fusion.110
  929.0 9.1 fusion.109
  939.3 4.2 convolution_bitcast_fusion.3
  947.8 5.7 convolution_bitcast_fusion.2
  953.5 2.4 copy.168
  958.0 4.3 convolution_bitcast_fusion.1
  974.5 39.9 %all-reduce = (f32[768]{0:T(1024)}, f32[768]{0:T(1024)}, f32[768]{0:T(1024)}, f32[768]{0:T(1024)}, f32[768]{0:T(1024)}, /*index=5*/f32[3072]{0:T(1024)}, f32[768]{0:T(1024)}, f32[768]{0:T(1024)}, f32[768]{0:T(1024)}) all-reduce(f32[768]{0:T(1024)} %dynamic_update_slice.26, ...), channel_id=1, replica_groups=mesh['dp'=8,'head'=4] {'dp','head'}, use_global_device_ids=true, to_apply=%region_23.24 | all-reduce | flops 9216 | bytes 73728 | tf_op jit(solution)/shard_map/psum | solution.py:287
  1014.4 5.3 reduce-scatter.25.cloned.1.call-done
  1019.7 3.6 add_convert_fusion.1
  1023.3 70.3 %reduce-scatter.29.cloned.1.call-done = f32[768,96]{0,1:T(8,128)} async-done(((f32[768,768]{0,1:T(8,128)}), f32[768,96]{0,1:T(8,128)}) %reduce-scatter.29.cloned.1.call-update) | async-done | bytes 294928 | tf_op jit(solution)/shard_map/reduce_scatter | solution.py:269
  1093.6 73.0 %reduce-scatter.27.cloned.1.call-done = f32[96,768]{1,0:T(8,128)} async-done(((f32[768,768]{1,0:T(8,128)}), f32[96,768]{1,0:T(8,128)}) %reduce-scatter.27.cloned.1.call-update) | async-done | bytes 294928 | tf_op jit(solution)/shard_map/reduce_scatter | solution.py:268
  1166.5 66.4 %reduce-scatter.31.cloned.1.call-done = f32[96,192]{1,0:T(8,128)} async-done(((f32[768,192]{1,0:T(8,128)}), f32[96,192]{1,0:T(8,128)}) %reduce-scatter.31.cloned.1.call-update) | async-done | bytes 73744
  1232.9 66.1 %reduce-scatter.33.cloned.1.call-done = f32[96,192]{1,0:T(8,128)} async-done(((f32[768,192]{1,0:T(8,128)}), f32[96,192]{1,0:T(8,128)}) %reduce-scatter.33.cloned.1.call-update) | async-done | bytes 73744
  1299.0 66.2 %reduce-scatter.35.cloned.1.call-done = f32[96,192]{1,0:T(8,128)} async-done(((f32[768,192]{1,0:T(8,128)}), f32[96,192]{1,0:T(8,128)}) %reduce-scatter.35.cloned.1.call-update) | async-done | bytes 73744
  (251 shorter events, 163.7 us)
Async XLA Ops:
  8.0 434.3 %copy-start = (bf16[6,128,768]{2,1,0:T(8,128)(2,1)S(1)}, bf16[6,128,768]{2,1,0:T(8,128)(2,1)}, u32[]{:S(2)}) copy-start(bf16[6,128,768]{2,1,0:T(8,128)(2,1)} %param.41) | copy-start | bytes 3538948
  8.0 337.4 %reduce-scatter.19.cloned.1.call-start = ((), (), s32[]{:S(2)}) async-start(), calls=%async_computation.10 | async-start | bytes 11796480 | tf_op jit(solution)/shard_map/reduce_scatter | solution.py:144
  8.1 107.5 %slice-start = ((s8[4718592]{0:T(1024)(128)(4,1)}), s8[4194304]{0:T(1024)(128)(4,1)S(1)}, s32[]{:S(2)}) async-start(s8[4718592]{0:T(1024)(128)(4,1)} %bitcast.215), calls=%async_computation.25 | async-start | bytes 8388608
  41.2 4.2 copy-start.12
  41.2 74.4 %slice-start.1 = ((s8[4718592]{0:T(1024)(128)(4,1)}), s8[524288]{0:T(1024)(128)(4,1)S(1)}, s32[]{:S(2)}) async-start(s8[4718592]{0:T(1024)(128)(4,1)} %bitcast.215), calls=%async_computation.26 | async-start | bytes 1048576
  46.6 180.5 %collective-permute-start = (bf16[6,512,192]{1,2,0:T(8,128)(2,1)}, bf16[6,512,192]{1,2,0:T(8,128)(2,1)}, u32[]{:S(2)}, u32[]{:S(2)}) collective-permute-start(bf16[6,512,192]{1,2,0:T(8,128)(2,1)} %bitcast.173), channel_id=1, source_target_pairs={{16,0},{20,4},{24,8},{28,12},{0,16},{4,20},{8,24},{12,28},{17,1},{... | collective-permute-start | bytes 3538952 | tf_op jit(solution)/shard_map/ppermute | solution.py:17
  118.4 67.0 %copy-start.35 = (f32[192]{0:T(256)S(1)}, f32[192]{0:T(256)}, u32[]{:S(2)}) copy-start(f32[192]{0:T(256)} %param.25) | copy-start | bytes 2308
  118.4 110.7 %collective-permute-start.1 = (bf16[6,512,192]{1,2,0:T(8,128)(2,1)}, bf16[6,512,192]{1,2,0:T(8,128)(2,1)}, u32[]{:S(2)}, u32[]{:S(2)}) collective-permute-start(bf16[6,512,192]{1,2,0:T(8,128)(2,1)} %bitcast.172), channel_id=1, source_target_pairs={{16,0},{20,4},{24,8},{28,12},{0,16},{4,20},{8,24},{12,28},{17,1},{... | collective-permute-start | bytes 3538952 | tf_op jit(solution)/shard_map/ppermute | solution.py:17
  185.4 4.2 copy-start.13
  189.6 4.1 copy-start.21
  189.6 37.4 %copy-start.36 = (s32[3]{0:T(128)S(1)}, s32[3]{0:T(128)}, u32[]{:S(2)}) copy-start(s32[3]{0:T(128)} %param.39) | copy-start | bytes 40
  227.0 4.1 copy-start.29
  227.0 4.1 copy-start.9
  227.0 4.1 copy-start.10
  259.4 7.3 copy-start.5
  259.4 7.3 copy-start.6
  266.7 78.7 %copy-start.32 = (f32[768]{0:T(1024)S(1)}, f32[768]{0:T(1024)}, u32[]{:S(2)}) copy-start(f32[768]{0:T(1024)} %param.30) | copy-start | bytes 9220
  266.8 84.1 %all-gather.8.cloned.1.call-start = ((), (), s32[]{:S(2)}) async-start(), calls=%async_computation.12 | async-start | bytes 1327104 | tf_op jit(solution)/shard_map/all_gather | solution.py:96
  267.4 120.0 %all-gather.6.cloned.1.call-start = ((), (), s32[]{:S(2)}) async-start(), calls=%async_computation.11 | async-start | bytes 5898240 | tf_op jit(solution)/shard_map/all_gather | solution.py:151
  348.5 38.9 %copy-start.34 = (f32[768]{0:T(1024)S(1)}, f32[768]{0:T(1024)}, u32[]{:S(2)}) copy-start(f32[768]{0:T(1024)} %param.34) | copy-start | bytes 9220
  349.9 80.9 %all-gather.10.cloned.1.call-start = ((), (), s32[]{:S(2)}) async-start(), calls=%async_computation.13 | async-start | bytes 1327104 | tf_op jit(solution)/shard_map/all_gather | solution.py:97
  350.5 166.8 %reduce-scatter.21.cloned.1.call-start = ((), (), s32[]{:S(2)}) async-start(), calls=%async_computation.14 | async-start | bytes 11796480 | tf_op jit(solution)/shard_map/reduce_scatter | solution.py:155
  441.1 122.8 %all-gather.12.cloned.1.call-start = ((), (), s32[]{:S(2)}) async-start(), calls=%async_computation.15 | async-start | bytes 5898240 | tf_op jit(solution)/shard_map/all_gather | solution.py:174
  519.7 4.1 copy-start.2
  520.2 6.1 copy-start.18
  523.8 2.4 copy-start.24
  523.8 2.4 copy-start.25
  526.3 135.6 %reduce-scatter.23.cloned.1.call-start = ((), (), s32[]{:S(2)}) async-start(), calls=%async_computation.16 | async-start | bytes 11796480 | tf_op jit(solution)/shard_map/reduce_scatter | solution.py:190
  563.9 13.6 copy-start.33
  577.5 6.4 copy-start.37
  583.9 123.5 %all-gather.14.cloned.1.call-start = ((), (), s32[]{:S(2)}) async-start(), calls=%async_computation.17 | async-start | bytes 5898240 | tf_op jit(solution)/shard_map/all_gather | solution.py:197
  667.6 2.4 copy-start.3
  667.6 2.4 copy-start.22
  670.0 300.1 %reduce-scatter.37.cloned.1.call-start = ((), (), s32[]{:S(2)}) async-start(), calls=%async_computation.24 | async-start | bytes 884736
  784.1 56.8 %copy-start.8 = (bf16[6,512,3,64]{1,3,2,0:T(8,128)(2,1)S(1)}, bf16[6,512,3,64]{1,3,2,0:T(8,128)(2,1)}, u32[]{:S(2)}) copy-start(bf16[6,512,3,64]{1,3,2,0:T(8,128)(2,1)} %get-tuple-element.102) | copy-start | bytes 3538948
  784.1 56.8 %copy-start.30 = (pred[3]{0:T(512)(128)(4,1)S(1)}, pred[3]{0:T(512)(128)(4,1)}, u32[]{:S(2)}) copy-start(pred[3]{0:T(512)(128)(4,1)} %copy-done.29) | copy-start | bytes 13
  786.5 54.4 %collective-permute-start.2 = (bf16[6,512,3,64]{1,3,2,0:T(8,128)(2,1)S(1)}, bf16[6,512,3,64]{1,3,2,0:T(8,128)(2,1)S(1)}, u32[]{:S(2)}, u32[]{:S(2)}) collective-permute-start(bf16[6,512,3,64]{1,3,2,0:T(8,128)(2,1)S(1)} %copy.144), channel_id=1, source_target_pairs={{16,0},{20,4},{24,8},{28,12},{0,16},{4,20},{8,24},{12,28},{17,1},{... | collective-permute-start | bytes 3538952 | tf_op jit(solution)/shard_map/ppermute | solution.py:17
  840.9 8.4 slice-start.2
  845.5 3.9 slice-start.3
  846.9 60.1 %collective-permute-start.3 = (bf16[6,512,3,64]{1,3,2,0:T(8,128)(2,1)}, bf16[6,512,3,64]{1,3,2,0:T(8,128)(2,1)}, u32[]{:S(2)}, u32[]{:S(2)}) collective-permute-start(bf16[6,512,3,64]{1,3,2,0:T(8,128)(2,1)} %copy.149), channel_id=1, source_target_pairs={{16,0},{20,4},{24,8},{28,12},{0,16},{4,20},{8,24},{12,28},{17,1},{... | collective-permute-start | bytes 3538952 | tf_op jit(solution)/shard_map/ppermute | solution.py:17
  852.2 167.5 %reduce-scatter.25.cloned.1.call-start = ((), (), s32[]{:S(2)}) async-start(), calls=%async_computation.18 | async-start | bytes 11796480 | tf_op jit(solution)/shard_map/reduce_scatter | solution.py:255
  858.1 48.9 %copy-start.31 = (pred[3]{0:T(512)(128)(4,1)S(1)}, pred[3]{0:T(512)(128)(4,1)}, u32[]{:S(2)}) copy-start(pred[3]{0:T(512)(128)(4,1)} %copy-done.29) | copy-start | bytes 13
  919.4 174.1 %reduce-scatter.29.cloned.1.call-start = ((), (), s32[]{:S(2)}) async-start(), calls=%async_computation.20 | async-start | bytes 2654208 | tf_op jit(solution)/shard_map/reduce_scatter | solution.py:269
  928.7 237.9 %reduce-scatter.27.cloned.1.call-start = ((), (), s32[]{:S(2)}) async-start(), calls=%async_computation.19 | async-start | bytes 2654208 | tf_op jit(solution)/shard_map/reduce_scatter | solution.py:268
  938.1 294.8 %reduce-scatter.31.cloned.1.call-start = ((), (), s32[]{:S(2)}) async-start(), calls=%async_computation.21 | async-start | bytes 884736
  945.8 353.2 %reduce-scatter.33.cloned.1.call-start = ((), (), s32[]{:S(2)}) async-start(), calls=%async_computation.22 | async-start | bytes 884736
  956.0 409.2 %reduce-scatter.35.cloned.1.call-start = ((), (), s32[]{:S(2)}) async-start(), calls=%async_computation.23 | async-start | bytes 884736
  974.5 390.7 %copy-start.1 = (bf16[6,128,768]{2,1,0:T(8,128)(2,1)S(1)}, bf16[6,128,768]{2,1,0:T(8,128)(2,1)}, u32[]{:S(2)}) copy-start(bf16[6,128,768]{2,1,0:T(8,128)(2,1)} %param.41) | copy-start | bytes 3538948
  (13 other events, 19.5 us)
Sparse Core Ops, SparseCore 0:
  266.9 78.4 reduce-scatter.18
  526.4 37.4 all-gather.11
  584.0 77.8 reduce-scatter.22
Sparse Core Ops, SparseCore 1:
  269.4 41.9 all-gather.7
  350.0 37.3 all-gather.5
  389.4 41.3 all-gather.9
  441.2 76.0 reduce-scatter.20
  670.1 37.3 all-gather.13
  852.3 86.8 reduce-scatter.36
  941.6 78.1 reduce-scatter.24
  1023.6 69.9 reduce-scatter.28
  1097.5 69.0 reduce-scatter.26
  1170.4 62.4 reduce-scatter.30
  1236.7 62.3 reduce-scatter.32
  1302.9 62.2 reduce-scatter.34
where the time goes:
time: 1380 us; the launch traced here: 1370 us
  waiting for transfers between devices  796 us (58%)
  blocking collectives  238 us (17%)
  matrix products  194 us (14%)
  local copies, waits for them, and re-layouts  75.5 us (5%)
  other arithmetic  49.1 us (4%)
  between operations  16.3 us (1%)
    unnamed x19, waiting for transfers between devices  200 us
    ppermute x4, waiting for transfers between devices, from_behind(): return lax.ppermute(block, axis, route)  99 us
    reduce_scatter x1, waiting for transfers between devices, per_device(): lax.psum_scatter(branch_term, 'head', scatter_dimension=1, tiled=True)  78 us
    reduce_scatter x1, waiting for transfers between devices, per_device(): lax.psum_scatter(d_hidden_term, 'head', scatter_dimension=1, tiled=True)  77.9 us
    reduce_scatter x1, waiting for transfers between devices, per_device(): lax.psum_scatter(g_up, 'dp', scatter_dimension=0, tiled=True)  73 us
    reduce_scatter x1, waiting for transfers between devices, per_device(): lax.psum_scatter(g_down, 'dp', scatter_dimension=1, tiled=True)  70.3 us
    all_gather x1, blocking collectives, per_device(): lax.all_gather(key_weight, 'dp', axis=0, tiled=True)  69 us
    reduce_scatter x1, waiting for transfers between devices, per_device(): lax.psum_scatter(feed_term, 'head', scatter_dimension=1, tiled=True)  64.5 us
  transfers between devices with their start and end apart: 19, of which 15 were waited for; matrix products, arithmetic and copies ran while one was open for 10% of the time, Pallas kernels for 0%

commit v1 on v0

v1 whole, which is shorter than its diff:
```python
import functools

import jax
import jax.numpy as jnp
from jax import lax
from jax.experimental import pallas as pl
from jax.experimental.pallas import tpu as pltpu
from jax.sharding import PartitionSpec as P

HEADS = 12
HD = 64
FF = 3072
EPSILON = 1e-12
F32 = jnp.float32
BF16 = jnp.bfloat16
SCALE = HD ** (-0.5)


def flip(block, axis, bit):
    n = lax.axis_size(axis)
    return lax.ppermute(block, axis, [(i, i ^ bit) for i in range(n)])


def shift(block, axis, distance):
    n = lax.axis_size(axis)
    return lax.ppermute(block, axis, [(i, (i + distance) % n) for i in range(n)])


def sibling(block):
    return flip(block, "head", 1)


def across(block):
    return flip(block, "head", 2)


def partner(block):
    return shift(block, "dp", lax.axis_size("dp") // 2)


def pick(array, index, axis=0):
    return lax.dynamic_index_in_dim(array, index, axis, keepdims=False)


def ordered(low, own, other, axis=0):
    return jnp.stack(
        (jnp.where(low == 0, own, other), jnp.where(low == 0, other, own)), axis=axis
    )


def mm(a, b):
    return jnp.dot(a, b, preferred_element_type=F32)


def mm_t(a, b):
    return lax.dot_general(a, b, (((1,), (1,)), ((), ())), preferred_element_type=F32)


def t_mm(a, b):
    return lax.dot_general(a, b, (((0,), (0,)), ((), ())), preferred_element_type=F32)


def norm_parts(rows):
    centered = rows - jnp.mean(rows, axis=-1, keepdims=True)
    inverse = lax.rsqrt(jnp.mean(centered * centered, axis=-1, keepdims=True) + EPSILON)
    return centered * inverse, inverse


def norm_back(incoming, normed, inverse, gain):
    scaled = incoming * gain
    return inverse * (
        scaled
        - jnp.mean(scaled, axis=-1, keepdims=True)
        - normed * jnp.mean(scaled * normed, axis=-1, keepdims=True)
    )


def gather(piece, x_first):
    n = lax.axis_size("dp")
    if n != 8:
        mine = lax.all_gather(piece, "dp", axis=0, tiled=False)
        return jnp.stack((mine, across(mine)))
    index = lax.axis_index("dp")
    z, x = index // 2, index % 2
    column = jnp.zeros((4,) + piece.shape, piece.dtype)
    column = lax.dynamic_update_index_in_dim(column, piece, z, 0)
    for k in (1, 2, 3):
        column = lax.dynamic_update_index_in_dim(
            column, shift(piece, "dp", 2 * k), (z - k) % 4, 0
        )
    if x_first:
        plane = ordered(x, column, flip(column, "dp", 1), axis=1)
        both = jnp.stack((plane, across(plane)))
    else:
        both = jnp.stack((column, across(column)))
        both = ordered(x, both, flip(both, "dp", 1), axis=2)
    return both.reshape((2, 8) + piece.shape)


def reduce_scatter(terms, x_last):
    n = lax.axis_size("dp")
    if n != 8:
        total = terms[0].astype(F32) + across(terms[1].astype(BF16)).astype(F32)
        return lax.psum_scatter(total, "dp", scatter_dimension=0, tiled=False)
    index = lax.axis_index("dp")
    z, x = index // 2, index % 2
    terms = terms.reshape((2, 4, 2) + terms.shape[2:])
    if x_last:
        arrived = across(terms[1])
        plane = (terms[0].astype(F32) + arrived.astype(F32)).astype(BF16)
        arrived = flip(pick(plane, 1 - x, 1), "dp", 1)
        column = pick(plane, x, 1).astype(F32) + arrived.astype(F32)
    else:
        arrived = flip(pick(terms, 1 - x, 2), "dp", 1)
        both = (pick(terms, x, 2).astype(F32) + arrived.astype(F32)).astype(BF16)
        column = both[0].astype(F32) + across(both[1]).astype(F32)
    column = column.astype(BF16)
    total = pick(column, z).astype(F32)
    for k in (1, 2, 3):
        total = total + shift(pick(column, (z + k) % 4), "dp", 2 * k).astype(F32)
    return total


def sum_all(vector):
    n = lax.axis_size("dp")
    if n != 8:
        return lax.psum(vector, ("dp", "head"))
    vector = vector + sibling(vector)
    vector = vector + across(vector)
    vector = vector + flip(vector, "dp", 1)
    return (vector + shift(vector, "dp", 4)) + (
        shift(vector, "dp", 2) + shift(vector, "dp", 6)
    )


def lane_masks(scale):
    lane = lax.broadcasted_iota(jnp.int32, (1, 2 * HD), 1)
    first = jnp.where(lane < HD, 1.0, 0.0)
    return [(first * scale).astype(BF16), ((1.0 - first) * scale).astype(BF16)]


def rows_of(ref):
    a, b, w = ref.shape
    return ref[...].reshape(a * b, w)


def pair_lanes(halves):
    lane = lax.broadcasted_iota(jnp.int32, halves[0].shape, 1)
    return jnp.where(lane < HD, halves[0], halves[1])


def attend_kernel(q_ref, k_ref, v_ref, o_ref):
    q, k, v = rows_of(q_ref), rows_of(k_ref), rows_of(v_ref)
    outs = []
    for mask in lane_masks(SCALE):
        s = mm_t(q * mask, k)
        raised = jnp.exp(s - jnp.max(s, axis=-1, keepdims=True))
        total = jnp.sum(raised, axis=-1, keepdims=True)
        outs.append(mm(raised.astype(BF16), v) / total)
    o_ref[...] = pair_lanes(outs).astype(BF16).reshape(o_ref.shape)


def query_back_kernel(q_ref, g_ref, k_ref, v_ref, dq_ref):
    q, g, k, v = rows_of(q_ref), rows_of(g_ref), rows_of(k_ref), rows_of(v_ref)
    outs = []
    for mask, one in zip(lane_masks(SCALE), lane_masks(1.0)):
        s = mm_t(q * mask, k)
        raised = jnp.exp(s - jnp.max(s, axis=-1, keepdims=True))
        probs = raised / jnp.sum(raised, axis=-1, keepdims=True)
        d_probs = mm_t(g * one, v)
        inner = jnp.sum(d_probs * probs, axis=-1, keepdims=True)
        d_scores = (probs * (d_probs - inner)).astype(BF16)
        outs.append(mm(d_scores, k) * SCALE)
    dq_ref[...] = pair_lanes(outs).astype(BF16).reshape(dq_ref.shape)


def key_back_kernel(q_ref, g_ref, k_ref, v_ref, dk_ref, dv_ref):
    q, g, k, v = rows_of(q_ref), rows_of(g_ref), rows_of(k_ref), rows_of(v_ref)
    d_keys, d_values = [], []
    for mask, one in zip(lane_masks(SCALE), lane_masks(1.0)):
        s = mm_t(k, q * mask)
        raised = jnp.exp(s - jnp.max(s, axis=0, keepdims=True))
        probs = raised / jnp.sum(raised, axis=0, keepdims=True)
        d_probs = mm_t(v, g * one)
        inner = jnp.sum(d_probs * probs, axis=0, keepdims=True)
        d_scores = (probs * (d_probs - inner)).astype(BF16)
        d_keys.append(mm(d_scores, q) * SCALE)
        d_values.append(mm(probs.astype(BF16), g))
    dk_ref[...] = pair_lanes(d_keys).astype(BF16).reshape(dk_ref.shape)
    dv_ref[...] = pair_lanes(d_values).astype(BF16).reshape(dv_ref.shape)


def per_head_pair(kernel, arrays, out_count, out_like, flops):
    _, blocks, _, width = arrays[0].shape

    def spec(array):
        return pl.BlockSpec(
            (2, None, array.shape[2], 2 * HD), lambda b, t: (0, b, 0, t)
        )

    shape = jax.ShapeDtypeStruct(out_like.shape, BF16)
    out = pl.pallas_call(
        kernel,
        grid=(blocks, width // (2 * HD)),
        in_specs=[spec(a) for a in arrays],
        out_specs=[spec(out_like)] * out_count,
        out_shape=[shape] * out_count,
        cost_estimate=pl.CostEstimate(
            flops=flops,
            transcendentals=0,
            bytes_accessed=2 * (sum(a.size for a in arrays) + out_count * out_like.size),
        ),
    )(*arrays)
    return out


def per_device(
    tokens,
    query_weight,
    query_bias,
    key_weight,
    value_weight,
    value_bias,
    out_weight,
    out_bias,
    first_gain,
    first_shift,
    up_weight,
    up_bias,
    down_weight,
    down_bias,
    second_gain,
    second_shift,
    block_order,
    masked_rows,
    out_grad,
):
    block_count, block_rows, width = tokens.shape
    quarter = block_rows // 4
    slots = masked_rows.shape[1]
    cap = slots // 4
    blocks = block_count // 2
    piece_rows = query_weight.shape[0]
    local = query_weight.shape[1]
    columns = 2 * local
    hidden_piece = up_weight.shape[1]
    head = lax.axis_index("head")
    c, p = head % 2, head // 2

    piece = jnp.concatenate((query_weight, key_weight, value_weight, out_weight.T), axis=1)
    half = piece_rows // 2
    w_one = gather(piece[:half], True)
    w_two = gather(piece[half:], False)
    w_attn = jnp.stack((w_one, w_two), axis=2).reshape(2, width, 4, local)
    w_attn = jnp.transpose(w_attn, (2, 1, 0, 3)).reshape(4, width, columns)
    w_query, w_key, w_value, w_out_t = (w_attn[i] for i in range(4))
    w_out_other = sibling(w_out_t)
    w_up = gather(up_weight, True).reshape(2, width, hidden_piece)
    w_down = gather(down_weight.T, False).reshape(2, width, hidden_piece)

    small = jnp.concatenate(
        (query_bias, value_bias, up_bias, block_order.astype(F32))
    )
    small_other = across(small)

    def both(start, size):
        return jnp.concatenate(
            (small[start : start + size], small_other[start : start + size])
        )

    b_query = both(0, local)
    b_value = both(local, local)
    b_up = jnp.stack((up_bias, small_other[2 * local : 2 * local + hidden_piece]))
    swapped = jnp.repeat(both(2 * local + hidden_piece, local // HD) > 0.5, HD)

    mine = pick(tokens.reshape(2, blocks, 2, 2, quarter, width), p)
    x_rows = jnp.stack((pick(mine, c, 2), pick(mine, 1 - c, 2)))
    x_flat = x_rows.reshape(-1, width)
    x_other = partner(x_rows).reshape(-1, width)
    own_count = x_flat.shape[0] // 2
    attn_shape = (2, blocks, 2 * quarter, columns)
    compact_shape = (2, blocks, 2 * cap, columns)

    listed = pick(masked_rows.reshape(2, blocks, slots), p)
    run = jnp.where(listed >= 0, listed // quarter, -1)
    earlier = jnp.arange(slots)[:, None] > jnp.arange(slots)[None, :]
    rank = jnp.sum((run[:, :, None] == run[:, None, :]) & earlier, axis=-1)
    which = jnp.stack((c, c + 2, 1 - c, 3 - c)).reshape(2, 1, 2, 1, 1)
    picks = (
        (run[None, :, None, None, :] == which)
        & (rank[None, :, None, None, :] == jnp.arange(cap)[:, None])
    ).astype(BF16)
    places = (listed[:, :, None] % quarter == jnp.arange(quarter)).astype(BF16)
    select = jnp.einsum(
        "sbeki,bir->sbekr", picks, places, preferred_element_type=F32
    ).astype(BF16)
    select = select.reshape(-1, cap, quarter)
    runs_own = 2 * blocks

    def compact(rows, which=slice(None), **kw):
        source = select[which]
        out = jnp.einsum(
            "ukr,urw->ukw",
            source.astype(rows.dtype),
            rows.reshape(source.shape[0], quarter, -1),
            preferred_element_type=F32,
            **kw,
        )
        return out.reshape(-1, rows.shape[-1])

    def spread(rows, which=slice(None), **kw):
        source = select[which]
        out = jnp.einsum(
            "ukr,ukw->urw",
            source.astype(rows.dtype),
            rows.reshape(source.shape[0], cap, -1),
            preferred_element_type=F32,
            **kw,
        )
        return out.reshape(-1, rows.shape[-1])

    own_runs, other_runs = slice(0, runs_own), slice(runs_own, None)
    exact = {"precision": lax.Precision.HIGHEST}
    grads_in = pick(out_grad.reshape(2, blocks, slots, width), p)
    grad_y = jnp.einsum(
        "beki,biw->bekw", picks[0], grads_in, preferred_element_type=F32
    ).reshape(-1, width)

    queries = (mm(x_flat, w_query) + b_query).astype(BF16)
    keys = mm(x_flat, w_key).astype(BF16)
    values = (mm(x_flat, w_value) + b_value).astype(BF16)
    keys_used = jnp.where(swapped, mm(x_other, w_key).astype(BF16), keys)
    values_used = jnp.where(
        swapped, (mm(x_other, w_value) + b_value).astype(BF16), values
    )
    unit_flops = 4 * block_rows * block_rows * columns * blocks
    (attention,) = per_head_pair(
        attend_kernel,
        [a.reshape(attn_shape) for a in (queries, keys_used, values_used)],
        1,
        queries.reshape(attn_shape),
        unit_flops,
    )
    q_compact = compact(queries).astype(BF16).reshape(compact_shape)
    q_far = partner(q_compact)
    swapped_lanes = swapped[None, None, None, :]
    attn_other = sibling(attention[1]).reshape(own_count, columns)
    branch = mm_t(attention[0].reshape(own_count, columns), w_out_t) + mm_t(
        attn_other, w_out_other
    )
    sum_one = x_flat[:own_count].astype(F32) + branch + out_bias
    hidden = norm_parts(sum_one)[0] * first_gain + first_shift
    hidden_low = hidden.astype(BF16)
    hidden_other = sibling(hidden_low)
    hidden_all = jnp.concatenate((hidden_low, hidden_other))

    def feed(i):
        pre = mm(hidden_all, w_up[i]) + b_up[i]
        activated = jax.nn.gelu(pre, approximate=False).astype(BF16)
        return mm_t(activated, w_down[i])

    feed_term = feed(0) + feed(1)
    feed_out = (
        feed_term[:own_count]
        + sibling(feed_term[own_count:].astype(BF16)).astype(F32)
        + down_bias
    )
    sum_two = hidden + feed_out
    out_rows = (norm_parts(sum_two)[0] * second_gain + second_shift).astype(BF16)

    def to_output(rows):
        rows = rows.reshape(blocks, 2, quarter, width)
        kept = pick(rows, p, 1)
        moved = across(pick(rows, 1 - p, 1))
        return ordered(p, kept, moved).reshape(block_count, quarter, width)

    out_y = to_output(out_rows)

    one_c = compact(sum_one, own_runs, **exact)
    two_c = compact(sum_two, own_runs, **exact)
    normed_two, inverse_two = norm_parts(two_c)
    normed_one, inverse_one = norm_parts(one_c)
    hidden_c = (normed_one * first_gain + first_shift).astype(BF16)
    d_second = norm_back(grad_y, normed_two, inverse_two, second_gain)
    g_second_gain = jnp.sum(grad_y * normed_two, axis=0)
    g_second_shift = jnp.sum(grad_y, axis=0)
    d_feed = d_second.astype(BF16)
    g_down_bias = jnp.sum(d_feed.astype(F32), axis=0)
    d_feed_all = jnp.concatenate((d_feed, sibling(d_feed)))
    hidden_c_all = jnp.concatenate(
        (hidden_c, compact(hidden_other, other_runs).astype(BF16))
    )
    g_up, g_down, g_up_bias, d_hidden_term = [], [], [], 0.0
    for i in range(2):
        pre = mm(hidden_c_all, w_up[i]) + b_up[i]
        cdf = 0.5 * (1.0 + lax.erf(pre * (0.5**0.5)))
        density = jnp.exp(-0.5 * pre * pre) * (0.5 / jnp.pi) ** 0.5
        activated = (pre * cdf).astype(BF16)
        d_pre = (mm(d_feed_all, w_down[i]) * (cdf + pre * density)).astype(BF16)
        g_up_bias.append(jnp.sum(d_pre.astype(F32), axis=0))
        g_up.append(t_mm(hidden_c_all, d_pre).astype(BF16))
        g_down.append(t_mm(d_feed_all, activated).astype(BF16))
        d_hidden_term = d_hidden_term + mm_t(d_pre, w_up[i])
    compact_own = d_feed.shape[0]
    d_hidden = (
        d_second
        + d_hidden_term[:compact_own]
        + sibling(d_hidden_term[compact_own:].astype(BF16)).astype(F32)
    )
    pieces = (2, width // piece_rows, piece_rows, hidden_piece)
    s_up = reduce_scatter(jnp.stack(g_up).reshape(pieces), True)
    s_down = reduce_scatter(jnp.stack(g_down).reshape(pieces), False).T
    g_first_gain = jnp.sum(d_hidden * normed_one, axis=0)
    g_first_shift = jnp.sum(d_hidden, axis=0)
    d_first = norm_back(d_hidden, normed_one, inverse_one, first_gain)
    d_branch = d_first.astype(BF16)
    g_out_bias = jnp.sum(d_branch.astype(F32), axis=0)
    d_branch_all = jnp.concatenate((d_branch, sibling(d_branch)))
    d_attention = mm(d_branch_all, w_out_t).astype(BF16).reshape(compact_shape)
    d_attention_far = partner(d_attention)

    (d_queries_c,) = per_head_pair(
        query_back_kernel,
        [
            q_compact,
            d_attention,
            keys_used.reshape(attn_shape),
            values_used.reshape(attn_shape),
        ],
        1,
        q_compact,
        6 * slots * block_rows * columns * blocks,
    )
    d_keys, d_values = per_head_pair(
        key_back_kernel,
        [
            jnp.where(swapped_lanes, q_far, q_compact),
            jnp.where(swapped_lanes, d_attention_far, d_attention),
            keys.reshape(attn_shape),
            values.reshape(attn_shape),
        ],
        2,
        keys.reshape(attn_shape),
        8 * slots * block_rows * columns * blocks,
    )
    d_queries_c = d_queries_c.reshape(-1, columns)
    d_queries = spread(d_queries_c).astype(BF16)
    d_keys = d_keys.reshape(-1, columns)
    d_values = d_values.reshape(-1, columns)
    term = mm_t(d_queries, w_query) + mm_t(d_keys, w_key) + mm_t(d_values, w_value)
    grad_rows = (
        term[:own_count]
        + sibling(term[own_count:].astype(BF16)).astype(F32)
        + spread(d_first, own_runs, **exact)
    ).astype(BF16)
    grad_x = to_output(grad_rows)

    g_query_bias = jnp.sum(d_queries_c.astype(F32), axis=0)
    g_value_bias = jnp.sum(d_values.astype(F32), axis=0)
    g_attn = jnp.stack(
        (
            t_mm(x_flat, d_queries).astype(BF16),
            t_mm(x_flat, d_keys).astype(BF16),
            t_mm(x_flat, d_values).astype(BF16),
            t_mm(d_branch_all, compact(attention.reshape(-1, columns)).astype(BF16)).astype(BF16),
        ),
        axis=1,
    )
    g_attn = jnp.transpose(g_attn.reshape(width, 4, 2, local), (2, 0, 1, 3)).reshape(
        2, width // piece_rows, 2, half, 4 * local
    )
    s_attn = jnp.concatenate(
        (
            reduce_scatter(g_attn[:, :, 0], True),
            reduce_scatter(g_attn[:, :, 1], False),
        )
    )

    def widen(own_first, size):
        own_first = own_first.reshape(2, -1)
        by_p = ordered(p, own_first[0], own_first[1])
        zero = jnp.zeros_like(by_p)
        return jnp.where(
            c == 0,
            jnp.stack((by_p, zero), axis=1),
            jnp.stack((zero, by_p), axis=1),
        ).reshape(size)

    vectors = [
        widen(g_query_bias, HEADS * HD),
        widen(g_value_bias, HEADS * HD),
        g_out_bias,
        g_first_gain,
        g_first_shift,
        widen(jnp.stack(g_up_bias), 4 * hidden_piece),
        g_down_bias,
        g_second_gain,
        g_second_shift,
    ]
    summed = sum_all(jnp.concatenate(vectors))
    ends, start = [], 0
    for vector in vectors:
        ends.append(summed[start : start + vector.shape[0]])
        start += vector.shape[0]
    (
        v_query_bias,
        v_value_bias,
        v_out_bias,
        v_first_gain,
        v_first_shift,
        v_up_bias,
        v_down_bias,
        v_second_gain,
        v_second_shift,
    ) = ends
    return (
        out_y,
        grad_x,
        s_attn[:, :local],
        v_query_bias,
        s_attn[:, local : 2 * local],
        s_attn[:, 2 * local : 3 * local],
        v_value_bias,
        s_attn[:, 3 * local :].T,
        v_out_bias,
        v_first_gain,
        v_first_shift,
        s_up,
        v_up_bias,
        s_down,
        v_down_bias,
        v_second_gain,
        v_second_shift,
    )


def solution(mesh):
    in_specs = (
        P("dp", None, None),
        P("dp", "head"),
        P("head"),
        P("dp", "head"),
        P("dp", "head"),
        P("head"),
        P("head", "dp"),
        P(),
        P(),
        P(),
        P("dp", "head"),
        P("head"),
        P("head", "dp"),
        P(),
        P(),
        P(),
        P("head"),
        P("dp", None),
        P("dp", None, None),
    )
    out_specs = (
        P("dp", "head", None),
        P("dp", "head", None),
        P("dp", "head"),
        P(),
        P("dp", "head"),
        P("dp", "head"),
        P(),
        P("head", "dp"),
        P(),
        P(),
        P(),
        P("dp", "head"),
        P(),
        P("head", "dp"),
        P(),
        P(),
        P(),
    )
    return jax.shard_map(
        per_device, mesh=mesh, in_specs=in_specs, out_specs=out_specs, check_vma=False
    )
```

time: 1380 us -> 539 us (0.39)
  waiting for transfers between devices: 796 us -> 117 us
  blocking collectives: 238 us -> 0 us
  matrix products: 194 us -> 113 us
  starting transfers between devices: 4.47 us -> 81.7 us
  local copies, waits for them, and re-layouts: 75.5 us -> 118 us
  Pallas kernels: 0 us -> 35 us
  other arithmetic: 49.1 us -> 63.8 us
    reduce_scatter x6 -> x0, waiting for transfers between devices: 369 us -> none  [the longest x1 78 us: per_device(): lax.psum_scatter(branch_term, 'head', scatter_dimension=1, tiled=True)]
    unnamed x19 -> x0, waiting for transfers between devices: 200 us -> none
    all_gather x4 -> x0, blocking collectives: 198 us -> none  [the longest x1 69 us: per_device(): lax.all_gather(key_weight, 'dp', axis=0, tiled=True)]
    all_gather x5 -> x0, waiting for transfers between devices: 128 us -> none  [the longest x1 37.5 us: per_device(): d_feed_all = lax.all_gather(d_feed, 'head', axis=1, tiled=True)]
    ppermute x4 -> x60, starting transfers between devices: 2.48 us -> 81.7 us  [the longest x30 56.6 us: shift(): lax.ppermute(block, axis, [(i, (i + distance) % n) for i in range(n)])]
    dot_general x57 -> x36, matrix products: 191 us -> 113 us  [the longest x9 60.9 us: mm_t(): lax.dot_general(a, b, (((1,), (1,)), ((), ())), preferred_element_type=F32)]
    psum x1 -> x0, blocking collectives: 39.9 us -> none  [per_device(): lax.psum((widen(g_query_bias, HEADS * HD), widen(g_value_bias, HEADS * HD...]
    slice x0 -> x19, local copies, waits for them, and re-layouts: none -> 37.9 us  [the longest x5 25.7 us: per_device(): w_query, w_key, w_value, w_out_t = (w_attn[i] for i in range(4))]
  transfers between devices with their start and end apart: 19 -> 60, of which waited for: 15 -> 20; matrix products, arithmetic and copies ran while one was open for 10% -> 54% of each run, Pallas kernels for 0% -> 7%
where the time goes in v1:
time: 539 us; the launch traced here: 532 us
  local copies, waits for them, and re-layouts  118 us (22%)
  waiting for transfers between devices  117 us (22%)
  matrix products  113 us (21%)
  starting transfers between devices  81.7 us (15%)
  other arithmetic  63.8 us (12%)
  Pallas kernels  35 us (6%)
    ppermute x30, waiting for transfers between devices, shift(): lax.ppermute(block, axis, [(i, (i + distance) % n) for i in range(n)])  85.7 us
    dot_general x9, matrix products, mm_t(): lax.dot_general(a, b, (((1,), (1,)), ((), ())), preferred_element_type=F32)  60.9 us
    ppermute x30, starting transfers between devices, shift(): lax.ppermute(block, axis, [(i, (i + distance) % n) for i in range(n)])  56.6 us
    pallas_call x3, Pallas kernels, per_head_pair(): pl.pallas_call(kernel, grid=(blocks, width // (2 * HD)), in_specs=[spec(a...  35 us
    ppermute x30, waiting for transfers between devices, flip(): return lax.ppermute(block, axis, [(i, i ^ bit) for i in range(n)])  31.5 us
    slice x5, local copies, waits for them, and re-layouts, per_device(): w_query, w_key, w_value, w_out_t = (w_attn[i] for i in range(4))  25.7 us
    ppermute x30, starting transfers between devices, flip(): return lax.ppermute(block, axis, [(i, i ^ bit) for i in range(n)])  25 us
    dot_general x10, matrix products, mm(): return jnp.dot(a, b, preferred_element_type=F32)  24.8 us
  transfers between devices with their start and end apart: 60, of which 20 were waited for; matrix products, arithmetic and copies ran while one was open for 54% of the time, Pallas kernels for 7%

profile of v1, /device:TPU:0, one launch (start us, length us, event | category | flops | bytes accessed | tf_op | source)
XLA Modules:
  0.0 531.9 jit_solution(7520677379303929779)
XLA Ops:
  0.7 3.1 collective-permute-start.19
  30.6 6.5 %collective-permute-done = bf16[48,768]{1,0:T(8,128)(2,1)S(1)} collective-permute-done((bf16[48,768]{1,0:T(8,128)(2,1)}, bf16[48,768]{1,0:T(8,128)(2,1)S(1)}, u32[]{:S(2)}, u32[]{:S(2)}) %collective-permute-start) | collective-permute-done | bytes 73760 | tf_op jit(solution)/shard_map/ppermute | solution.py:26
  37.1 5.9 %collective-permute-done.6 = bf16[48,768]{1,0:T(8,128)(2,1)S(1)} collective-permute-done((bf16[48,768]{1,0:T(8,128)(2,1)}, bf16[48,768]{1,0:T(8,128)(2,1)S(1)}, u32[]{:S(2)}, u32[]{:S(2)}) %collective-permute-start.6) | collective-permute-done | bytes 73760 | tf_op jit(solution)/shard_map/ppermute | solution.py:26
  43.3 5.1 collective-permute-done.1
  48.4 4.5 collective-permute-done.7
  54.8 3.6 collective-permute-done.2
  59.3 2.8 collective-permute-start.17
  70.7 45.2 %collective-permute-done.16 = bf16[96,768]{1,0:T(8,128)(2,1)S(1)} collective-permute-done((bf16[96,768]{1,0:T(8,128)(2,1)}, bf16[96,768]{1,0:T(8,128)(2,1)S(1)}, u32[]{:S(2)}, u32[]{:S(2)}) %collective-permute-start.16) | collective-permute-done | bytes 147488 | tf_op jit(solution)/shard_map/ppermute | solution.py:26
  121.6 4.2 collective-permute-done.22
  130.7 3.5 collective-permute-done.9
  135.0 4.1 reshape.624
  139.0 10.5 %fusion.163 = (bf16[1,768,2,192]{3,0,1,2:T(2,128)(2,1)S(1)}, bf16[1,768,2,192]{3,0,1,2:T(2,128)(2,1)}, bf16[1,768,2,192]{3,0,1,2:T(2,128)(2,1)}, bf16[1,768,2,192]{3,0,1,2:T(2,128)(2,1)}) fusion(bf16[4,768,2,192]{3,0,1,2:T(4,128)(2,1)} %bitcast.363), kind=kLoop, calls=%fused_computation.386 | loop fusion | bytes 4718592 | tf_op jit(solution)/shard_map/slice | solution.py:256
  149.5 4.7 copy.79
  154.2 4.6 copy.80
  158.8 3.4 copy.81
  164.8 3.3 convolution_convert_fusion
  172.2 4.5 fusion.22
  176.7 4.1 fusion.23
  180.8 11.9 %shard_map.314 = bf16[2,3,256,384]{3,2,1,0:T(8,128)(2,1)} custom-call(bf16[2,3,256,384]{3,2,1,0:T(8,128)(2,1)} %bitcast.389, bf16[2,3,256,384]{3,2,1,0:T(8,128)(2,1)} %bitcast.379, bf16[2,3,256,384]{3,2,1,0:T(8,128)(2,1)} %bitcast.381), custom_call_target="tpu_custom_call" | custom-call | flops 1207959552 | bytes 4718592 | tf_op jit(solution)/shard_map/pallas_call | solution.py:202
  213.0 17.2 %fusion.32 = f32[1536,768]{1,0:T(8,128)} fusion(bf16[768,768]{1,0:T(8,128)(2,1)} %bitcast.434, bf16[768,768]{1,0:T(8,128)(2,1)} %bitcast.44, f32[768]{0:T(1024)} %param.30, bf16[768,768]{1,0:T(8,128)(2,1)} %copy-done.47, bf16[768,768]{1,0:T(8,128)(2,1)} %copy-done.43), kind=kOutput, calls=%fused_computation.81 | convolution fusion | flops 3706454016 | bytes 9440256 | tf_op jit(solution)/shard_map/dot_general | solution.py:56
  230.3 18.6 %convolution_add_fusion = f32[1536,768]{1,0:T(8,128)} fusion(f32[1536,768]{1,0:T(8,128)} %fusion.32, bf16[768,768]{1,0:T(8,128)(2,1)} %bitcast.432, bf16[768,768]{1,0:T(8,128)(2,1)} %bitcast.55, f32[768]{0:T(1024)} %slice.245, bf16[768,768]{1,0:T(8,128)(2,1)} %copy-done.47, bf16[768,768]{1,0:T(8,128)(2,1)} %copy-done.43), kind=kOutput, calls=%fused_computation.39 | convolution fusion | flops 3707633664 | bytes 14158848 | tf_op jit(solution)/shard_map/dot_general | solution.py:56
  248.9 2.8 slice.339
  258.9 3.1 convolution_add_fusion.5
  262.0 2.9 convolution_add_fusion.4
  265.0 2.8 fusion.161
  275.0 2.9 multiply_reduce_fusion.2
  314.5 11.1 %shard_map.315 = bf16[2,3,64,384]{3,2,1,0:T(8,128)(2,1)} custom-call(bf16[2,3,64,384]{3,2,1,0:T(8,128)(2,1)} %bitcast.73.q_ref, bf16[2,3,64,384]{3,2,1,0:T(8,128)(2,1)} %bitcast.428, bf16[2,3,256,384]{3,2,1,0:T(8,128)(2,1)} %bitcast.380, bf16[2,3,256,384]{3,2,1,0:T(8,128)(2,1)} %bitcast.382), custom_call_target="tpu_custom_call" | custom-call | flops 452984832 | bytes 3244032 | tf_op jit(solution)/shard_map/pallas_call | solution.py:202
  333.8 4.7 copy.91
  338.5 3.9 convolution_convert_fusion.9
  342.5 4.7 copy.88
  349.9 5.0 fusion.174
  357.0 12.0 %shard_map.316 = (bf16[2,3,256,384]{3,2,1,0:T(8,128)(2,1)}, bf16[2,3,256,384]{3,2,1,0:T(8,128)(2,1)}) custom-call(bf16[2,3,64,384]{3,2,1,0:T(8,128)(2,1)} %get-tuple-element.154.q_ref, bf16[2,3,64,384]{3,2,1,0:T(8,128)(2,1)} %get-tuple-element.153.g_ref, bf16[2,3,256,384]{3,2,1,0:T(8,128)(2,1)} %bitcast.440, bf16[2,3,256,384]{3,2,1,0:T(8,128)(2,1)} %bitcast.441), custom_call_target="tpu_custom_call" | custom-call | flops 603979776 | bytes 5308416 | tf_op jit(solution)/shard_map/pallas_call | solution.py:202
  369.1 5.2 fusion.175
  389.0 8.0 %add_add_fusion = f32[1536,768]{1,0:T(8,128)} fusion(f32[1536,768]{1,0:T(8,128)} %fusion.174, f32[1536,768]{1,0:T(8,128)} %fusion.175, bf16[1536,384]{1,0:T(8,128)(2,1)} %bitcast.392, bf16[768,384]{0,1:T(8,128)(2,1)} %bitcast.402), kind=kOutput, calls=%fused_computation.8 | convolution fusion | flops 908328960 | bytes 15925248 | tf_op jit(solution)/shard_map/dot_general | solution.py:56
  398.9 4.7 copy.90
  403.6 4.7 copy.89
  410.5 10.7 %maximum_bitcast_fusion = bf16[2,768,4,192]{3,2,1,0:T(4,128)(2,1)} fusion(bf16[768,1,2,192]{3,1,0,2:T(2,128)(2,1)} %copy.91, bf16[768,1,2,192]{3,1,0,2:T(2,128)(2,1)} %copy.90, bf16[768,1,2,192]{3,1,0,2:T(2,128)(2,1)} %copy.89, bf16[768,1,2,192]{3,1,0,2:T(2,128)(2,1)} %copy.88), kind=kLoop, calls=%fused_computation.40 | loop fusion | flops 9437184 | bytes 4718592 | tf_op jit(solution)/shard_map/transpose | solution.py:469
  421.2 6.4 %reshape.653 = bf16[2,8,2,48,768]{4,3,2,1,0:T(8,128)(2,1)} reshape(bf16[2,768,4,192]{3,2,1,0:T(4,128)(2,1)} %maximum_bitcast_fusion) | data formatting | bytes 4718592 | tf_op jit(solution)/shard_map/reshape | solution.py:469
  432.5 14.9 %collective-permute-start.48 = (f32[9216]{0:T(1024)S(1)}, f32[9216]{0:T(1024)S(1)}, u32[]{:S(2)}, u32[]{:S(2)}) collective-permute-start(f32[9216]{0:T(1024)S(1)} %add.549), channel_id=1, source_target_pairs={{0,8},{4,12},{8,16},{12,20},{16,24},{20,28},{24,0},{28,4},{1,9},{5... | collective-permute-start | bytes 110600 | tf_op jit(solution)/shard_map/ppermute | solution.py:26
  462.1 5.6 %collective-permute-done.39 = bf16[2,4,48,768]{3,2,1,0:T(8,128)(2,1)S(1)} collective-permute-done((bf16[2,4,48,768]{3,2,1,0:T(8,128)(2,1)S(1)}, bf16[2,4,48,768]{3,2,1,0:T(8,128)(2,1)S(1)}, u32[]{:S(2)}, u32[]{:S(2)}) %collective-permute-start.39) | collective-permute-done | bytes 589856 | tf_op jit(solution)/shard_map/ppermute | solution.py:21
  471.5 15.3 %collective-permute-done.40 = bf16[4,48,768]{2,1,0:T(8,128)(2,1)S(1)} collective-permute-done((bf16[4,48,768]{2,1,0:T(8,128)(2,1)S(1)}, bf16[4,48,768]{2,1,0:T(8,128)(2,1)S(1)}, u32[]{:S(2)}, u32[]{:S(2)}) %collective-permute-start.40) | collective-permute-done | bytes 294944 | tf_op jit(solution)/shard_map/ppermute | solution.py:21
  486.8 2.6 collective-permute-start.43
  493.0 2.9 collective-permute-start.38
  498.4 3.8 collective-permute-start.54
  502.3 3.1 collective-permute-done.37
  505.4 3.8 collective-permute-start.59
  514.4 3.7 collective-permute-start.58
  522.1 6.3 %collective-permute-done.58 = bf16[96,768]{1,0:T(8,128)(2,1)S(1)} collective-permute-done((bf16[96,768]{1,0:T(8,128)(2,1)}, bf16[96,768]{1,0:T(8,128)(2,1)S(1)}, u32[]{:S(2)}, u32[]{:S(2)}) %collective-permute-start.58) | collective-permute-done | bytes 147488 | tf_op jit(solution)/shard_map/ppermute | solution.py:26
  (484 shorter events, 199.9 us)
Async XLA Ops:
  0.7 58.6 %collective-permute-start.19 = (bf16[96,768]{1,0:T(8,128)(2,1)}, bf16[96,768]{1,0:T(8,128)(2,1)}, u32[]{:S(2)}, u32[]{:S(2)}) collective-permute-start(bf16[96,768]{1,0:T(8,128)(2,1)} %bitcast.459), channel_id=1, source_target_pairs={{0,8},{4,12},{8,16},{12,20},{16,24},{20,28},{24,0},{28,4},{1,9},{5... | collective-permute-start | bytes 442376 | tf_op jit(solution)/shard_map/ppermute | solution.py:26
  3.8 59.2 %collective-permute-start.20 = (bf16[96,768]{1,0:T(8,128)(2,1)}, bf16[96,768]{1,0:T(8,128)(2,1)}, u32[]{:S(2)}, u32[]{:S(2)}) collective-permute-start(bf16[96,768]{1,0:T(8,128)(2,1)} %bitcast.460), channel_id=1, source_target_pairs={{0,16},{4,20},{8,24},{12,28},{16,0},{20,4},{24,8},{28,12},{1,17},{... | collective-permute-start | bytes 442376 | tf_op jit(solution)/shard_map/ppermute | solution.py:26
  6.4 59.7 %collective-permute-start.21 = (bf16[96,768]{1,0:T(8,128)(2,1)}, bf16[96,768]{1,0:T(8,128)(2,1)}, u32[]{:S(2)}, u32[]{:S(2)}) collective-permute-start(bf16[96,768]{1,0:T(8,128)(2,1)} %bitcast.461), channel_id=1, source_target_pairs={{0,24},{4,28},{8,0},{12,4},{16,8},{20,12},{24,16},{28,20},{1,25},{... | collective-permute-start | bytes 442376 | tf_op jit(solution)/shard_map/ppermute | solution.py:26
  7.7 59.8 %collective-permute-start.15 = (bf16[96,768]{1,0:T(8,128)(2,1)}, bf16[96,768]{1,0:T(8,128)(2,1)}, u32[]{:S(2)}, u32[]{:S(2)}) collective-permute-start(bf16[96,768]{1,0:T(8,128)(2,1)} %param.29), channel_id=1, source_target_pairs={{0,8},{4,12},{8,16},{12,20},{16,24},{20,28},{24,0},{28,4},{1,9},{5... | collective-permute-start | bytes 442376 | tf_op jit(solution)/shard_map/ppermute | solution.py:26
  9.9 14.4 %collective-permute-start.10 = (f32[1155]{0:T(1024)S(1)}, f32[1155]{0:T(1024)S(1)}, u32[]{:S(2)}, u32[]{:S(2)}) collective-permute-start(f32[1155]{0:T(1024)S(1)} %concatenate.37), channel_id=1, source_target_pairs={{0,2},{1,3},{2,0},{3,1},{4,6},{5,7},{6,4},{7,5},{8,10},{9,11},{10,... | collective-permute-start | bytes 13868 | tf_op jit(solution)/shard_map/ppermute | solution.py:21
  58.3 57.6 %collective-permute-start.16 = (bf16[96,768]{1,0:T(8,128)(2,1)}, bf16[96,768]{1,0:T(8,128)(2,1)S(1)}, u32[]{:S(2)}, u32[]{:S(2)}) collective-permute-start(bf16[96,768]{1,0:T(8,128)(2,1)} %param.29), channel_id=1, source_target_pairs={{0,16},{4,20},{8,24},{12,28},{16,0},{20,4},{24,8},{28,12},{1,17},{... | collective-permute-start | bytes 442376 | tf_op jit(solution)/shard_map/ppermute | solution.py:26
  59.3 57.8 %collective-permute-start.17 = (bf16[96,768]{1,0:T(8,128)(2,1)}, bf16[96,768]{1,0:T(8,128)(2,1)S(1)}, u32[]{:S(2)}, u32[]{:S(2)}) collective-permute-start(bf16[96,768]{1,0:T(8,128)(2,1)} %param.29), channel_id=1, source_target_pairs={{0,24},{4,28},{8,0},{12,4},{16,8},{20,12},{24,16},{28,20},{1,25},{... | collective-permute-start | bytes 442376 | tf_op jit(solution)/shard_map/ppermute | solution.py:26
  63.0 109.1 %collective-permute-start.11 = (bf16[2,3,2,128,768]{4,3,2,1,0:T(8,128)(2,1)}, bf16[2,3,2,128,768]{4,3,2,1,0:T(8,128)(2,1)}, u32[]{:S(2)}, u32[]{:S(2)}) collective-permute-start(bf16[2,3,2,128,768]{4,3,2,1,0:T(8,128)(2,1)} %pad_maximum_fusion), channel_id=1, source_target_pairs={{0,16},{4,20},{8,24},{12,28},{16,0},{20,4},{24,8},{28,12},{1,17},{... | collective-permute-start | bytes 7077896 | tf_op jit(solution)/shard_map/ppermute | solution.py:26
  66.0 53.2 %collective-permute-start.8 = (bf16[4,48,768]{2,1,0:T(8,128)(2,1)S(1)}, bf16[4,48,768]{2,1,0:T(8,128)(2,1)S(1)}, u32[]{:S(2)}, u32[]{:S(2)}) collective-permute-start(bf16[4,48,768]{2,1,0:T(8,128)(2,1)S(1)} %bitcast_dynamic-update-slice_fusion.8), channel_id=1, source_target_pairs={{0,2},{1,3},{2,0},{3,1},{4,6},{5,7},{6,4},{7,5},{8,10},{9,11},{10,... | collective-permute-start | bytes 884744 | tf_op jit(solution)/shard_map/ppermute | solution.py:21
  67.6 52.4 %collective-permute-start.3 = (bf16[4,48,768]{2,1,0:T(8,128)(2,1)S(1)}, bf16[4,48,768]{2,1,0:T(8,128)(2,1)S(1)}, u32[]{:S(2)}, u32[]{:S(2)}) collective-permute-start(bf16[4,48,768]{2,1,0:T(8,128)(2,1)S(1)} %bitcast_dynamic-update-slice_fusion.12), channel_id=1, source_target_pairs={{0,4},{4,0},{8,12},{12,8},{16,20},{20,16},{24,28},{28,24},{1,5},{5... | collective-permute-start | bytes 884744 | tf_op jit(solution)/shard_map/ppermute | solution.py:21
  115.9 9.9 %collective-permute-start.22 = (bf16[4,96,768]{2,1,0:T(8,128)(2,1)S(1)}, bf16[4,96,768]{2,1,0:T(8,128)(2,1)S(1)}, u32[]{:S(2)}, u32[]{:S(2)}) collective-permute-start(bf16[4,96,768]{2,1,0:T(8,128)(2,1)S(1)} %bitcast_dynamic-update-slice_fusion.1), channel_id=1, source_target_pairs={{0,2},{1,3},{2,0},{3,1},{4,6},{5,7},{6,4},{7,5},{8,10},{9,11},{10,... | collective-permute-start | bytes 1769480 | tf_op jit(solution)/shard_map/ppermute | solution.py:21
  117.8 10.7 %collective-permute-start.18 = (bf16[4,96,768]{2,1,0:T(8,128)(2,1)}, bf16[4,96,768]{2,1,0:T(8,128)(2,1)S(1)}, u32[]{:S(2)}, u32[]{:S(2)}) collective-permute-start(bf16[4,96,768]{2,1,0:T(8,128)(2,1)} %bitcast_dynamic-update-slice_fusion.4), channel_id=1, source_target_pairs={{0,4},{4,0},{8,12},{12,8},{16,20},{20,16},{24,28},{28,24},{1,5},{5... | collective-permute-start | bytes 1769480 | tf_op jit(solution)/shard_map/ppermute | solution.py:21
  119.3 14.9 %collective-permute-start.9 = (bf16[2,4,48,768]{3,2,1,0:T(8,128)(2,1)S(1)}, bf16[2,4,48,768]{3,2,1,0:T(8,128)(2,1)S(1)}, u32[]{:S(2)}, u32[]{:S(2)}) collective-permute-start(bf16[2,4,48,768]{3,2,1,0:T(8,128)(2,1)S(1)} %pad_maximum_fusion.14), channel_id=1, source_target_pairs={{0,4},{4,0},{8,12},{12,8},{16,20},{20,16},{24,28},{28,24},{1,5},{5... | collective-permute-start | bytes 1769480 | tf_op jit(solution)/shard_map/ppermute | solution.py:21
  120.0 14.4 %collective-permute-start.4 = (bf16[4,2,48,768]{3,2,1,0:T(8,128)(2,1)S(1)}, bf16[4,2,48,768]{3,2,1,0:T(8,128)(2,1)S(1)}, u32[]{:S(2)}, u32[]{:S(2)}) collective-permute-start(bf16[4,2,48,768]{3,2,1,0:T(8,128)(2,1)S(1)} %pad_maximum_fusion.13), channel_id=1, source_target_pairs={{0,2},{1,3},{2,0},{3,1},{4,6},{5,7},{6,4},{7,5},{8,10},{9,11},{10,... | collective-permute-start | bytes 1769480 | tf_op jit(solution)/shard_map/ppermute | solution.py:21
  127.0 77.0 %collective-permute-start.23 = (bf16[2,4,96,768]{3,2,1,0:T(8,128)(2,1)}, bf16[2,4,96,768]{3,2,1,0:T(8,128)(2,1)}, u32[]{:S(2)}, u32[]{:S(2)}) collective-permute-start(bf16[2,4,96,768]{3,2,1,0:T(8,128)(2,1)} %pad_maximum_fusion.10), channel_id=1, source_target_pairs={{0,4},{4,0},{8,12},{12,8},{16,20},{20,16},{24,28},{28,24},{1,5},{5... | collective-permute-start | bytes 3538952 | tf_op jit(solution)/shard_map/ppermute | solution.py:21
  164.8 35.2 %collective-permute-start.13 = (bf16[768,384]{0,1:T(8,128)(2,1)}, bf16[768,384]{0,1:T(8,128)(2,1)S(1)}, u32[]{:S(2)}, u32[]{:S(2)}) collective-permute-start(bf16[768,384]{0,1:T(8,128)(2,1)} %bitcast.416), channel_id=1, source_target_pairs={{0,1},{1,0},{2,3},{3,2},{4,5},{5,4},{6,7},{7,6},{8,9},{9,8},{10,11... | collective-permute-start | bytes 1769480 | tf_op jit(solution)/shard_map/ppermute | solution.py:21
  196.0 34.3 %collective-permute-start.24 = (bf16[4,2,96,768]{3,2,1,0:T(8,128)(2,1)}, bf16[4,2,96,768]{3,2,1,0:T(8,128)(2,1)}, u32[]{:S(2)}, u32[]{:S(2)}) collective-permute-start(bf16[4,2,96,768]{3,2,1,0:T(8,128)(2,1)} %pad_maximum_fusion.9), channel_id=1, source_target_pairs={{0,2},{1,3},{2,0},{3,1},{4,6},{5,7},{6,4},{7,5},{8,10},{9,11},{10,... | collective-permute-start | bytes 3538952 | tf_op jit(solution)/shard_map/ppermute | solution.py:21
  198.6 156.4 %collective-permute-start.30 = (bf16[2,3,64,384]{3,2,1,0:T(8,128)(2,1)}, bf16[2,3,64,384]{3,2,1,0:T(8,128)(2,1)}, u32[]{:S(2)}, u32[]{:S(2)}) collective-permute-start(bf16[2,3,64,384]{3,2,1,0:T(8,128)(2,1)} %bitcast.73.q_ref), channel_id=1, source_target_pairs={{0,16},{4,20},{8,24},{12,28},{16,0},{20,4},{24,8},{28,12},{1,17},{... | collective-permute-start | bytes 884744 | tf_op jit(solution)/shard_map/ppermute | solution.py:26
  204.0 8.0 %collective-permute-start.14 = (bf16[768,768]{1,0:T(8,128)(2,1)S(1)}, bf16[768,768]{1,0:T(8,128)(2,1)S(1)}, u32[]{:S(2)}, u32[]{:S(2)}) collective-permute-start(bf16[768,768]{1,0:T(8,128)(2,1)S(1)} %fusion.31), channel_id=1, source_target_pairs={{0,1},{1,0},{2,3},{3,2},{4,5},{5,4},{6,7},{7,6},{8,9},{9,8},{10,11... | collective-permute-start | bytes 3538952 | tf_op jit(solution)/shard_map/ppermute | solution.py:21
  251.7 13.2 %collective-permute-start.25 = (bf16[768,768]{1,0:T(8,128)(2,1)}, bf16[768,768]{1,0:T(8,128)(2,1)}, u32[]{:S(2)}, u32[]{:S(2)}) collective-permute-start(bf16[768,768]{1,0:T(8,128)(2,1)} %slice.339), channel_id=1, source_target_pairs={{0,1},{1,0},{2,3},{3,2},{4,5},{5,4},{6,7},{7,6},{8,9},{9,8},{10,11... | collective-permute-start | bytes 3538952 | tf_op jit(solution)/shard_map/ppermute | solution.py:21
  286.7 19.9 %collective-permute-start.26 = (bf16[3,128,768]{2,1,0:T(8,128)(2,1)}, bf16[3,128,768]{2,1,0:T(8,128)(2,1)}, u32[]{:S(2)}, u32[]{:S(2)}) collective-permute-start(bf16[3,128,768]{2,1,0:T(8,128)(2,1)} %dynamic-slice_bitcast_fusion.4), channel_id=1, source_target_pairs={{0,2},{1,3},{2,0},{3,1},{4,6},{5,7},{6,4},{7,5},{8,10},{9,11},{10,... | collective-permute-start | bytes 1769480 | tf_op jit(solution)/shard_map/ppermute | solution.py:21
  296.7 12.2 %collective-permute-start.28 = (bf16[192,768]{1,0:T(8,128)(2,1)}, bf16[192,768]{1,0:T(8,128)(2,1)}, u32[]{:S(2)}, u32[]{:S(2)}) collective-permute-start(bf16[192,768]{1,0:T(8,128)(2,1)} %slice.340), channel_id=1, source_target_pairs={{0,1},{1,0},{2,3},{3,2},{4,5},{5,4},{6,7},{7,6},{8,9},{9,8},{10,11... | collective-permute-start | bytes 884744 | tf_op jit(solution)/shard_map/ppermute | solution.py:21
  299.3 156.9 %collective-permute-start.50 = (bf16[4,2,96,768]{3,2,0,1:T(8,128)(2,1)}, bf16[4,2,96,768]{3,2,0,1:T(8,128)(2,1)}, u32[]{:S(2)}, u32[]{:S(2)}) collective-permute-start(bf16[4,2,96,768]{3,2,0,1:T(8,128)(2,1)} %copy.93), channel_id=1, source_target_pairs={{0,2},{1,3},{2,0},{3,1},{4,6},{5,7},{6,4},{7,5},{8,10},{9,11},{10,... | collective-permute-start | bytes 3538952 | tf_op jit(solution)/shard_map/ppermute | solution.py:21
  303.0 156.1 %collective-permute-start.55 = (bf16[2,4,96,768]{3,2,1,0:T(8,128)(2,1)}, bf16[2,4,96,768]{3,2,1,0:T(8,128)(2,1)}, u32[]{:S(2)}, u32[]{:S(2)}) collective-permute-start(bf16[2,4,96,768]{3,2,1,0:T(8,128)(2,1)} %fusion.45), channel_id=1, source_target_pairs={{0,4},{4,0},{8,12},{12,8},{16,20},{20,16},{24,28},{28,24},{1,5},{5... | collective-permute-start | bytes 3538952 | tf_op jit(solution)/shard_map/ppermute | solution.py:21
  325.7 29.3 %collective-permute-start.31 = (bf16[2,3,64,384]{3,2,1,0:T(8,128)(2,1)}, bf16[2,3,64,384]{3,2,1,0:T(8,128)(2,1)}, u32[]{:S(2)}, u32[]{:S(2)}) collective-permute-start(bf16[2,3,64,384]{3,2,1,0:T(8,128)(2,1)} %bitcast.429), channel_id=1, source_target_pairs={{0,16},{4,20},{8,24},{12,28},{16,0},{20,4},{24,8},{28,12},{1,17},{... | collective-permute-start | bytes 884744 | tf_op jit(solution)/shard_map/ppermute | solution.py:26
  389.0 19.3 %collective-permute-start.44 = (f32[9216]{0:T(1024)}, f32[9216]{0:T(1024)}, u32[]{:S(2)}, u32[]{:S(2)}) collective-permute-start(f32[9216]{0:T(1024)} %constant_dynamic-update-slice_fusion), channel_id=1, source_target_pairs={{0,1},{1,0},{2,3},{3,2},{4,5},{5,4},{6,7},{7,6},{8,9},{9,8},{10,11... | collective-permute-start | bytes 110600 | tf_op jit(solution)/shard_map/ppermute | solution.py:21
  409.8 17.8 %collective-permute-start.45 = (f32[9216]{0:T(1024)}, f32[9216]{0:T(1024)}, u32[]{:S(2)}, u32[]{:S(2)}) collective-permute-start(f32[9216]{0:T(1024)} %add.547), channel_id=1, source_target_pairs={{0,2},{1,3},{2,0},{3,1},{4,6},{5,7},{6,4},{7,5},{8,10},{9,11},{10,... | collective-permute-start | bytes 110600 | tf_op jit(solution)/shard_map/ppermute | solution.py:21
  432.5 18.7 %collective-permute-start.48 = (f32[9216]{0:T(1024)S(1)}, f32[9216]{0:T(1024)S(1)}, u32[]{:S(2)}, u32[]{:S(2)}) collective-permute-start(f32[9216]{0:T(1024)S(1)} %add.549), channel_id=1, source_target_pairs={{0,8},{4,12},{8,16},{12,20},{16,24},{20,28},{24,0},{28,4},{1,9},{5... | collective-permute-start | bytes 110600 | tf_op jit(solution)/shard_map/ppermute | solution.py:26
  451.2 58.1 %collective-permute-start.32 = (bf16[768,768]{1,0:T(8,128)(2,1)S(1)}, bf16[768,768]{1,0:T(8,128)(2,1)S(1)}, u32[]{:S(2)}, u32[]{:S(2)}) collective-permute-start(bf16[768,768]{1,0:T(8,128)(2,1)S(1)} %slice.338), channel_id=1, source_target_pairs={{0,1},{1,0},{2,3},{3,2},{4,5},{5,4},{6,7},{7,6},{8,9},{9,8},{10,11... | collective-permute-start | bytes 3538952 | tf_op jit(solution)/shard_map/ppermute | solution.py:21
  451.5 16.2 %collective-permute-start.39 = (bf16[2,4,48,768]{3,2,1,0:T(8,128)(2,1)S(1)}, bf16[2,4,48,768]{3,2,1,0:T(8,128)(2,1)S(1)}, u32[]{:S(2)}, u32[]{:S(2)}) collective-permute-start(bf16[2,4,48,768]{3,2,1,0:T(8,128)(2,1)S(1)} %dynamic-slice_bitcast_fusion.2), channel_id=1, source_target_pairs={{0,4},{4,0},{8,12},{12,8},{16,20},{20,16},{24,28},{28,24},{1,5},{5... | collective-permute-start | bytes 1769480 | tf_op jit(solution)/shard_map/ppermute | solution.py:21
  454.1 16.2 %collective-permute-start.34 = (bf16[4,2,48,768]{3,2,1,0:T(8,128)(2,1)S(1)}, bf16[4,2,48,768]{3,2,1,0:T(8,128)(2,1)S(1)}, u32[]{:S(2)}, u32[]{:S(2)}) collective-permute-start(bf16[4,2,48,768]{3,2,1,0:T(8,128)(2,1)S(1)} %bitcast.446), channel_id=1, source_target_pairs={{0,2},{1,3},{2,0},{3,1},{4,6},{5,7},{6,4},{7,5},{8,10},{9,11},{10,... | collective-permute-start | bytes 1769480 | tf_op jit(solution)/shard_map/ppermute | solution.py:21
  458.0 32.8 %collective-permute-start.51 = (bf16[4,96,768]{2,1,0:T(8,128)(2,1)S(1)}, bf16[4,96,768]{2,1,0:T(8,128)(2,1)S(1)}, u32[]{:S(2)}, u32[]{:S(2)}) collective-permute-start(bf16[4,96,768]{2,1,0:T(8,128)(2,1)S(1)} %dynamic-slice_bitcast_fusion.1), channel_id=1, source_target_pairs={{0,4},{4,0},{8,12},{12,8},{16,20},{20,16},{24,28},{28,24},{1,5},{5... | collective-permute-start | bytes 1769480 | tf_op jit(solution)/shard_map/ppermute | solution.py:21
  460.9 31.9 %collective-permute-start.56 = (bf16[4,96,768]{2,1,0:T(8,128)(2,1)S(1)}, bf16[4,96,768]{2,1,0:T(8,128)(2,1)S(1)}, u32[]{:S(2)}, u32[]{:S(2)}) collective-permute-start(bf16[4,96,768]{2,1,0:T(8,128)(2,1)S(1)} %slice_bitcast_fusion), channel_id=1, source_target_pairs={{0,2},{1,3},{2,0},{3,1},{4,6},{5,7},{6,4},{7,5},{8,10},{9,11},{10,... | collective-permute-start | bytes 1769480 | tf_op jit(solution)/shard_map/ppermute | solution.py:21
  467.9 18.9 %collective-permute-start.40 = (bf16[4,48,768]{2,1,0:T(8,128)(2,1)S(1)}, bf16[4,48,768]{2,1,0:T(8,128)(2,1)S(1)}, u32[]{:S(2)}, u32[]{:S(2)}) collective-permute-start(bf16[4,48,768]{2,1,0:T(8,128)(2,1)S(1)} %slice_bitcast_fusion.3), channel_id=1, source_target_pairs={{0,2},{1,3},{2,0},{3,1},{4,6},{5,7},{6,4},{7,5},{8,10},{9,11},{10,... | collective-permute-start | bytes 884744 | tf_op jit(solution)/shard_map/ppermute | solution.py:21
  470.5 19.0 %collective-permute-start.35 = (bf16[4,48,768]{2,1,0:T(8,128)(2,1)S(1)}, bf16[4,48,768]{2,1,0:T(8,128)(2,1)S(1)}, u32[]{:S(2)}, u32[]{:S(2)}) collective-permute-start(bf16[4,48,768]{2,1,0:T(8,128)(2,1)S(1)} %dynamic-slice_bitcast_fusion.5), channel_id=1, source_target_pairs={{0,4},{4,0},{8,12},{12,8},{16,20},{20,16},{24,28},{28,24},{1,5},{5... | collective-permute-start | bytes 884744 | tf_op jit(solution)/shard_map/ppermute | solution.py:21
  486.8 10.0 %collective-permute-start.43 = (bf16[48,768]{1,0:T(8,128)(2,1)S(1)}, bf16[48,768]{1,0:T(8,128)(2,1)S(1)}, u32[]{:S(2)}, u32[]{:S(2)}) collective-permute-start(bf16[48,768]{1,0:T(8,128)(2,1)S(1)} %get-tuple-element.126), channel_id=1, source_target_pairs={{0,24},{4,28},{8,0},{12,4},{16,8},{20,12},{24,16},{28,20},{1,25},{... | collective-permute-start | bytes 221192 | tf_op jit(solution)/shard_map/ppermute | solution.py:26
  489.5 8.9 %collective-permute-start.42 = (bf16[48,768]{1,0:T(8,128)(2,1)S(1)}, bf16[48,768]{1,0:T(8,128)(2,1)S(1)}, u32[]{:S(2)}, u32[]{:S(2)}) collective-permute-start(bf16[48,768]{1,0:T(8,128)(2,1)S(1)} %get-tuple-element.127), channel_id=1, source_target_pairs={{0,16},{4,20},{8,24},{12,28},{16,0},{20,4},{24,8},{28,12},{1,17},{... | collective-permute-start | bytes 221192 | tf_op jit(solution)/shard_map/ppermute | solution.py:26
  490.8 7.6 %collective-permute-start.41 = (bf16[48,768]{1,0:T(8,128)(2,1)S(1)}, bf16[48,768]{1,0:T(8,128)(2,1)S(1)}, u32[]{:S(2)}, u32[]{:S(2)}) collective-permute-start(bf16[48,768]{1,0:T(8,128)(2,1)S(1)} %get-tuple-element.125), channel_id=1, source_target_pairs={{0,8},{4,12},{8,16},{12,20},{16,24},{20,28},{24,0},{28,4},{1,9},{5... | collective-permute-start | bytes 221192 | tf_op jit(solution)/shard_map/ppermute | solution.py:26
  493.0 9.3 %collective-permute-start.38 = (bf16[48,768]{1,0:T(8,128)(2,1)S(1)}, bf16[48,768]{1,0:T(8,128)(2,1)S(1)}, u32[]{:S(2)}, u32[]{:S(2)}) collective-permute-start(bf16[48,768]{1,0:T(8,128)(2,1)S(1)} %get-tuple-element.129), channel_id=1, source_target_pairs={{0,24},{4,28},{8,0},{12,4},{16,8},{20,12},{24,16},{28,20},{1,25},{... | collective-permute-start | bytes 221192 | tf_op jit(solution)/shard_map/ppermute | solution.py:26
  496.8 8.6 %collective-permute-start.37 = (bf16[48,768]{1,0:T(8,128)(2,1)S(1)}, bf16[48,768]{1,0:T(8,128)(2,1)S(1)}, u32[]{:S(2)}, u32[]{:S(2)}) collective-permute-start(bf16[48,768]{1,0:T(8,128)(2,1)S(1)} %get-tuple-element.130), channel_id=1, source_target_pairs={{0,16},{4,20},{8,24},{12,28},{16,0},{20,4},{24,8},{28,12},{1,17},{... | collective-permute-start | bytes 221192 | tf_op jit(solution)/shard_map/ppermute | solution.py:26
  498.4 7.1 %collective-permute-start.36 = (bf16[48,768]{1,0:T(8,128)(2,1)S(1)}, bf16[48,768]{1,0:T(8,128)(2,1)S(1)}, u32[]{:S(2)}, u32[]{:S(2)}) collective-permute-start(bf16[48,768]{1,0:T(8,128)(2,1)S(1)} %get-tuple-element.128), channel_id=1, source_target_pairs={{0,8},{4,12},{8,16},{12,20},{16,24},{20,28},{24,0},{28,4},{1,9},{5... | collective-permute-start | bytes 221192 | tf_op jit(solution)/shard_map/ppermute | solution.py:26
  498.4 16.0 %collective-permute-start.54 = (bf16[96,768]{1,0:T(8,128)(2,1)}, bf16[96,768]{1,0:T(8,128)(2,1)}, u32[]{:S(2)}, u32[]{:S(2)}) collective-permute-start(bf16[96,768]{1,0:T(8,128)(2,1)} %get-tuple-element.117), channel_id=1, source_target_pairs={{0,24},{4,28},{8,0},{12,4},{16,8},{20,12},{24,16},{28,20},{1,25},{... | collective-permute-start | bytes 442376 | tf_op jit(solution)/shard_map/ppermute | solution.py:26
  502.3 15.9 %collective-permute-start.53 = (bf16[96,768]{1,0:T(8,128)(2,1)}, bf16[96,768]{1,0:T(8,128)(2,1)}, u32[]{:S(2)}, u32[]{:S(2)}) collective-permute-start(bf16[96,768]{1,0:T(8,128)(2,1)} %get-tuple-element.118), channel_id=1, source_target_pairs={{0,16},{4,20},{8,24},{12,28},{16,0},{20,4},{24,8},{28,12},{1,17},{... | collective-permute-start | bytes 442376 | tf_op jit(solution)/shard_map/ppermute | solution.py:26
  505.4 14.7 %collective-permute-start.52 = (bf16[96,768]{1,0:T(8,128)(2,1)}, bf16[96,768]{1,0:T(8,128)(2,1)}, u32[]{:S(2)}, u32[]{:S(2)}) collective-permute-start(bf16[96,768]{1,0:T(8,128)(2,1)} %get-tuple-element.116), channel_id=1, source_target_pairs={{0,8},{4,12},{8,16},{12,20},{16,24},{20,28},{24,0},{28,4},{1,9},{5... | collective-permute-start | bytes 442376 | tf_op jit(solution)/shard_map/ppermute | solution.py:26
  505.4 16.6 %collective-permute-start.59 = (bf16[96,768]{1,0:T(8,128)(2,1)}, bf16[96,768]{1,0:T(8,128)(2,1)}, u32[]{:S(2)}, u32[]{:S(2)}) collective-permute-start(bf16[96,768]{1,0:T(8,128)(2,1)} %get-tuple-element.114), channel_id=1, source_target_pairs={{0,24},{4,28},{8,0},{12,4},{16,8},{20,12},{24,16},{28,20},{1,25},{... | collective-permute-start | bytes 442376 | tf_op jit(solution)/shard_map/ppermute | solution.py:26
  510.8 19.4 %collective-permute-start.33 = (bf16[3,128,768]{2,1,0:T(8,128)(2,1)S(1)}, bf16[3,128,768]{2,1,0:T(8,128)(2,1)S(1)}, u32[]{:S(2)}, u32[]{:S(2)}) collective-permute-start(bf16[3,128,768]{2,1,0:T(8,128)(2,1)S(1)} %dynamic-slice_bitcast_fusion.3), channel_id=1, source_target_pairs={{0,2},{1,3},{2,0},{3,1},{4,6},{5,7},{6,4},{7,5},{8,10},{9,11},{10,... | collective-permute-start | bytes 1769480 | tf_op jit(solution)/shard_map/ppermute | solution.py:21
  514.4 14.0 %collective-permute-start.58 = (bf16[96,768]{1,0:T(8,128)(2,1)}, bf16[96,768]{1,0:T(8,128)(2,1)S(1)}, u32[]{:S(2)}, u32[]{:S(2)}) collective-permute-start(bf16[96,768]{1,0:T(8,128)(2,1)} %get-tuple-element.115), channel_id=1, source_target_pairs={{0,16},{4,20},{8,24},{12,28},{16,0},{20,4},{24,8},{28,12},{1,17},{... | collective-permute-start | bytes 442376 | tf_op jit(solution)/shard_map/ppermute | solution.py:26
  518.2 10.2 %collective-permute-start.57 = (bf16[96,768]{1,0:T(8,128)(2,1)}, bf16[96,768]{1,0:T(8,128)(2,1)S(1)}, u32[]{:S(2)}, u32[]{:S(2)}) collective-permute-start(bf16[96,768]{1,0:T(8,128)(2,1)} %get-tuple-element.113), channel_id=1, source_target_pairs={{0,8},{4,12},{8,16},{12,20},{16,24},{20,28},{24,0},{28,4},{1,9},{5... | collective-permute-start | bytes 442376 | tf_op jit(solution)/shard_map/ppermute | solution.py:26
  (109 other events, 874.1 us)

commit v2 on v1

--- a/solution.py
+++ b/solution.py
@@ -14,6 +14,7 @@
 F32 = jnp.float32
 BF16 = jnp.bfloat16
 SCALE = HD ** (-0.5)
+MESH = pl.DeviceIdType.MESH
 
 
 def flip(block, axis, bit):
@@ -188,6 +189,344 @@
         d_values.append(mm(probs.astype(BF16), g))
     dk_ref[...] = pair_lanes(d_keys).astype(BF16).reshape(dk_ref.shape)
     dv_ref[...] = pair_lanes(d_values).astype(BF16).reshape(dv_ref.shape)
+
+
+def halves_joined(low, high):
+    lane = lax.broadcasted_iota(jnp.int32, low.shape, 1)
+    return jnp.where(lane < HD, low, pltpu.roll(high, HD, 1))
+
+
+def highs_joined(low, high):
+    lane = lax.broadcasted_iota(jnp.int32, low.shape, 1)
+    return jnp.where(lane < HD, pltpu.roll(low, HD, 1), high)
+
+
+def head_tiles(row_own, row_other):
+    return (
+        row_own[:, :128],
+        row_other[:, :128],
+        halves_joined(row_own[:, 128:256], row_other[:, 128:256]),
+    )
+
+
+def project(x, wa_ref, count):
+    width = x.shape[1]
+    tiles = []
+    for p in range(2):
+        w = wa_ref[p].reshape(width, wa_ref.shape[-1])
+        out = mm(x, w[:, count[0] : count[1]])
+        tiles.append([out[:, 128 * i : 128 * (i + 1)] for i in range(out.shape[1] // 128)])
+    return tiles
+
+
+def forward_own(b, x_ref, wa_ref, bias, q_ref, k_ref, v_ref):
+    rows = x_ref.shape[2] * x_ref.shape[3] * 2
+    x = x_ref[:, b].reshape(rows, x_ref.shape[-1])
+    one, two = project(x, wa_ref, (0, 640))
+    b_query, b_value = bias
+    parts = (
+        (q_ref, (one[0], two[0], halves_joined(one[3], two[3])), b_query),
+        (k_ref, (one[1], two[1], highs_joined(one[3], two[3])), None),
+        (v_ref, (one[2], two[2], halves_joined(one[4], two[4])), b_value),
+    )
+    for ref, tiles, added in parts:
+        for t in range(3):
+            tile = tiles[t] if added is None else tiles[t] + added[t]
+            ref[:, b, :, 128 * t : 128 * (t + 1)] = tile.astype(BF16).reshape(2, rows // 2, 128)
+
+
+def forward_attend(b, xp_ref, wa_ref, bias, swapped, q_ref, k_ref, v_ref, ku_ref, vu_ref, o_ref):
+    rows = xp_ref.shape[2] * xp_ref.shape[3] * 2
+    x = xp_ref[:, b].reshape(rows, xp_ref.shape[-1])
+    one, two = project(x, wa_ref, (128, 640))
+    far_keys = (one[0], two[0], highs_joined(one[2], two[2]))
+    far_values = (one[1], two[1], halves_joined(one[3], two[3]))
+    masks = lane_masks(SCALE)
+    for t in range(3):
+        lanes = slice(128 * t, 128 * (t + 1))
+
+        def load(ref):
+            return ref[:, b, :, lanes].reshape(rows, 128)
+
+        take_far = swapped[t] > 0.5
+        k = jnp.where(take_far, far_keys[t], load(k_ref).astype(F32)).astype(BF16)
+        v = jnp.where(
+            take_far, far_values[t] + bias[1][t], load(v_ref).astype(F32)
+        ).astype(BF16)
+        ku_ref[:, b, :, lanes] = k.reshape(2, rows // 2, 128)
+        vu_ref[:, b, :, lanes] = v.reshape(2, rows // 2, 128)
+        q = load(q_ref)
+        outs = []
+        for mask in masks:
+            s = mm_t(q * mask, k)
+            raised = jnp.exp(s - jnp.max(s, axis=-1, keepdims=True))
+            total = jnp.sum(raised, axis=-1, keepdims=True)
+            outs.append(mm(raised.astype(BF16), v) / total)
+        o_ref[:, b, :, lanes] = pair_lanes(outs).astype(BF16).reshape(2, rows // 2, 128)
+
+
+def forward_listed(b, member, row_ref, col_ref, q_ref, picks_ref, select_ref, qc_ref):
+    slots = row_ref.shape[-1]
+    quarter = q_ref.shape[2] // 2
+    cap = slots // 4
+    row, col = row_ref[b], col_ref[b]
+    bits = quarter.bit_length() - 1
+    run_row = lax.shift_right_arithmetic(row, bits)
+    run_col = lax.shift_right_arithmetic(col, bits)
+    before = lax.broadcasted_iota(jnp.int32, (slots, slots), 0) < lax.broadcasted_iota(
+        jnp.int32, (slots, slots), 1
+    )
+    same = jnp.where(run_col == run_row, jnp.where(before, 1.0, 0.0), 0.0)
+    rank = jnp.sum(same, axis=0, keepdims=True)
+    line = lax.broadcasted_iota(jnp.int32, (slots, 1), 0)
+    place = line // cap
+    wanted_run = jnp.where(
+        place == 0, member, jnp.where(place == 1, member + 2, jnp.where(place == 2, 1 - member, 3 - member))
+    )
+    wanted_rank = (line % cap).astype(F32)
+    picks = jnp.where(run_row == wanted_run, jnp.where(rank == wanted_rank, 1.0, 0.0), 0.0).astype(BF16)
+    lane = lax.broadcasted_iota(jnp.int32, (slots, quarter), 1)
+    places = jnp.where(jnp.bitwise_and(col, quarter - 1) == lane, 1.0, 0.0).astype(BF16)
+    select = mm(picks, places).astype(BF16)
+    picks_ref[b] = picks
+    select_ref[b] = select
+    for s in range(2):
+        for e in range(2):
+            at = (2 * s + e) * cap
+            rows = q_ref[s, b, quarter * e : quarter * (e + 1), :]
+            qc_ref[s, b, cap * e : cap * (e + 1), :] = mm(select[at : at + cap], rows).astype(BF16)
+
+
+def forward_kernel(comm, *refs):
+    if comm:
+        (
+            a_ref, b_ref, t_ref, small_ref, row_ref, col_ref,
+            wa_ref, wb_ref, x_ref, o_ref, k_ref, v_ref, ku_ref, vu_ref, qc_ref, picks_ref, select_ref, far_ref,
+            xp_ref, q_ref, local_sem, send_sem, recv_sem,
+        ) = refs
+    else:
+        (
+            wa_ref, x_ref, xp_ref, small_ref, far_ref, row_ref, col_ref,
+            o_ref, k_ref, v_ref, ku_ref, vu_ref, qc_ref, picks_ref, select_ref,
+            q_ref,
+        ) = refs
+    blocks = x_ref.shape[1]
+    head = lax.axis_index("head")
+    member, pair = lax.rem(head, 2), lax.div(head, 2)
+
+    def listed(b, carry):
+        forward_listed(b, member, row_ref, col_ref, q_ref, picks_ref, select_ref, qc_ref)
+        return carry
+
+    def bias_of():
+        own, other = small_ref[...], far_ref[...]
+        rows = [head_tiles(own[i : i + 1], other[i : i + 1]) for i in range(3)]
+        return (rows[0], rows[1]), rows[2]
+
+    if not comm:
+        bias, swapped = bias_of()
+
+        def own_block(b, carry):
+            forward_own(b, x_ref, wa_ref, bias, q_ref, k_ref, v_ref)
+            return carry
+    if comm:
+        index = lax.axis_index("dp")
+        z, x = lax.div(index, 2), lax.rem(index, 2)
+        x_peer = {"dp": 2 * z + 1 - x}
+        y_peer = {"head": lax.rem(head + 2, 4)}
+        sibling_peer = {"head": 2 * pair + 1 - member}
+        z_peers = [{"dp": lax.rem(index + 2 * k, 8)} for k in (1, 2, 3)]
+        barrier = pltpu.get_barrier_semaphore()
+        for peer in [x_peer, y_peer, sibling_peer] + z_peers:
+            pl.semaphore_signal(barrier, inc=1, device_id=peer, device_id_type=MESH)
+        counter = [0]
+
+        def local(src, dst, i):
+            copy = pltpu.make_async_copy(src, dst, local_sem.at[i])
+            copy.start()
+            return copy
+
+        def send(src, dst, peer):
+            i = counter[0]
+            counter[0] += 1
+            copy = pltpu.make_async_remote_copy(
+                src_ref=src,
+                dst_ref=dst,
+                send_sem=send_sem.at[i],
+                recv_sem=recv_sem.at[i],
+                device_id=peer,
+                device_id_type=MESH,
+            )
+            copy.start()
+            sent.append(copy)
+            return copy
+
+        def far_copy(b):
+            return pltpu.make_async_remote_copy(
+                src_ref=x_ref.at[0, b],
+                dst_ref=xp_ref.at[0, b],
+                send_sem=send_sem.at[15 + b],
+                recv_sem=recv_sem.at[15 + b],
+                device_id=z_peers[1],
+                device_id_type=MESH,
+            )
+
+        def near_copy(b):
+            return pltpu.make_async_remote_copy(
+                src_ref=xp_ref.at[0, b],
+                dst_ref=xp_ref.at[1, b],
+                send_sem=send_sem.at[15 + blocks + b],
+                recv_sem=recv_sem.at[15 + blocks + b],
+                device_id=sibling_peer,
+                device_id_type=MESH,
+            )
+
+        sent = []
+        quarters = (member, member + 2, 1 - member, 3 - member)
+        fills = [
+            local(t_ref.at[pl.ds(blocks * pair, blocks), quarters[2 * s + e]], x_ref.at[s, :, e], 2 * s + e)
+            for s in range(2)
+            for e in range(2)
+        ]
+        fill_a = local(a_ref, wa_ref.at[0, z, x], 4)
+        fill_b = local(b_ref, wb_ref.at[0, :, z, x], 5)
+        pl.semaphore_wait(barrier, 6)
+        a_z = [send(a_ref, wa_ref.at[0, z, x], peer) for peer in z_peers]
+        far = send(small_ref, far_ref, y_peer)
+        b_z = [send(b_ref, wb_ref.at[0, :, z, x], peer) for peer in z_peers]
+        for fill in fills:
+            fill.wait()
+        for b in range(blocks):
+            far_copy(b).start()
+        half = a_ref.shape[0] // 2
+        up, low = pl.ds(0, half), pl.ds(half, half)
+        fill_a.wait()
+        for copy in a_z:
+            copy.wait_recv()
+        a_x = send(wa_ref.at[0, :, x, up], wa_ref.at[0, :, x, up], x_peer)
+        a_y = send(wa_ref.at[0, :, x, low], wa_ref.at[1, :, x, low], y_peer)
+        a_x.wait_recv()
+        a_xy = send(wa_ref.at[0, :, :, up], wa_ref.at[1, :, :, up], y_peer)
+        a_y.wait_recv()
+        a_yx = send(wa_ref.at[:, :, x, low], wa_ref.at[:, :, x, low], x_peer)
+        fill_b.wait()
+        for copy in b_z:
+            copy.wait_recv()
+        b_x = send(wb_ref.at[0, 0, :, x], wb_ref.at[0, 0, :, x], x_peer)
+        b_y = send(wb_ref.at[0, 1, :, x], wb_ref.at[1, 1, :, x], y_peer)
+        far.wait_recv()
+        a_xy.wait_recv()
+        a_yx.wait_recv()
+        bias, swapped = bias_of()
+
+        def own_block(b, carry):
+            forward_own(b, x_ref, wa_ref, bias, q_ref, k_ref, v_ref)
+            return carry
+
+    lax.fori_loop(0, blocks, own_block, 0)
+    lax.fori_loop(0, blocks, listed, 0)
+    if comm:
+        b_x.wait_recv()
+        b_xy = send(wb_ref.at[0, 0], wb_ref.at[1, 0], y_peer)
+        b_y.wait_recv()
+        b_yx = send(wb_ref.at[:, 1, :, x], wb_ref.at[:, 1, :, x], x_peer)
+        def attend_block(b, carry):
+            far_copy(b).wait_recv()
+            near = near_copy(b)
+            near.start()
+            near.wait_recv()
+            forward_attend(b, xp_ref, wa_ref, bias, swapped, q_ref, k_ref, v_ref, ku_ref, vu_ref, o_ref)
+            return carry
+
+        lax.fori_loop(0, blocks, attend_block, 0)
+        b_xy.wait_recv()
+        b_yx.wait_recv()
+        for copy in sent:
+            copy.wait_send()
+        for b in range(blocks):
+            far_copy(b).wait_send()
+            near_copy(b).wait_send()
+    else:
+
+        def attend_block(b, carry):
+            forward_attend(b, xp_ref, wa_ref, bias, swapped, q_ref, k_ref, v_ref, ku_ref, vu_ref, o_ref)
+            return carry
+
+        lax.fori_loop(0, blocks, attend_block, 0)
+
+
+def vmem_spec():
+    return pl.BlockSpec(memory_space=pltpu.VMEM)
+
+
+def any_spec():
+    return pl.BlockSpec(memory_space=pl.ANY)
+
+
+def forward(tokens, piece_a, piece_b, small, listed, member, pair):
+    n = lax.axis_size("dp")
+    block_count, block_rows, width = tokens.shape
+    blocks, quarter = block_count // 2, block_rows // 4
+    slots = listed.shape[1]
+    cap = slots // 4
+    lanes = 6 * HD
+    tokens = tokens.reshape(block_count, 4, quarter, width)
+    row, col = listed[:, None, :], listed[:, :, None]
+    rows_shape = (2, blocks, 2, quarter, width)
+
+    def out(*shape, dtype=BF16):
+        return jax.ShapeDtypeStruct(shape, dtype)
+
+    dense = (2, blocks, 2 * quarter, lanes)
+    tail = [out(*dense)] * 5 + [
+        out(2, blocks, 2 * cap, lanes),
+        out(blocks, slots, slots),
+        out(blocks, slots, quarter),
+    ]
+    params = dict(vmem_limit_bytes=60 * 2**20, has_side_effects=True)
+    if n == 8:
+        shapes = [
+            out(2, 4, 2, *piece_a.shape),
+            out(2, 2, 4, 2, *piece_b.shape[1:]),
+            out(*rows_shape),
+            *tail,
+            out(*small.shape, dtype=F32),
+        ]
+        specs = [vmem_spec()] * len(shapes)
+        specs[1] = any_spec()
+        results = pl.pallas_call(
+            functools.partial(forward_kernel, True),
+            out_shape=shapes,
+            in_specs=[vmem_spec(), vmem_spec(), any_spec()] + [vmem_spec()] * 3,
+            out_specs=specs,
+            scratch_shapes=[
+                pltpu.VMEM(rows_shape, BF16),
+                pltpu.VMEM(dense, BF16),
+                pltpu.SemaphoreType.DMA((6,)),
+                pltpu.SemaphoreType.DMA((15 + 2 * blocks,)),
+                pltpu.SemaphoreType.DMA((15 + 2 * blocks,)),
+            ],
+            compiler_params=pltpu.CompilerParams(collective_id=1, **params),
+        )(piece_a, piece_b, tokens, small, row, col)
+        w_attn, w_feed, rows, *rest, far = results
+    else:
+        mine = pick(tokens.reshape(2, blocks, 2, 2, quarter, width), pair)
+        rows = jnp.stack((pick(mine, member, 2), pick(mine, 1 - member, 2)))
+        w_attn = gather(piece_a, True)
+        w_feed = jnp.stack([gather(piece_b[i], True) for i in range(2)], axis=1)
+        far = across(small)
+        shapes = tail
+        rest = pl.pallas_call(
+            functools.partial(forward_kernel, False),
+            out_shape=shapes,
+            in_specs=[vmem_spec()] * 7,
+            out_specs=[vmem_spec()] * len(shapes),
+            scratch_shapes=[pltpu.VMEM(dense, BF16)],
+            compiler_params=pltpu.CompilerParams(vmem_limit_bytes=60 * 2**20),
+        )(w_attn.reshape(2, width, -1), rows, partner(rows), small, far, row, col)
+    w_attn = w_attn.reshape(2, width, -1)
+    w_feed = w_feed.reshape(2, 2, width, -1)
+    return (w_attn, w_feed, rows, *rest, far)
 
 
 def per_head_pair(kernel, arrays, out_count, out_like, flops):
@@ -247,54 +586,70 @@
     head = lax.axis_index("head")
     c, p = head % 2, head // 2
 
-    piece = jnp.concatenate((query_weight, key_weight, value_weight, out_weight.T), axis=1)
+    out_t = out_weight.T
+    first, last = slice(0, 2 * HD), slice(2 * HD, 3 * HD)
+    piece = jnp.concatenate(
+        (
+            query_weight[:, first],
+            key_weight[:, first],
+            value_weight[:, first],
+            query_weight[:, last],
+            key_weight[:, last],
+            value_weight[:, last],
+            out_t[:, last],
+            out_t[:, first],
+        ),
+        axis=1,
+    )
     half = piece_rows // 2
-    w_one = gather(piece[:half], True)
-    w_two = gather(piece[half:], False)
-    w_attn = jnp.stack((w_one, w_two), axis=2).reshape(2, width, 4, local)
-    w_attn = jnp.transpose(w_attn, (2, 1, 0, 3)).reshape(4, width, columns)
-    w_query, w_key, w_value, w_out_t = (w_attn[i] for i in range(4))
+
+    def line(vector, size):
+        return jnp.pad(vector, (0, size - vector.shape[0]))
+
+    small = jnp.stack(
+        [
+            line(row, hidden_piece)
+            for row in (
+                query_bias,
+                value_bias,
+                jnp.repeat(block_order.astype(F32), HD),
+                up_bias,
+            )
+        ]
+        + [jnp.zeros((hidden_piece,), F32)] * 4
+    )
+    listed = pick(masked_rows.reshape(2, blocks, slots), p)
+    (
+        w_attn, w_feed, x_rows, attention, keys, values, keys_used, values_used, q_compact, picks_b, select_b, small_far,
+    ) = forward(tokens, piece, jnp.stack((up_weight, down_weight.T)), small, listed, c, p)
+
+    def tiles(i, second, j):
+        return jnp.concatenate(
+            (
+                w_attn[0][:, 128 * i : 128 * i + 128],
+                w_attn[1][:, 128 * i : 128 * i + 128],
+                w_attn[0][:, 128 * j + 64 * second : 128 * j + 64 * second + 64],
+                w_attn[1][:, 128 * j + 64 * second : 128 * j + 64 * second + 64],
+            ),
+            axis=1,
+        )
+
+    w_query, w_key, w_value, w_out_t = tiles(0, 0, 3), tiles(1, 1, 3), tiles(2, 0, 4), tiles(5, 1, 4)
     w_out_other = sibling(w_out_t)
-    w_up = gather(up_weight, True).reshape(2, width, hidden_piece)
-    w_down = gather(down_weight.T, False).reshape(2, width, hidden_piece)
-
-    small = jnp.concatenate(
-        (query_bias, value_bias, up_bias, block_order.astype(F32))
-    )
-    small_other = across(small)
-
-    def both(start, size):
-        return jnp.concatenate(
-            (small[start : start + size], small_other[start : start + size])
-        )
-
-    b_query = both(0, local)
-    b_value = both(local, local)
-    b_up = jnp.stack((up_bias, small_other[2 * local : 2 * local + hidden_piece]))
-    swapped = jnp.repeat(both(2 * local + hidden_piece, local // HD) > 0.5, HD)
-
-    mine = pick(tokens.reshape(2, blocks, 2, 2, quarter, width), p)
-    x_rows = jnp.stack((pick(mine, c, 2), pick(mine, 1 - c, 2)))
+    w_up, w_down = w_feed[:, 0], w_feed[:, 1]
+    b_up = jnp.stack((up_bias, small_far[3]))
+    order, order_far = small[2, :local], small_far[2, :local]
+    swapped = (
+        jnp.concatenate((order[:128], order_far[:128], order[128:], order_far[128:])) > 0.5
+    )
     x_flat = x_rows.reshape(-1, width)
-    x_other = partner(x_rows).reshape(-1, width)
     own_count = x_flat.shape[0] // 2
     attn_shape = (2, blocks, 2 * quarter, columns)
     compact_shape = (2, blocks, 2 * cap, columns)
-
-    listed = pick(masked_rows.reshape(2, blocks, slots), p)
-    run = jnp.where(listed >= 0, listed // quarter, -1)
-    earlier = jnp.arange(slots)[:, None] > jnp.arange(slots)[None, :]
-    rank = jnp.sum((run[:, :, None] == run[:, None, :]) & earlier, axis=-1)
-    which = jnp.stack((c, c + 2, 1 - c, 3 - c)).reshape(2, 1, 2, 1, 1)
-    picks = (
-        (run[None, :, None, None, :] == which)
-        & (rank[None, :, None, None, :] == jnp.arange(cap)[:, None])
-    ).astype(BF16)
-    places = (listed[:, :, None] % quarter == jnp.arange(quarter)).astype(BF16)
-    select = jnp.einsum(
-        "sbeki,bir->sbekr", picks, places, preferred_element_type=F32
-    ).astype(BF16)
-    select = select.reshape(-1, cap, quarter)
+    picks = jnp.transpose(picks_b.reshape(blocks, 2, 2, cap, slots), (1, 0, 2, 3, 4))
+    select = jnp.transpose(
+        select_b.reshape(blocks, 2, 2, cap, quarter), (1, 0, 2, 3, 4)
+    ).reshape(-1, cap, quarter)
     runs_own = 2 * blocks
 
     def compact(rows, which=slice(None), **kw):
@@ -326,22 +681,6 @@
         "beki,biw->bekw", picks[0], grads_in, preferred_element_type=F32
     ).reshape(-1, width)
 
-    queries = (mm(x_flat, w_query) + b_query).astype(BF16)
-    keys = mm(x_flat, w_key).astype(BF16)
-    values = (mm(x_flat, w_value) + b_value).astype(BF16)
-    keys_used = jnp.where(swapped, mm(x_other, w_key).astype(BF16), keys)
-    values_used = jnp.where(
-        swapped, (mm(x_other, w_value) + b_value).astype(BF16), values
-    )
-    unit_flops = 4 * block_rows * block_rows * columns * blocks
-    (attention,) = per_head_pair(
-        attend_kernel,
-        [a.reshape(attn_shape) for a in (queries, keys_used, values_used)],
-        1,
-        queries.reshape(attn_shape),
-        unit_flops,
-    )
-    q_compact = compact(queries).astype(BF16).reshape(compact_shape)
     q_far = partner(q_compact)
     swapped_lanes = swapped[None, None, None, :]
     attn_other = sibling(attention[1]).reshape(own_count, columns)
@@ -466,7 +805,12 @@
         ),
         axis=1,
     )
-    g_attn = jnp.transpose(g_attn.reshape(width, 4, 2, local), (2, 0, 1, 3)).reshape(
+    g_attn = jnp.stack(
+        (
+            jnp.concatenate((g_attn[..., 0:128], g_attn[..., 256:320]), axis=-1),
+            jnp.concatenate((g_attn[..., 128:256], g_attn[..., 320:384]), axis=-1),
+        )
+    ).reshape(
         2, width // piece_rows, 2, half, 4 * local
     )
     s_attn = jnp.concatenate(
@@ -477,7 +821,13 @@
     )
 
     def widen(own_first, size):
-        own_first = own_first.reshape(2, -1)
+        if own_first.shape[0] != 2:
+            own_first = jnp.stack(
+                (
+                    jnp.concatenate((own_first[0:128], own_first[256:320])),
+                    jnp.concatenate((own_first[128:256], own_first[320:384])),
+                )
+            )
         by_p = ordered(p, own_first[0], own_first[1])
         zero = jnp.zeros_like(by_p)
         return jnp.where(

time: 539 us -> 440 us (0.82)
  Pallas kernels: 35 us -> 133 us
  waiting for transfers between devices: 117 us -> 37.4 us
  local copies, waits for them, and re-layouts: 118 us -> 79.6 us
  starting transfers between devices: 81.7 us -> 43.4 us
  matrix products: 113 us -> 89.6 us
  other arithmetic: 63.8 us -> 47.3 us
    pallas_call x0 -> x1, Pallas kernels: none -> 110 us  [forward(): pl.pallas_call(functools.partial(forward_kernel, True), out_shape=shapes,...]
    ppermute x30 -> x17, waiting for transfers between devices: 85.7 us -> 17.2 us  [shift(): lax.ppermute(block, axis, [(i, (i + distance) % n) for i in range(n)])]
    ppermute x30 -> x17, starting transfers between devices: 56.6 us -> 29.7 us  [shift(): lax.ppermute(block, axis, [(i, (i + distance) % n) for i in range(n)])]
    slice x12 -> x16, local copies, waits for them, and re-layouts: 29.3 us -> 8.69 us  [the longest x1 1.34 us: per_device(): b_up = jnp.stack((up_bias, small_far[3]))]
    dot_general x10 -> x5, matrix products: 24.8 us -> 10.3 us  [mm(): return jnp.dot(a, b, preferred_element_type=F32)]
    another operation x11 -> x8, local copies, waits for them, and re-layouts: 21.9 us -> 9.37 us  [the longest x2 8.02 us: per_device(): jnp.stack((jnp.concatenate((g_attn[..., 0:128], g_attn[..., 256:320]), ax...]
    pallas_call x3 -> x2, Pallas kernels: 35 us -> 23.2 us  [per_head_pair(): pl.pallas_call(kernel, grid=(blocks, width // (2 * HD)), in_specs=[spec(a...]
    ppermute x30 -> x21, starting transfers between devices: 25 us -> 13.7 us  [flip(): return lax.ppermute(block, axis, [(i, i ^ bit) for i in range(n)])]
  transfers between devices with their start and end apart: 60 -> 38, of which waited for: 20 -> 12; matrix products, arithmetic and copies ran while one was open for 54% -> 45% of each run, Pallas kernels for 7% -> 5%
where the time goes in v2:
time: 440 us; the launch traced here: 433 us
  Pallas kernels  133 us (30%)
  matrix products  89.6 us (20%)
  local copies, waits for them, and re-layouts  79.6 us (18%)
  other arithmetic  47.3 us (11%)
  starting transfers between devices  43.4 us (10%)
  waiting for transfers between devices  37.4 us (8%)
    pallas_call x1, Pallas kernels, forward(): pl.pallas_call(functools.partial(forward_kernel, True), out_shape=shapes,...  110 us
    dot_general x9, matrix products, mm_t(): lax.dot_general(a, b, (((1,), (1,)), ((), ())), preferred_element_type=F32)  53 us
    ppermute x17, starting transfers between devices, shift(): lax.ppermute(block, axis, [(i, (i + distance) % n) for i in range(n)])  29.7 us
    pallas_call x2, Pallas kernels, per_head_pair(): pl.pallas_call(kernel, grid=(blocks, width // (2 * HD)), in_specs=[spec(a...  23.2 us
    ppermute x21, waiting for transfers between devices, flip(): return lax.ppermute(block, axis, [(i, i ^ bit) for i in range(n)])  20.2 us
    unnamed x184, local copies, waits for them, and re-layouts  19.2 us
    ppermute x17, waiting for transfers between devices, shift(): lax.ppermute(block, axis, [(i, (i + distance) % n) for i in range(n)])  17.2 us
    dot_general x8, matrix products, t_mm(): lax.dot_general(a, b, (((0,), (0,)), ((), ())), preferred_element_type=F32)  13.7 us
  transfers between devices with their start and end apart: 38, of which 12 were waited for; matrix products, arithmetic and copies ran while one was open for 45% of the time, Pallas kernels for 5%

profile of v2, /device:TPU:0, one launch (start us, length us, event | category | flops | bytes accessed | tf_op | source)
XLA Modules:
  0.0 433.2 jit_solution(12103077462925902099)
XLA Ops:
  11.1 1.7 pad_maximum_fusion.15.refs_1_
  14.2 110.2 %shard_map.314 = (bf16[2,4,2,96,768]{4,3,2,1,0:T(8,128)(2,1)}, bf16[2,2,4,2,96,768]{5,4,3,2,1,0:T(8,128)(2,1)}, bf16[2,3,2,128,768]{4,3,2,1,0:T(8,128)(2,1)}, bf...) custom-call(bf16[96,768]{1,0:T(8,128)(2,1)} %concatenate.140.refs_0_, ...), custom_call_target="tpu_custom_call" | custom-call | tf_op jit(solution)/shard_map/pallas_call | solution.py:497
  141.8 2.4 convolution_convert_fusion.9
  146.7 18.2 %fusion.36 = f32[1536,768]{1,0:T(8,128)} fusion(f32[768]{0:T(1024)} %param.30, bf16[768,768]{1,0:T(8,128)(2,1)} %collective-permute-done.2, bf16[768,768]{1,0:T(8,128)(2,1)} %fusion.35, bf16[2,2,768,768]{3,2,1,0:T(8,128)(2,1)} %bitcast.330), kind=kOutput, calls=%fused_computation.77 | convolution fusion | flops 3706454016 | bytes 9441280 | tf_op jit(solution)/shard_map/dot_general | solution.py:57
  164.9 18.2 %convolution_add_fusion = f32[1536,768]{1,0:T(8,128)} fusion(f32[1536,768]{1,0:T(8,128)} %fusion.36, f32[768]{0:T(1024)} %slice_reduce_fusion, bf16[768,768]{1,0:T(8,128)(2,1)} %collective-permute-done.2, bf16[768,768]{1,0:T(8,128)(2,1)} %fusion.35, bf16[2,2,768,768]{3,2,1,0:T(8,128)(2,1)} %bitcast.331), kind=kOutput, calls=%fused_computation.39 | convolution fusion | flops 3707633664 | bytes 14159872 | tf_op jit(solution)/shard_map/dot_general | solution.py:57
  183.1 2.8 slice.514
  189.3 2.1 add_convert_fusion.1
  191.4 1.7 convolution_convert_fusion.11
  193.1 3.1 convolution_add_fusion.3
  196.2 2.9 convolution_add_fusion.2
  199.2 2.8 fusion.195
  206.6 2.1 multiply_reduce_fusion
  209.3 2.9 multiply_reduce_fusion.2
  216.7 2.4 fusion.192
  223.5 2.2 convert_reduce_fusion.2
  225.8 2.2 fusion.67
  239.0 1.9 convolution_convert_fusion.3
  243.5 1.9 multiply_reduce_fusion.3
  249.1 2.7 collective-permute-start.9
  251.8 11.1 %shard_map.315 = bf16[2,3,64,384]{3,2,1,0:T(8,128)(2,1)} custom-call(bf16[2,3,64,384]{3,2,1,0:T(8,128)(2,1)} %get-tuple-element.37.q_ref, bf16[2,3,64,384]{3,2,1,0:T(8,128)(2,1)} %bitcast.43.g_ref, bf16[2,3,256,384]{3,2,1,0:T(8,128)(2,1)} %get-tuple-element.39.k_ref, bf16[2,3,256,384]{3,2,1,0:T(8,128)(2,1)} %get-tuple-element.40.v_ref), custom_call_target="tpu_custom_call" | custom-call | flops 452984832 | bytes 3244032 | tf_op jit(solution)/shard_map/pallas_call | solution.py:541
  264.0 2.5 convolution_convert_fusion.4
  269.3 5.2 %fusion.69 = f32[1536,768]{1,0:T(8,128)} fusion(bf16[1536,384]{1,0:T(8,128)(2,1)} %bitcast.304, bf16[768,64]{1,0:T(8,128)(2,1)} %get-tuple-element.184, bf16[768,64]{1,0:T(8,128)(2,1)} %get-tuple-element.118, bf16[768,128]{1,0:T(8,128)(2,1)} %get-tuple-element.180, bf16[768,128]{1,0:T(8,128)(2,1)} %get-tuple-element.110), kind=kOutput, calls=%fused_computation.152 | convolution fusion | flops 908328960 | bytes 6488064 | tf_op jit(solution)/shard_map/dot_general | solution.py:57
  275.9 2.0 fusion.40
  277.9 2.1 broadcast_select_fusion
  280.0 12.0 %shard_map.316 = (bf16[2,3,256,384]{3,2,1,0:T(8,128)(2,1)}, bf16[2,3,256,384]{3,2,1,0:T(8,128)(2,1)}) custom-call(bf16[2,3,64,384]{3,2,1,0:T(8,128)(2,1)} %get-tuple-element.167.q_ref, bf16[2,3,64,384]{3,2,1,0:T(8,128)(2,1)} %get-tuple-element.166.g_ref, bf16[2,3,256,384]{3,2,1,0:T(8,128)(2,1)} %get-tuple-element.41.k_ref, ...), custom_call_target="tpu_custom_call" | custom-call | flops 603979776 | bytes 5308416 | tf_op jit(solution)/shard_map/pallas_call | solution.py:541
  293.6 4.1 fusion.42
  297.7 2.0 fusion.41
  312.1 3.1 fusion.77
  316.9 3.6 add_add_fusion
  324.6 3.6 copy.51
  328.2 4.0 stack.148
  332.2 3.6 copy.50
  335.8 4.0 stack.147
  342.8 1.7 collective-permute-done.24
  344.6 6.9 %collective-permute-start.26 = (f32[9216]{0:T(1024)S(1)}, f32[9216]{0:T(1024)S(1)}, u32[]{:S(2)}, u32[]{:S(2)}) collective-permute-start(f32[9216]{0:T(1024)S(1)} %add.426), channel_id=1, source_target_pairs={{0,8},{4,12},{8,16},{12,20},{16,24},{20,28},{24,0},{28,4},{1,9},{5... | collective-permute-start | bytes 110600 | tf_op jit(solution)/shard_map/ppermute | solution.py:27
  353.1 1.9 slice.513
  359.0 1.7 fusion.34
  364.7 6.9 %collective-permute-done.17 = bf16[2,4,48,768]{3,2,1,0:T(8,128)(2,1)S(1)} collective-permute-done((bf16[2,4,48,768]{3,2,1,0:T(8,128)(2,1)S(1)}, bf16[2,4,48,768]{3,2,1,0:T(8,128)(2,1)S(1)}, u32[]{:S(2)}, u32[]{:S(2)}) %collective-permute-start.17) | collective-permute-done | bytes 589856 | tf_op jit(solution)/shard_map/ppermute | solution.py:22
  374.2 10.0 %collective-permute-done.29 = bf16[4,96,768]{2,1,0:T(8,128)(2,1)S(1)} collective-permute-done((bf16[4,96,768]{2,1,0:T(8,128)(2,1)S(1)}, bf16[4,96,768]{2,1,0:T(8,128)(2,1)S(1)}, u32[]{:S(2)}, u32[]{:S(2)}) %collective-permute-start.29) | collective-permute-done | bytes 589856 | tf_op jit(solution)/shard_map/ppermute | solution.py:22
  385.3 2.8 collective-permute-start.32
  390.5 2.9 collective-permute-start.21
  395.9 4.3 collective-permute-start.16
  402.4 2.1 collective-permute-start.31
  404.6 8.5 %collective-permute-done.15 = bf16[48,768]{1,0:T(8,128)(2,1)S(1)} collective-permute-done((bf16[48,768]{1,0:T(8,128)(2,1)S(1)}, bf16[48,768]{1,0:T(8,128)(2,1)S(1)}, u32[]{:S(2)}, u32[]{:S(2)}) %collective-permute-start.15) | collective-permute-done | bytes 73760 | tf_op jit(solution)/shard_map/ppermute | solution.py:27
  413.1 3.8 collective-permute-start.37
  422.4 1.9 fusion.111
  424.3 5.3 %collective-permute-done.36 = bf16[96,768]{1,0:T(8,128)(2,1)S(1)} collective-permute-done((bf16[96,768]{1,0:T(8,128)(2,1)}, bf16[96,768]{1,0:T(8,128)(2,1)S(1)}, u32[]{:S(2)}, u32[]{:S(2)}) %collective-permute-start.36) | collective-permute-done | bytes 147488 | tf_op jit(solution)/shard_map/ppermute | solution.py:27
  429.7 1.8 fusion.109
  (397 shorter events, 120.6 us)
Async XLA Ops:
  0.7 208.6 %copy-start = (bf16[6,128,768]{2,1,0:T(8,128)(2,1)S(1)}, bf16[6,128,768]{2,1,0:T(8,128)(2,1)}, u32[]{:S(2)}) copy-start(bf16[6,128,768]{2,1,0:T(8,128)(2,1)} %param.37) | copy-start | bytes 3538948
  126.0 7.1 %collective-permute-start = (bf16[3,256,384]{2,1,0:T(8,128)(2,1)S(1)}, bf16[3,256,384]{2,1,0:T(8,128)(2,1)S(1)}, u32[]{:S(2)}, u32[]{:S(2)}) collective-permute-start(bf16[3,256,384]{2,1,0:T(8,128)(2,1)S(1)} %get-tuple-element.124), channel_id=1, source_target_pairs={{0,1},{1,0},{2,3},{3,2},{4,5},{5,4},{6,7},{7,6},{8,9},{9,8},{10,11... | collective-permute-start | bytes 1769480 | tf_op jit(solution)/shard_map/ppermute | solution.py:22
  129.3 3.8 collective-permute-start.1
  129.4 148.4 %collective-permute-start.8 = (bf16[2,3,64,384]{3,2,1,0:T(8,128)(2,1)}, bf16[2,3,64,384]{3,2,1,0:T(8,128)(2,1)}, u32[]{:S(2)}, u32[]{:S(2)}) collective-permute-start(bf16[2,3,64,384]{3,2,1,0:T(8,128)(2,1)} %get-tuple-element.37.q_ref), channel_id=1, source_target_pairs={{0,16},{4,20},{8,24},{12,28},{16,0},{20,4},{24,8},{28,12},{1,17},{... | collective-permute-start | bytes 884744 | tf_op jit(solution)/shard_map/ppermute | solution.py:27
  136.3 10.4 %collective-permute-start.2 = (bf16[768,768]{1,0:T(8,128)(2,1)}, bf16[768,768]{1,0:T(8,128)(2,1)}, u32[]{:S(2)}, u32[]{:S(2)}) collective-permute-start(bf16[768,768]{1,0:T(8,128)(2,1)} %fusion.35), channel_id=1, source_target_pairs={{0,1},{1,0},{2,3},{3,2},{4,5},{5,4},{6,7},{7,6},{8,9},{9,8},{10,11... | collective-permute-start | bytes 3538952 | tf_op jit(solution)/shard_map/ppermute | solution.py:22
  185.9 13.2 %collective-permute-start.3 = (bf16[768,768]{1,0:T(8,128)(2,1)}, bf16[768,768]{1,0:T(8,128)(2,1)}, u32[]{:S(2)}, u32[]{:S(2)}) collective-permute-start(bf16[768,768]{1,0:T(8,128)(2,1)} %slice.514), channel_id=1, source_target_pairs={{0,1},{1,0},{2,3},{3,2},{4,5},{5,4},{6,7},{7,6},{8,9},{9,8},{10,11... | collective-permute-start | bytes 3538952 | tf_op jit(solution)/shard_map/ppermute | solution.py:22
  208.7 10.9 %copy-start.2 = (f32[768,768]{1,0:T(8,128)S(1)}, f32[768,768]{1,0:T(8,128)}, u32[]{:S(2)}) copy-start(f32[768,768]{1,0:T(8,128)} %copy-done.1) | copy-start | bytes 7077892
  219.1 8.9 %copy-start.53 = (bf16[192,768]{1,0:T(8,128)(2,1)}, bf16[192,768]{1,0:T(8,128)(2,1)S(1)}, u32[]{:S(2)}) copy-start(bf16[192,768]{1,0:T(8,128)(2,1)S(1)} %get-tuple-element.92) | copy-start | bytes 884740
  219.1 4.4 %collective-permute-start.5 = (bf16[192,768]{1,0:T(8,128)(2,1)S(1)}, bf16[192,768]{1,0:T(8,128)(2,1)S(1)}, u32[]{:S(2)}, u32[]{:S(2)}) collective-permute-start(bf16[192,768]{1,0:T(8,128)(2,1)S(1)} %get-tuple-element.92), channel_id=1, source_target_pairs={{0,1},{1,0},{2,3},{3,2},{4,5},{5,4},{6,7},{7,6},{8,9},{9,8},{10,11... | collective-permute-start | bytes 884744 | tf_op jit(solution)/shard_map/ppermute | solution.py:22
  222.0 18.9 %collective-permute-start.4 = (bf16[3,128,768]{2,1,0:T(8,128)(2,1)}, bf16[3,128,768]{2,1,0:T(8,128)(2,1)}, u32[]{:S(2)}, u32[]{:S(2)}) collective-permute-start(bf16[3,128,768]{2,1,0:T(8,128)(2,1)} %dynamic-slice_bitcast_fusion.3), channel_id=1, source_target_pairs={{0,2},{1,3},{2,0},{3,1},{4,6},{5,7},{6,4},{7,5},{8,10},{9,11},{10,... | collective-permute-start | bytes 1769480 | tf_op jit(solution)/shard_map/ppermute | solution.py:22
  231.3 12.2 %collective-permute-start.6 = (bf16[192,768]{1,0:T(8,128)(2,1)}, bf16[192,768]{1,0:T(8,128)(2,1)}, u32[]{:S(2)}, u32[]{:S(2)}) collective-permute-start(bf16[192,768]{1,0:T(8,128)(2,1)} %slice.515), channel_id=1, source_target_pairs={{0,1},{1,0},{2,3},{3,2},{4,5},{5,4},{6,7},{7,6},{8,9},{9,8},{10,11... | collective-permute-start | bytes 884744 | tf_op jit(solution)/shard_map/ppermute | solution.py:22
  234.0 125.0 %collective-permute-start.28 = (bf16[4,2,96,768]{3,2,0,1:T(8,128)(2,1)}, bf16[4,2,96,768]{3,2,0,1:T(8,128)(2,1)}, u32[]{:S(2)}, u32[]{:S(2)}) collective-permute-start(bf16[4,2,96,768]{3,2,0,1:T(8,128)(2,1)} %copy.55), channel_id=1, source_target_pairs={{0,2},{1,3},{2,0},{3,1},{4,6},{5,7},{6,4},{7,5},{8,10},{9,11},{10,... | collective-permute-start | bytes 3538952 | tf_op jit(solution)/shard_map/ppermute | solution.py:22
  238.1 123.6 %collective-permute-start.33 = (bf16[2,4,96,768]{3,2,1,0:T(8,128)(2,1)}, bf16[2,4,96,768]{3,2,1,0:T(8,128)(2,1)}, u32[]{:S(2)}, u32[]{:S(2)}) collective-permute-start(bf16[2,4,96,768]{3,2,1,0:T(8,128)(2,1)} %fusion.60), channel_id=1, source_target_pairs={{0,4},{4,0},{8,12},{12,8},{16,20},{20,16},{24,28},{28,24},{1,5},{5... | collective-permute-start | bytes 3538952 | tf_op jit(solution)/shard_map/ppermute | solution.py:22
  246.3 1.6 collective-permute-start.7
  249.1 28.8 %collective-permute-start.9 = (bf16[2,3,64,384]{3,2,1,0:T(8,128)(2,1)}, bf16[2,3,64,384]{3,2,1,0:T(8,128)(2,1)}, u32[]{:S(2)}, u32[]{:S(2)}) collective-permute-start(bf16[2,3,64,384]{3,2,1,0:T(8,128)(2,1)} %bitcast.43.g_ref), channel_id=1, source_target_pairs={{0,16},{4,20},{8,24},{12,28},{16,0},{20,4},{24,8},{28,12},{1,17},{... | collective-permute-start | bytes 884744 | tf_op jit(solution)/shard_map/ppermute | solution.py:27
  297.7 11.8 %copy-start.64 = (f32[768]{0:T(1024)S(1)}, f32[768]{0:T(1024)}, u32[]{:S(2)}) copy-start(f32[768]{0:T(1024)} %get-tuple-element.79) | copy-start | bytes 9220
  312.1 8.5 %collective-permute-start.22 = (f32[9216]{0:T(1024)}, f32[9216]{0:T(1024)S(1)}, u32[]{:S(2)}, u32[]{:S(2)}) collective-permute-start(f32[9216]{0:T(1024)} %constant_dynamic-update-slice_fusion), channel_id=1, source_target_pairs={{0,1},{1,0},{2,3},{3,2},{4,5},{5,4},{6,7},{7,6},{8,9},{9,8},{10,11... | collective-permute-start | bytes 110600 | tf_op jit(solution)/shard_map/ppermute | solution.py:22
  321.9 17.9 %collective-permute-start.23 = (f32[9216]{0:T(1024)}, f32[9216]{0:T(1024)}, u32[]{:S(2)}, u32[]{:S(2)}) collective-permute-start(f32[9216]{0:T(1024)} %add.424), channel_id=1, source_target_pairs={{0,2},{1,3},{2,0},{3,1},{4,6},{5,7},{6,4},{7,5},{8,10},{9,11},{10,... | collective-permute-start | bytes 110600 | tf_op jit(solution)/shard_map/ppermute | solution.py:22
  340.6 12.5 %copy-start.5 = (bf16[1,8,2,48,768]{4,3,2,1,0:T(8,128)(2,1)S(1)}, bf16[1,8,2,48,768]{4,3,2,1,0:T(8,128)(2,1)}, u32[]{:S(2)}) copy-start(bf16[1,8,2,48,768]{4,3,2,1,0:T(8,128)(2,1)} %stack.148) | copy-start | bytes 3538948
  340.6 4.0 collective-permute-start.24
  344.6 10.4 %collective-permute-start.26 = (f32[9216]{0:T(1024)S(1)}, f32[9216]{0:T(1024)S(1)}, u32[]{:S(2)}, u32[]{:S(2)}) collective-permute-start(f32[9216]{0:T(1024)S(1)} %add.426), channel_id=1, source_target_pairs={{0,8},{4,12},{8,16},{12,20},{16,24},{20,28},{24,0},{28,4},{1,9},{5... | collective-permute-start | bytes 110600 | tf_op jit(solution)/shard_map/ppermute | solution.py:27
  351.5 4.0 collective-permute-start.27
  351.8 4.9 %collective-permute-start.25 = (f32[9216]{0:T(1024)S(1)}, f32[9216]{0:T(1024)S(1)}, u32[]{:S(2)}, u32[]{:S(2)}) collective-permute-start(f32[9216]{0:T(1024)S(1)} %add.426), channel_id=1, source_target_pairs={{0,16},{4,20},{8,24},{12,28},{16,0},{20,4},{24,8},{28,12},{1,17},{... | collective-permute-start | bytes 110600 | tf_op jit(solution)/shard_map/ppermute | solution.py:27
  355.0 62.0 %collective-permute-start.10 = (bf16[768,768]{1,0:T(8,128)(2,1)S(1)}, bf16[768,768]{1,0:T(8,128)(2,1)S(1)}, u32[]{:S(2)}, u32[]{:S(2)}) collective-permute-start(bf16[768,768]{1,0:T(8,128)(2,1)S(1)} %slice.513), channel_id=1, source_target_pairs={{0,1},{1,0},{2,3},{3,2},{4,5},{5,4},{6,7},{7,6},{8,9},{9,8},{10,11... | collective-permute-start | bytes 3538952 | tf_op jit(solution)/shard_map/ppermute | solution.py:22
  355.4 16.2 %collective-permute-start.17 = (bf16[2,4,48,768]{3,2,1,0:T(8,128)(2,1)S(1)}, bf16[2,4,48,768]{3,2,1,0:T(8,128)(2,1)S(1)}, u32[]{:S(2)}, u32[]{:S(2)}) collective-permute-start(bf16[2,4,48,768]{3,2,1,0:T(8,128)(2,1)S(1)} %dynamic-slice_bitcast_fusion.1), channel_id=1, source_target_pairs={{0,4},{4,0},{8,12},{12,8},{16,20},{20,16},{24,28},{28,24},{1,5},{5... | collective-permute-start | bytes 1769480 | tf_op jit(solution)/shard_map/ppermute | solution.py:22
  356.6 16.2 %collective-permute-start.12 = (bf16[4,2,48,768]{3,2,1,0:T(8,128)(2,1)S(1)}, bf16[4,2,48,768]{3,2,1,0:T(8,128)(2,1)S(1)}, u32[]{:S(2)}, u32[]{:S(2)}) collective-permute-start(bf16[4,2,48,768]{3,2,1,0:T(8,128)(2,1)S(1)} %bitcast.348), channel_id=1, source_target_pairs={{0,2},{1,3},{2,0},{3,1},{4,6},{5,7},{6,4},{7,5},{8,10},{9,11},{10,... | collective-permute-start | bytes 1769480 | tf_op jit(solution)/shard_map/ppermute | solution.py:22
  360.8 23.5 %collective-permute-start.29 = (bf16[4,96,768]{2,1,0:T(8,128)(2,1)S(1)}, bf16[4,96,768]{2,1,0:T(8,128)(2,1)S(1)}, u32[]{:S(2)}, u32[]{:S(2)}) collective-permute-start(bf16[4,96,768]{2,1,0:T(8,128)(2,1)S(1)} %dynamic-slice_bitcast_fusion), channel_id=1, source_target_pairs={{0,4},{4,0},{8,12},{12,8},{16,20},{20,16},{24,28},{28,24},{1,5},{5... | collective-permute-start | bytes 1769480 | tf_op jit(solution)/shard_map/ppermute | solution.py:22
  361.8 11.1 %slice-start.4 = ((bf16[1,8,2,48,768]{4,3,2,1,0:T(8,128)(2,1)}), bf16[1,8,1,48,768]{4,3,2,1,0:T(8,128)(2,1)S(1)}, s32[]{:S(2)}) async-start(bf16[1,8,2,48,768]{4,3,2,1,0:T(8,128)(2,1)} %stack.147), calls=%async_computation.4 | async-start | bytes 1179648 | tf_op jit(solution)/shard_map/slice | solution.py:111
  363.4 53.6 %slice-start.2 = ((s8[4718592]{0:T(1024)(128)(4,1)}), s8[4194304]{0:T(1024)(128)(4,1)S(1)}, s32[]{:S(2)}) async-start(s8[4718592]{0:T(1024)(128)(4,1)} %bitcast.297), calls=%async_computation.2 | async-start | bytes 8388608
  363.5 24.7 %collective-permute-start.34 = (bf16[4,96,768]{2,1,0:T(8,128)(2,1)S(1)}, bf16[4,96,768]{2,1,0:T(8,128)(2,1)S(1)}, u32[]{:S(2)}, u32[]{:S(2)}) collective-permute-start(bf16[4,96,768]{2,1,0:T(8,128)(2,1)S(1)} %slice_bitcast_fusion.16), channel_id=1, source_target_pairs={{0,2},{1,3},{2,0},{3,1},{4,6},{5,7},{6,4},{7,5},{8,10},{9,11},{10,... | collective-permute-start | bytes 1769480 | tf_op jit(solution)/shard_map/ppermute | solution.py:22
  371.8 18.5 %collective-permute-start.18 = (bf16[4,48,768]{2,1,0:T(8,128)(2,1)S(1)}, bf16[4,48,768]{2,1,0:T(8,128)(2,1)S(1)}, u32[]{:S(2)}, u32[]{:S(2)}) collective-permute-start(bf16[4,48,768]{2,1,0:T(8,128)(2,1)S(1)} %slice_bitcast_fusion.19), channel_id=1, source_target_pairs={{0,2},{1,3},{2,0},{3,1},{4,6},{5,7},{6,4},{7,5},{8,10},{9,11},{10,... | collective-permute-start | bytes 884744 | tf_op jit(solution)/shard_map/ppermute | solution.py:22
  373.0 44.0 %slice-start.3 = ((s8[4718592]{0:T(1024)(128)(4,1)}), s8[524288]{0:T(1024)(128)(4,1)S(1)}, s32[]{:S(2)}) async-start(s8[4718592]{0:T(1024)(128)(4,1)} %bitcast.297), calls=%async_computation.3 | async-start | bytes 1048576
  373.0 20.6 %collective-permute-start.13 = (bf16[4,48,768]{2,1,0:T(8,128)(2,1)S(1)}, bf16[4,48,768]{2,1,0:T(8,128)(2,1)S(1)}, u32[]{:S(2)}, u32[]{:S(2)}) collective-permute-start(bf16[4,48,768]{2,1,0:T(8,128)(2,1)S(1)} %dynamic-slice_bitcast_fusion.4), channel_id=1, source_target_pairs={{0,4},{4,0},{8,12},{12,8},{16,20},{20,16},{24,28},{28,24},{1,5},{5... | collective-permute-start | bytes 884744 | tf_op jit(solution)/shard_map/ppermute | solution.py:22
  385.3 36.5 %collective-permute-start.32 = (bf16[96,768]{1,0:T(8,128)(2,1)}, bf16[96,768]{1,0:T(8,128)(2,1)}, u32[]{:S(2)}, u32[]{:S(2)}) collective-permute-start(bf16[96,768]{1,0:T(8,128)(2,1)} %get-tuple-element.130), channel_id=1, source_target_pairs={{0,24},{4,28},{8,0},{12,4},{16,8},{20,12},{24,16},{28,20},{1,25},{... | collective-permute-start | bytes 442376 | tf_op jit(solution)/shard_map/ppermute | solution.py:27
  388.3 28.7 %copy-start.24 = (bf16[4,96,768]{2,1,0:T(8,128)(2,1)}, bf16[4,96,768]{2,1,0:T(8,128)(2,1)S(1)}, u32[]{:S(2)}) copy-start(bf16[4,96,768]{2,1,0:T(8,128)(2,1)S(1)} %fusion.63) | copy-start | bytes 1769476
  390.5 5.4 %collective-permute-start.21 = (bf16[48,768]{1,0:T(8,128)(2,1)S(1)}, bf16[48,768]{1,0:T(8,128)(2,1)S(1)}, u32[]{:S(2)}, u32[]{:S(2)}) collective-permute-start(bf16[48,768]{1,0:T(8,128)(2,1)S(1)} %get-tuple-element.137), channel_id=1, source_target_pairs={{0,24},{4,28},{8,0},{12,4},{16,8},{20,12},{24,16},{28,20},{1,25},{... | collective-permute-start | bytes 221192 | tf_op jit(solution)/shard_map/ppermute | solution.py:27
  393.4 8.1 %collective-permute-start.20 = (bf16[48,768]{1,0:T(8,128)(2,1)S(1)}, bf16[48,768]{1,0:T(8,128)(2,1)S(1)}, u32[]{:S(2)}, u32[]{:S(2)}) collective-permute-start(bf16[48,768]{1,0:T(8,128)(2,1)S(1)} %get-tuple-element.138), channel_id=1, source_target_pairs={{0,16},{4,20},{8,24},{12,28},{16,0},{20,4},{24,8},{28,12},{1,17},{... | collective-permute-start | bytes 221192 | tf_op jit(solution)/shard_map/ppermute | solution.py:27
  393.6 8.0 %collective-permute-start.19 = (bf16[48,768]{1,0:T(8,128)(2,1)S(1)}, bf16[48,768]{1,0:T(8,128)(2,1)S(1)}, u32[]{:S(2)}, u32[]{:S(2)}) collective-permute-start(bf16[48,768]{1,0:T(8,128)(2,1)S(1)} %get-tuple-element.136), channel_id=1, source_target_pairs={{0,8},{4,12},{8,16},{12,20},{16,24},{20,28},{24,0},{28,4},{1,9},{5... | collective-permute-start | bytes 221192 | tf_op jit(solution)/shard_map/ppermute | solution.py:27
  395.9 6.5 %collective-permute-start.16 = (bf16[48,768]{1,0:T(8,128)(2,1)S(1)}, bf16[48,768]{1,0:T(8,128)(2,1)S(1)}, u32[]{:S(2)}, u32[]{:S(2)}) collective-permute-start(bf16[48,768]{1,0:T(8,128)(2,1)S(1)} %get-tuple-element.140), channel_id=1, source_target_pairs={{0,24},{4,28},{8,0},{12,4},{16,8},{20,12},{24,16},{28,20},{1,25},{... | collective-permute-start | bytes 221192 | tf_op jit(solution)/shard_map/ppermute | solution.py:27
  401.5 11.6 %collective-permute-start.15 = (bf16[48,768]{1,0:T(8,128)(2,1)S(1)}, bf16[48,768]{1,0:T(8,128)(2,1)S(1)}, u32[]{:S(2)}, u32[]{:S(2)}) collective-permute-start(bf16[48,768]{1,0:T(8,128)(2,1)S(1)} %get-tuple-element.141), channel_id=1, source_target_pairs={{0,16},{4,20},{8,24},{12,28},{16,0},{20,4},{24,8},{28,12},{1,17},{... | collective-permute-start | bytes 221192 | tf_op jit(solution)/shard_map/ppermute | solution.py:27
  401.5 11.6 %collective-permute-start.14 = (bf16[48,768]{1,0:T(8,128)(2,1)S(1)}, bf16[48,768]{1,0:T(8,128)(2,1)S(1)}, u32[]{:S(2)}, u32[]{:S(2)}) collective-permute-start(bf16[48,768]{1,0:T(8,128)(2,1)S(1)} %get-tuple-element.139), channel_id=1, source_target_pairs={{0,8},{4,12},{8,16},{12,20},{16,24},{20,28},{24,0},{28,4},{1,9},{5... | collective-permute-start | bytes 221192 | tf_op jit(solution)/shard_map/ppermute | solution.py:27
  402.4 19.4 %collective-permute-start.31 = (bf16[96,768]{1,0:T(8,128)(2,1)}, bf16[96,768]{1,0:T(8,128)(2,1)}, u32[]{:S(2)}, u32[]{:S(2)}) collective-permute-start(bf16[96,768]{1,0:T(8,128)(2,1)} %get-tuple-element.131), channel_id=1, source_target_pairs={{0,16},{4,20},{8,24},{12,28},{16,0},{20,4},{24,8},{28,12},{1,17},{... | collective-permute-start | bytes 442376 | tf_op jit(solution)/shard_map/ppermute | solution.py:27
  413.1 9.3 %collective-permute-start.30 = (bf16[96,768]{1,0:T(8,128)(2,1)}, bf16[96,768]{1,0:T(8,128)(2,1)}, u32[]{:S(2)}, u32[]{:S(2)}) collective-permute-start(bf16[96,768]{1,0:T(8,128)(2,1)} %get-tuple-element.129), channel_id=1, source_target_pairs={{0,8},{4,12},{8,16},{12,20},{16,24},{20,28},{24,0},{28,4},{1,9},{5... | collective-permute-start | bytes 442376 | tf_op jit(solution)/shard_map/ppermute | solution.py:27
  413.1 11.2 %collective-permute-start.37 = (bf16[96,768]{1,0:T(8,128)(2,1)}, bf16[96,768]{1,0:T(8,128)(2,1)}, u32[]{:S(2)}, u32[]{:S(2)}) collective-permute-start(bf16[96,768]{1,0:T(8,128)(2,1)} %get-tuple-element.127), channel_id=1, source_target_pairs={{0,24},{4,28},{8,0},{12,4},{16,8},{20,12},{24,16},{28,20},{1,25},{... | collective-permute-start | bytes 442376 | tf_op jit(solution)/shard_map/ppermute | solution.py:27
  418.5 13.0 %copy-start.13 = (bf16[768,768]{1,0:T(8,128)(2,1)S(1)}, bf16[768,768]{1,0:T(8,128)(2,1)}, u32[]{:S(2)}) copy-start(bf16[768,768]{1,0:T(8,128)(2,1)} %copy-done.12) | copy-start | bytes 3538948
  418.5 13.0 %collective-permute-start.11 = (bf16[3,128,768]{2,1,0:T(8,128)(2,1)S(1)}, bf16[3,128,768]{2,1,0:T(8,128)(2,1)S(1)}, u32[]{:S(2)}, u32[]{:S(2)}) collective-permute-start(bf16[3,128,768]{2,1,0:T(8,128)(2,1)S(1)} %dynamic-slice_bitcast_fusion.2), channel_id=1, source_target_pairs={{0,2},{1,3},{2,0},{3,1},{4,6},{5,7},{6,4},{7,5},{8,10},{9,11},{10,... | collective-permute-start | bytes 1769480 | tf_op jit(solution)/shard_map/ppermute | solution.py:22
  421.9 7.8 %collective-permute-start.36 = (bf16[96,768]{1,0:T(8,128)(2,1)}, bf16[96,768]{1,0:T(8,128)(2,1)S(1)}, u32[]{:S(2)}, u32[]{:S(2)}) collective-permute-start(bf16[96,768]{1,0:T(8,128)(2,1)} %get-tuple-element.128), channel_id=1, source_target_pairs={{0,16},{4,20},{8,24},{12,28},{16,0},{20,4},{24,8},{28,12},{1,17},{... | collective-permute-start | bytes 442376 | tf_op jit(solution)/shard_map/ppermute | solution.py:27
  421.9 7.8 %collective-permute-start.35 = (bf16[96,768]{1,0:T(8,128)(2,1)}, bf16[96,768]{1,0:T(8,128)(2,1)S(1)}, u32[]{:S(2)}, u32[]{:S(2)}) collective-permute-start(bf16[96,768]{1,0:T(8,128)(2,1)} %get-tuple-element.126), channel_id=1, source_target_pairs={{0,8},{4,12},{8,16},{12,20},{16,24},{20,28},{24,0},{28,4},{1,9},{5... | collective-permute-start | bytes 442376 | tf_op jit(solution)/shard_map/ppermute | solution.py:27
  (78 other events, 252.3 us)

commit v3 on v2

--- a/solution.py
+++ b/solution.py
@@ -122,18 +122,6 @@
     return total
 
 
-def sum_all(vector):
-    n = lax.axis_size("dp")
-    if n != 8:
-        return lax.psum(vector, ("dp", "head"))
-    vector = vector + sibling(vector)
-    vector = vector + across(vector)
-    vector = vector + flip(vector, "dp", 1)
-    return (vector + shift(vector, "dp", 4)) + (
-        shift(vector, "dp", 2) + shift(vector, "dp", 6)
-    )
-
-
 def lane_masks(scale):
     lane = lax.broadcasted_iota(jnp.int32, (1, 2 * HD), 1)
     first = jnp.where(lane < HD, 1.0, 0.0)
@@ -148,47 +136,6 @@
 def pair_lanes(halves):
     lane = lax.broadcasted_iota(jnp.int32, halves[0].shape, 1)
     return jnp.where(lane < HD, halves[0], halves[1])
-
-
-def attend_kernel(q_ref, k_ref, v_ref, o_ref):
-    q, k, v = rows_of(q_ref), rows_of(k_ref), rows_of(v_ref)
-    outs = []
-    for mask in lane_masks(SCALE):
-        s = mm_t(q * mask, k)
-        raised = jnp.exp(s - jnp.max(s, axis=-1, keepdims=True))
-        total = jnp.sum(raised, axis=-1, keepdims=True)
-        outs.append(mm(raised.astype(BF16), v) / total)
-    o_ref[...] = pair_lanes(outs).astype(BF16).reshape(o_ref.shape)
-
-
-def query_back_kernel(q_ref, g_ref, k_ref, v_ref, dq_ref):
-    q, g, k, v = rows_of(q_ref), rows_of(g_ref), rows_of(k_ref), rows_of(v_ref)
-    outs = []
-    for mask, one in zip(lane_masks(SCALE), lane_masks(1.0)):
-        s = mm_t(q * mask, k)
-        raised = jnp.exp(s - jnp.max(s, axis=-1, keepdims=True))
-        probs = raised / jnp.sum(raised, axis=-1, keepdims=True)
-        d_probs = mm_t(g * one, v)
-        inner = jnp.sum(d_probs * probs, axis=-1, keepdims=True)
-        d_scores = (probs * (d_probs - inner)).astype(BF16)
-        outs.append(mm(d_scores, k) * SCALE)
-    dq_ref[...] = pair_lanes(outs).astype(BF16).reshape(dq_ref.shape)
-
-
-def key_back_kernel(q_ref, g_ref, k_ref, v_ref, dk_ref, dv_ref):
-    q, g, k, v = rows_of(q_ref), rows_of(g_ref), rows_of(k_ref), rows_of(v_ref)
-    d_keys, d_values = [], []
-    for mask, one in zip(lane_masks(SCALE), lane_masks(1.0)):
-        s = mm_t(k, q * mask)
-        raised = jnp.exp(s - jnp.max(s, axis=0, keepdims=True))
-        probs = raised / jnp.sum(raised, axis=0, keepdims=True)
-        d_probs = mm_t(v, g * one)
-        inner = jnp.sum(d_probs * probs, axis=0, keepdims=True)
-        d_scores = (probs * (d_probs - inner)).astype(BF16)
-        d_keys.append(mm(d_scores, q) * SCALE)
-        d_values.append(mm(probs.astype(BF16), g))
-    dk_ref[...] = pair_lanes(d_keys).astype(BF16).reshape(dk_ref.shape)
-    dv_ref[...] = pair_lanes(d_values).astype(BF16).reshape(dv_ref.shape)
 
 
 def halves_joined(low, high):
@@ -301,13 +248,13 @@
     if comm:
         (
             a_ref, b_ref, t_ref, small_ref, row_ref, col_ref,
-            wa_ref, wb_ref, x_ref, o_ref, k_ref, v_ref, ku_ref, vu_ref, qc_ref, picks_ref, select_ref, far_ref,
+            wa_ref, wb_ref, x_ref, xt_ref, o_ref, k_ref, v_ref, ku_ref, vu_ref, qc_ref, picks_ref, select_ref, far_ref,
             xp_ref, q_ref, local_sem, send_sem, recv_sem,
         ) = refs
     else:
         (
             wa_ref, x_ref, xp_ref, small_ref, far_ref, row_ref, col_ref,
-            o_ref, k_ref, v_ref, ku_ref, vu_ref, qc_ref, picks_ref, select_ref,
+            xt_ref, o_ref, k_ref, v_ref, ku_ref, vu_ref, qc_ref, picks_ref, select_ref,
             q_ref,
         ) = refs
     blocks = x_ref.shape[1]
@@ -318,6 +265,13 @@
         forward_listed(b, member, row_ref, col_ref, q_ref, picks_ref, select_ref, qc_ref)
         return carry
 
+    def turned(i, carry):
+        s, rest = lax.div(i, 2 * blocks), lax.rem(i, 2 * blocks)
+        part = x_ref[s, lax.div(rest, 2), lax.rem(rest, 2)]
+        quarter = part.shape[0]
+        xt_ref[:, pl.ds(pl.multiple_of(i * quarter, quarter), quarter)] = part.T
+        return carry
+
     def bias_of():
         own, other = small_ref[...], far_ref[...]
         rows = [head_tiles(own[i : i + 1], other[i : i + 1]) for i in range(3)]
@@ -325,10 +279,12 @@
 
     if not comm:
         bias, swapped = bias_of()
+        lax.fori_loop(0, 4 * blocks, turned, 0)
 
         def own_block(b, carry):
             forward_own(b, x_ref, wa_ref, bias, q_ref, k_ref, v_ref)
             return carry
+
     if comm:
         index = lax.axis_index("dp")
         z, x = lax.div(index, 2), lax.rem(index, 2)
@@ -398,6 +354,7 @@
             fill.wait()
         for b in range(blocks):
             far_copy(b).start()
+        lax.fori_loop(0, 4 * blocks, turned, 0)
         half = a_ref.shape[0] // 2
         up, low = pl.ds(0, half), pl.ds(half, half)
         fill_a.wait()
@@ -478,7 +435,7 @@
         return jax.ShapeDtypeStruct(shape, dtype)
 
     dense = (2, blocks, 2 * quarter, lanes)
-    tail = [out(*dense)] * 5 + [
+    tail = [out(width, 2 * blocks * 2 * quarter)] + [out(*dense)] * 5 + [
         out(2, blocks, 2 * cap, lanes),
         out(blocks, slots, slots),
         out(blocks, slots, quarter),
@@ -529,28 +486,448 @@
     return (w_attn, w_feed, rows, *rest, far)
 
 
-def per_head_pair(kernel, arrays, out_count, out_like, flops):
-    _, blocks, _, width = arrays[0].shape
-
-    def spec(array):
-        return pl.BlockSpec(
-            (2, None, array.shape[2], 2 * HD), lambda b, t: (0, b, 0, t)
+def back_queries(b, qc_ref, g_ref, ku_ref, vu_ref, select_ref, o_ref, dt_ref, oc_ref, total_ref):
+    rows = ku_ref.shape[2] * 2
+    slots = qc_ref.shape[2] * 2
+    cap = slots // 4
+    quarter = rows // 4
+    select = select_ref[b]
+    tiles = []
+    for t in range(3):
+        lanes = slice(128 * t, 128 * (t + 1))
+        q = qc_ref[:, b, :, lanes].reshape(slots, 128)
+        g = g_ref[:, b, :, lanes].reshape(slots, 128)
+        k = ku_ref[:, b, :, lanes].reshape(rows, 128)
+        v = vu_ref[:, b, :, lanes].reshape(rows, 128)
+        outs = []
+        for mask, one in zip(lane_masks(SCALE), lane_masks(1.0)):
+            s = mm_t(q * mask, k)
+            raised = jnp.exp(s - jnp.max(s, axis=-1, keepdims=True))
+            probs = raised / jnp.sum(raised, axis=-1, keepdims=True)
+            d_probs = mm_t(g * one, v)
+            inner = jnp.sum(d_probs * probs, axis=-1, keepdims=True)
+            d_scores = (probs * (d_probs - inner)).astype(BF16)
+            outs.append(mm(d_scores, k) * SCALE)
+        tile = pair_lanes(outs).astype(BF16)
+        total_ref[0:1, lanes] += jnp.sum(tile.astype(F32), axis=0, keepdims=True)
+        tiles.append(tile)
+    for s in range(2):
+        for e in range(2):
+            at = (2 * s + e) * cap
+            chosen = select[at : at + cap]
+            own = slice(quarter * e, quarter * (e + 1))
+            dense = [t_mm(chosen, tile[at : at + cap]) for tile in tiles]
+            dt_ref[0, s, b, own, 0:128] = dense[0].astype(BF16)
+            dt_ref[1, s, b, own, 0:128] = dense[1].astype(BF16)
+            lane = lax.broadcasted_iota(jnp.int32, dense[2].shape, 1)
+            for p in range(2):
+                last = dense[2] if p == 0 else pltpu.roll(dense[2], HD, 1)
+                dt_ref[p, s, b, own, 384:512] = jnp.where(lane < HD, last, 0.0).astype(BF16)
+            rows_o = mm(chosen, o_ref[s, b, own, :])
+            at_o = slice(cap * e, cap * (e + 1))
+            lane = lax.broadcasted_iota(jnp.int32, (cap, 128), 1)
+            for p in range(2):
+                oc_ref[p, s, b, at_o, 128:256] = rows_o[:, 128 * p : 128 * (p + 1)].astype(BF16)
+                last = rows_o[:, 256:384] if p == 1 else pltpu.roll(rows_o[:, 256:384], HD, 1)
+                oc_ref[p, s, b, at_o, 0:128] = jnp.where(lane < HD, 0.0, last).astype(BF16)
+
+
+def back_keys(b, swapped, qc_ref, g_ref, qf_ref, gf_ref, k_ref, v_ref, dt_ref, total_ref):
+    rows = k_ref.shape[2] * 2
+    slots = qc_ref.shape[2] * 2
+    for t in range(3):
+        lanes = slice(128 * t, 128 * (t + 1))
+        take_far = swapped[t] > 0.5
+
+        def chosen(near, far):
+            near = near[:, b, :, lanes].reshape(slots, 128).astype(F32)
+            far = far[:, b, :, lanes].reshape(slots, 128).astype(F32)
+            return jnp.where(take_far, far, near).astype(BF16)
+
+        q, g = chosen(qc_ref, qf_ref), chosen(g_ref, gf_ref)
+        k = k_ref[:, b, :, lanes].reshape(rows, 128)
+        v = v_ref[:, b, :, lanes].reshape(rows, 128)
+        d_keys, d_values = [], []
+        for mask, one in zip(lane_masks(SCALE), lane_masks(1.0)):
+            s = mm_t(k, q * mask)
+            raised = jnp.exp(s - jnp.max(s, axis=0, keepdims=True))
+            probs = raised / jnp.sum(raised, axis=0, keepdims=True)
+            d_probs = mm_t(v, g * one)
+            inner = jnp.sum(d_probs * probs, axis=0, keepdims=True)
+            d_scores = (probs * (d_probs - inner)).astype(BF16)
+            d_keys.append(mm(d_scores, q) * SCALE)
+            d_values.append(mm(probs.astype(BF16), g))
+        dk, dv = pair_lanes(d_keys), pair_lanes(d_values)
+        total_ref[1:2, lanes] += jnp.sum(dv.astype(BF16).astype(F32), axis=0, keepdims=True)
+        half = (2, rows // 2, 128)
+        if t < 2:
+            dt_ref[t, :, b, :, 128:256] = dk.astype(BF16).reshape(half)
+            dt_ref[t, :, b, :, 256:384] = dv.astype(BF16).reshape(half)
+        else:
+            lane = lax.broadcasted_iota(jnp.int32, dk.shape, 1)
+            for p in range(2):
+                last = pltpu.roll(dk, HD, 1) if p == 0 else dk
+                before = dt_ref[p, :, b, :, 384:512].reshape(rows, 128).astype(F32)
+                dt_ref[p, :, b, :, 384:512] = (
+                    jnp.where(lane < HD, before, last).astype(BF16).reshape(half)
+                )
+                last = dv if p == 0 else pltpu.roll(dv, HD, 1)
+                dt_ref[p, :, b, :, 512:640] = (
+                    jnp.where(lane < HD, last, 0.0).astype(BF16).reshape(half)
+                )
+
+
+def back_weights(p, xt_ref, dt_ref, db_ref, oc_ref, ga_ref):
+    width = xt_ref.shape[0]
+    shape = ga_ref.shape[1:-1] + (128,)
+    listed = db_ref.shape[0] * db_ref.shape[1] * db_ref.shape[2]
+    d_branch = db_ref[...].reshape(listed, width)
+    outs = mm(xt_ref[...], dt_ref[p].reshape(xt_ref.shape[1], 640))
+    extra = t_mm(d_branch, oc_ref[p].reshape(listed, 256))
+    for i in range(6):
+        if i < 4:
+            tile = outs[:, 128 * i : 128 * (i + 1)]
+        elif i == 4:
+            tile = outs[:, 512:640] + extra[:, 0:128]
+        else:
+            tile = extra[:, 128:256]
+        ga_ref[p, ..., 128 * i : 128 * (i + 1)] = tile.astype(BF16).reshape(shape)
+
+
+def back_rows(s, b, wa_ref, dt_ref):
+    rows, width = dt_ref.shape[3], wa_ref.shape[-1]
+    out = 0.0
+    for p in range(2):
+        w = wa_ref[p].reshape(-1, wa_ref.shape[-1])
+        out = out + mm_t(dt_ref[p, s, b], w[:, 0:640])
+    return out
+
+
+def bias_totals(member, pair, total_ref):
+    lane = lax.broadcasted_iota(jnp.int32, (1, 128), 1)
+    line = lax.broadcasted_iota(jnp.int32, (8, 128), 0)
+    first = jnp.zeros((8, 128), F32)
+    second = jnp.zeros((8, 128), F32)
+    for i in range(2):
+        last = total_ref[i : i + 1, 256:384]
+        for p in range(2):
+            place = 4 * i + 2 * (pair if p == 0 else 1 - pair) + member
+            tile = total_ref[i : i + 1, 128 * p : 128 * (p + 1)]
+            third = last if p == 0 else pltpu.roll(last, HD, 1)
+            first = first + jnp.where(line == place, tile, 0.0)
+            second = second + jnp.where(line == place, jnp.where(lane < HD, third, 0.0), 0.0)
+    return first, second
+
+
+def back_kernel(comm, *refs):
+    if comm:
+        (
+            gb_ref, qc_ref, g_ref, k_ref, v_ref, ku_ref, vu_ref, o_ref, xt_ref, wa_ref,
+            select_ref, small_ref, far_ref, db_ref, df_ref, vec_ref,
+            gx_ref, sa_ref, sb_ref, sum_ref,
+            dt_ref, oc_ref, ga_ref, total_ref, qf_ref, gf_ref, term_ref, near_ref, rows_ref,
+            b1_up, b1_low, b2, b3, a1_up, a1_low, a2, a3, vec1, vec4,
+            local_sem, send_sem, recv_sem,
+        ) = refs
+    else:
+        (
+            qf_ref, gf_ref, qc_ref, g_ref, k_ref, v_ref, ku_ref, vu_ref, o_ref, xt_ref, wa_ref,
+            select_ref, small_ref, far_ref, db_ref,
+            ga_ref, term_ref, both_ref,
+            dt_ref, oc_ref, total_ref,
+        ) = refs
+    blocks = k_ref.shape[1]
+    head = lax.axis_index("head")
+    member, pair = lax.rem(head, 2), lax.div(head, 2)
+    swapped = head_tiles(small_ref[2:3], far_ref[2:3])
+    total_ref[...] = jnp.zeros_like(total_ref)
+
+    def queries(b, carry):
+        back_queries(b, qc_ref, g_ref, ku_ref, vu_ref, select_ref, o_ref, dt_ref, oc_ref, total_ref)
+        return carry
+
+    def keys(b, carry):
+        back_keys(b, swapped, qc_ref, g_ref, qf_ref, gf_ref, k_ref, v_ref, dt_ref, total_ref)
+        return carry
+
+    def weights(p, carry):
+        back_weights(p, xt_ref, dt_ref, db_ref, oc_ref, ga_ref)
+        return carry
+
+    if not comm:
+        lax.fori_loop(0, blocks, queries, 0)
+        lax.fori_loop(0, blocks, keys, 0)
+        lax.fori_loop(0, 2, weights, 0)
+
+        def rows(i, carry):
+            s, b = lax.div(i, blocks), lax.rem(i, blocks)
+            term_ref[s, b] = back_rows(s, b, wa_ref, dt_ref)
+            return carry
+
+        lax.fori_loop(0, 2 * blocks, rows, 0)
+        both_ref[0:8], both_ref[8:16] = bias_totals(member, pair, total_ref)
+        return
+
+    index = lax.axis_index("dp")
+    z, x = lax.div(index, 2), lax.rem(index, 2)
+    x_peer = {"dp": 2 * z + 1 - x}
+    y_peer = {"head": lax.rem(head + 2, 4)}
+    sibling_peer = {"head": 2 * pair + 1 - member}
+    z_peers = [{"dp": lax.rem(index + 2 * k, 8)} for k in (1, 2, 3)]
+    z_to = [lax.rem(z + k, 4) for k in (1, 2, 3)]
+    barrier = pltpu.get_barrier_semaphore()
+    for peer in [x_peer, y_peer, sibling_peer] + z_peers:
+        pl.semaphore_signal(barrier, inc=1, device_id=peer, device_id_type=MESH)
+    pl.semaphore_wait(barrier, 6)
+    sent = []
+
+    def send(src, dst, peer):
+        i = len(sent)
+        copy = pltpu.make_async_remote_copy(
+            src_ref=src,
+            dst_ref=dst,
+            send_sem=send_sem.at[i],
+            recv_sem=recv_sem.at[i],
+            device_id=peer,
+            device_id_type=MESH,
         )
-
-    shape = jax.ShapeDtypeStruct(out_like.shape, BF16)
-    out = pl.pallas_call(
-        kernel,
-        grid=(blocks, width // (2 * HD)),
-        in_specs=[spec(a) for a in arrays],
-        out_specs=[spec(out_like)] * out_count,
-        out_shape=[shape] * out_count,
-        cost_estimate=pl.CostEstimate(
-            flops=flops,
-            transcendentals=0,
-            bytes_accessed=2 * (sum(a.size for a in arrays) + out_count * out_like.size),
-        ),
-    )(*arrays)
-    return out
+        copy.start()
+        sent.append(copy)
+        return copy
+
+    def plus(a, b):
+        return (a.astype(F32) + b.astype(F32)).astype(BF16)
+
+    def first_phase(up_other, low_other, up_buffer, low_buffer):
+        return send(up_other, up_buffer, y_peer), send(low_other, low_buffer, x_peer)
+
+    far_g = send(g_ref, gf_ref, z_peers[1])
+    far_q = send(qc_ref, qf_ref, z_peers[1])
+    b_up = send(gb_ref.at[1, 0], b1_up, y_peer)
+    b_low = send(gb_ref.at[:, 1, :, 1 - x], b1_low, x_peer)
+    lax.fori_loop(0, blocks, queries, 0)
+    far_g.wait_recv()
+    far_q.wait_recv()
+    lax.fori_loop(0, blocks, keys, 0)
+
+    vec_rows = vec_ref.shape[0]
+    vec1[0, 0:vec_rows] = vec_ref[...]
+    vec1[0, vec_rows : vec_rows + 8], vec1[0, vec_rows + 8 : vec_rows + 16] = bias_totals(
+        member, pair, total_ref
+    )
+    v_sib = send(vec1.at[0], vec1.at[1], sibling_peer)
+
+    halves = gb_ref.shape[2]
+
+    def add_up(i, carry):
+        b1_up[i] = plus(b1_up[i], gb_ref[0, 0, i])
+        return carry
+
+    def add_low(i, carry):
+        for p in range(2):
+            b1_low[p, i] = plus(b1_low[p, i], gb_ref[p, 1, i, x])
+        return carry
+
+    b_up.wait_recv()
+    lax.fori_loop(0, halves, add_up, 0)
+    b_up = send(b1_up.at[:, 1 - x], b2.at[0], x_peer)
+    b_low.wait_recv()
+    lax.fori_loop(0, halves, add_low, 0)
+    b_low = send(b1_low.at[1], b2.at[1], y_peer)
+    v_sib.wait_recv()
+    vec1[2] = vec1[0] + vec1[1]
+    v_y = send(vec1.at[2], vec1.at[3], y_peer)
+
+    lax.fori_loop(0, 2, weights, 0)
+    half = ga_ref.shape[3] // 2
+    up, low = slice(0, half), slice(half, 2 * half)
+    a_up = send(ga_ref.at[1, :, :, pl.ds(0, half)], a1_up, y_peer)
+    a_low = send(ga_ref.at[:, :, 1 - x, pl.ds(half, half)], a1_low, x_peer)
+
+    def rows_other(b, carry):
+        term_ref[b] = back_rows(1, b, wa_ref, dt_ref).astype(BF16)
+        return carry
+
+    lax.fori_loop(0, blocks, rows_other, 0)
+    term = send(term_ref, near_ref, sibling_peer)
+
+    b_up.wait_recv()
+    b_low.wait_recv()
+
+    def add_second(i, carry):
+        b2[0, i] = plus(b2[0, i], b1_up[i, x])
+        b2[1, i] = plus(b2[1, i], b1_low[0, i])
+        return carry
+
+    lax.fori_loop(0, halves, add_second, 0)
+    b_z = [send(b2.at[:, to], b3.at[k], peer) for k, (to, peer) in enumerate(zip(z_to, z_peers))]
+    v_y.wait_recv()
+    vec1[4] = vec1[2] + vec1[3]
+    v_x = send(vec1.at[4], vec1.at[5], x_peer)
+
+    a_up.wait_recv()
+
+    def a_add_up(i, carry):
+        a1_up[i] = plus(a1_up[i], ga_ref[0, i, :, up])
+        return carry
+
+    lax.fori_loop(0, halves, a_add_up, 0)
+    a_up = send(a1_up.at[:, 1 - x], a2.at[0], x_peer)
+    a_low.wait_recv()
+
+    def a_add_low(i, carry):
+        for p in range(2):
+            a1_low[p, i] = plus(a1_low[p, i], ga_ref[p, i, x, low])
+        return carry
+
+    lax.fori_loop(0, halves, a_add_low, 0)
+    a_low = send(a1_low.at[1], a2.at[1], y_peer)
+
+    cap = df_ref.shape[1] // 2
+    quarter = rows_ref.shape[2]
+    term.wait_recv()
+
+    def rows_own(b, carry):
+        own = back_rows(0, b, wa_ref, dt_ref) + near_ref[b].astype(F32)
+        for e in range(2):
+            first = df_ref[b, cap * e : cap * (e + 1), :]
+            high = first.astype(BF16)
+            rest = (first - high.astype(F32)).astype(BF16)
+            chosen = select_ref[b, cap * e : cap * (e + 1), :]
+            spread = t_mm(chosen, high) + t_mm(chosen, rest)
+            rows_ref[e, b] = (own[quarter * e : quarter * (e + 1)] + spread).astype(BF16)
+        return carry
+
+    lax.fori_loop(0, blocks, rows_own, 0)
+    moved = send(rows_ref.at[1 - pair], gx_ref.at[pair], y_peer)
+    kept = pltpu.make_async_copy(rows_ref.at[pair], gx_ref.at[pair], local_sem.at[0])
+    kept.start()
+    v_x.wait_recv()
+    vec1[6] = vec1[4] + vec1[5]
+    own_vec = pltpu.make_async_copy(vec1.at[6], vec4.at[z], local_sem.at[1])
+    own_vec.start()
+    v_z = [send(vec1.at[6], vec4.at[z], peer) for peer in z_peers]
+
+    a_up.wait_recv()
+    a_low.wait_recv()
+
+    def a_add_second(i, carry):
+        a2[0, i] = plus(a2[0, i], a1_up[i, x])
+        a2[1, i] = plus(a2[1, i], a1_low[0, i])
+        return carry
+
+    lax.fori_loop(0, halves, a_add_second, 0)
+    a_z = [send(a2.at[:, to], a3.at[k], peer) for k, (to, peer) in enumerate(zip(z_to, z_peers))]
+
+    for copy in b_z:
+        copy.wait_recv()
+    for t in range(2):
+        total = b2[t, z].astype(F32)
+        for k in range(3):
+            total = total + b3[k, t].astype(F32)
+        sb_ref[t] = total
+    own_vec.wait()
+    for copy in v_z:
+        copy.wait_recv()
+    sum_ref[...] = (vec4[0] + vec4[1]) + (vec4[2] + vec4[3])
+    for copy in a_z:
+        copy.wait_recv()
+    for t, part in enumerate((up, low)):
+        total = a2[t, z].astype(F32)
+        for k in range(3):
+            total = total + a3[k, t].astype(F32)
+        sa_ref[part] = total
+    kept.wait()
+    moved.wait_recv()
+    for copy in sent:
+        copy.wait_send()
+
+
+def backward(gb, q_compact, d_attention, keys, values, keys_used, values_used, attention, rows_t, w_attn, select, small, far, d_branch, d_first, vectors):
+    n = lax.axis_size("dp")
+    _, blocks, block_half, lanes = keys.shape
+    width = rows_t.shape[0]
+    quarter = block_half // 2
+    piece = width // n
+    slots = select.shape[1]
+    vec_rows = vectors.shape[0] + 16
+
+    def out(*shape, dtype=BF16):
+        return jax.ShapeDtypeStruct(shape, dtype)
+
+    compact = (2, blocks, slots // 2, lanes)
+    scratch = [
+        pltpu.VMEM((2, 2, blocks, block_half, 640), BF16),
+        pltpu.VMEM((2, 2, blocks, slots // 2, 256), BF16),
+    ]
+    shared = (q_compact, d_attention, keys, values, keys_used, values_used, attention, rows_t, w_attn, select, small, far, d_branch)
+    if n == 8:
+        half = piece // 2
+        return pl.pallas_call(
+            functools.partial(back_kernel, True),
+            out_shape=[
+                out(2, blocks, quarter, width),
+                out(piece, width, dtype=F32),
+                out(2, piece, width, dtype=F32),
+                out(vec_rows, 128, dtype=F32),
+            ],
+            in_specs=[vmem_spec()] * 16,
+            out_specs=[vmem_spec()] * 4,
+            scratch_shapes=scratch
+            + [
+                pltpu.VMEM((2, 4, 2, piece, width), BF16),
+                pltpu.VMEM((8, lanes), F32),
+                pltpu.VMEM(compact, BF16),
+                pltpu.VMEM(compact, BF16),
+                pltpu.VMEM((blocks, block_half, width), BF16),
+                pltpu.VMEM((blocks, block_half, width), BF16),
+                pltpu.VMEM((2, blocks, quarter, width), BF16),
+                pltpu.VMEM((4, 2, piece, width), BF16),
+                pltpu.VMEM((2, 4, piece, width), BF16),
+                pltpu.VMEM((2, 4, piece, width), BF16),
+                pltpu.VMEM((3, 2, piece, width), BF16),
+                pltpu.VMEM((4, 2, half, width), BF16),
+                pltpu.VMEM((2, 4, half, width), BF16),
+                pltpu.VMEM((2, 4, half, width), BF16),
+                pltpu.VMEM((3, 2, half, width), BF16),
+                pltpu.VMEM((7, vec_rows, 128), F32),
+                pltpu.VMEM((4, vec_rows, 128), F32),
+                pltpu.SemaphoreType.DMA((2,)),
+                pltpu.SemaphoreType.DMA((24,)),
+                pltpu.SemaphoreType.DMA((24,)),
+            ],
+            compiler_params=pltpu.CompilerParams(
+                collective_id=2, vmem_limit_bytes=62 * 2**20, has_side_effects=True
+            ),
+        )(gb.reshape(2, 2, 4, 2, piece, width), *shared, d_first, vectors)
+    ga, term, both = pl.pallas_call(
+        functools.partial(back_kernel, False),
+        out_shape=[
+            out(2, 1, 1, width, width),
+            out(2, blocks, block_half, width, dtype=F32),
+            out(16, 128, dtype=F32),
+        ],
+        in_specs=[vmem_spec()] * 15,
+        out_specs=[vmem_spec()] * 3,
+        scratch_shapes=scratch + [pltpu.VMEM((8, lanes), F32)],
+        compiler_params=pltpu.CompilerParams(vmem_limit_bytes=62 * 2**20),
+    )(partner(q_compact), partner(d_attention), *shared)
+    pair = lax.axis_index("head") // 2
+    cap = slots // 4
+    chosen = select[:, : 2 * cap].reshape(blocks, 2, cap, quarter).astype(F32)
+    spread = jnp.einsum(
+        "bekr,bekw->berw",
+        chosen,
+        d_first.reshape(blocks, 2, cap, width),
+        precision=lax.Precision.HIGHEST,
+    )
+    own = term[0].reshape(spread.shape) + sibling(term[1].astype(BF16)).astype(F32).reshape(spread.shape)
+    own = (own + spread).astype(BF16)
+    grad_x = ordered(pair, pick(own, pair, 1), across(pick(own, 1 - pair, 1)))
+    pieces = (2, n, piece, width)
+    s_attn = reduce_scatter(ga.reshape(pieces), True)
+    s_feed = jnp.stack([reduce_scatter(gb[:, i].reshape(pieces), True) for i in range(2)])
+    return grad_x, s_attn, s_feed, lax.psum(jnp.concatenate((vectors, both)), ("dp", "head"))
 
 
 def per_device(
@@ -620,28 +997,26 @@
     )
     listed = pick(masked_rows.reshape(2, blocks, slots), p)
     (
-        w_attn, w_feed, x_rows, attention, keys, values, keys_used, values_used, q_compact, picks_b, select_b, small_far,
+        w_attn, w_feed, x_rows, rows_t, attention, keys, values, keys_used, values_used, q_compact, picks_b, select_b, small_far,
     ) = forward(tokens, piece, jnp.stack((up_weight, down_weight.T)), small, listed, c, p)
 
     def tiles(i, second, j):
+        second = HD * second
+
         return jnp.concatenate(
             (
                 w_attn[0][:, 128 * i : 128 * i + 128],
                 w_attn[1][:, 128 * i : 128 * i + 128],
-                w_attn[0][:, 128 * j + 64 * second : 128 * j + 64 * second + 64],
-                w_attn[1][:, 128 * j + 64 * second : 128 * j + 64 * second + 64],
+                w_attn[0][:, 128 * j + second : 128 * j + second + HD],
+                w_attn[1][:, 128 * j + second : 128 * j + second + HD],
             ),
             axis=1,
         )
 
-    w_query, w_key, w_value, w_out_t = tiles(0, 0, 3), tiles(1, 1, 3), tiles(2, 0, 4), tiles(5, 1, 4)
+    w_out_t = tiles(5, 1, 4)
     w_out_other = sibling(w_out_t)
     w_up, w_down = w_feed[:, 0], w_feed[:, 1]
     b_up = jnp.stack((up_bias, small_far[3]))
-    order, order_far = small[2, :local], small_far[2, :local]
-    swapped = (
-        jnp.concatenate((order[:128], order_far[:128], order[128:], order_far[128:])) > 0.5
-    )
     x_flat = x_rows.reshape(-1, width)
     own_count = x_flat.shape[0] // 2
     attn_shape = (2, blocks, 2 * quarter, columns)
@@ -681,8 +1056,6 @@
         "beki,biw->bekw", picks[0], grads_in, preferred_element_type=F32
     ).reshape(-1, width)
 
-    q_far = partner(q_compact)
-    swapped_lanes = swapped[None, None, None, :]
     attn_other = sibling(attention[1]).reshape(own_count, columns)
     branch = mm_t(attention[0].reshape(own_count, columns), w_out_t) + mm_t(
         attn_other, w_out_other
@@ -746,9 +1119,7 @@
         + d_hidden_term[:compact_own]
         + sibling(d_hidden_term[compact_own:].astype(BF16)).astype(F32)
     )
-    pieces = (2, width // piece_rows, piece_rows, hidden_piece)
-    s_up = reduce_scatter(jnp.stack(g_up).reshape(pieces), True)
-    s_down = reduce_scatter(jnp.stack(g_down).reshape(pieces), False).T
+    gb = jnp.stack((jnp.stack(g_up), jnp.stack(g_down)), axis=1)
     g_first_gain = jnp.sum(d_hidden * normed_one, axis=0)
     g_first_shift = jnp.sum(d_hidden, axis=0)
     d_first = norm_back(d_hidden, normed_one, inverse_one, first_gain)
@@ -756,128 +1127,63 @@
     g_out_bias = jnp.sum(d_branch.astype(F32), axis=0)
     d_branch_all = jnp.concatenate((d_branch, sibling(d_branch)))
     d_attention = mm(d_branch_all, w_out_t).astype(BF16).reshape(compact_shape)
-    d_attention_far = partner(d_attention)
-
-    (d_queries_c,) = per_head_pair(
-        query_back_kernel,
-        [
-            q_compact,
-            d_attention,
-            keys_used.reshape(attn_shape),
-            values_used.reshape(attn_shape),
-        ],
-        1,
-        q_compact,
-        6 * slots * block_rows * columns * blocks,
-    )
-    d_keys, d_values = per_head_pair(
-        key_back_kernel,
-        [
-            jnp.where(swapped_lanes, q_far, q_compact),
-            jnp.where(swapped_lanes, d_attention_far, d_attention),
-            keys.reshape(attn_shape),
-            values.reshape(attn_shape),
-        ],
-        2,
-        keys.reshape(attn_shape),
-        8 * slots * block_rows * columns * blocks,
-    )
-    d_queries_c = d_queries_c.reshape(-1, columns)
-    d_queries = spread(d_queries_c).astype(BF16)
-    d_keys = d_keys.reshape(-1, columns)
-    d_values = d_values.reshape(-1, columns)
-    term = mm_t(d_queries, w_query) + mm_t(d_keys, w_key) + mm_t(d_values, w_value)
-    grad_rows = (
-        term[:own_count]
-        + sibling(term[own_count:].astype(BF16)).astype(F32)
-        + spread(d_first, own_runs, **exact)
-    ).astype(BF16)
-    grad_x = to_output(grad_rows)
-
-    g_query_bias = jnp.sum(d_queries_c.astype(F32), axis=0)
-    g_value_bias = jnp.sum(d_values.astype(F32), axis=0)
-    g_attn = jnp.stack(
-        (
-            t_mm(x_flat, d_queries).astype(BF16),
-            t_mm(x_flat, d_keys).astype(BF16),
-            t_mm(x_flat, d_values).astype(BF16),
-            t_mm(d_branch_all, compact(attention.reshape(-1, columns)).astype(BF16)).astype(BF16),
-        ),
-        axis=1,
-    )
-    g_attn = jnp.stack(
-        (
-            jnp.concatenate((g_attn[..., 0:128], g_attn[..., 256:320]), axis=-1),
-            jnp.concatenate((g_attn[..., 128:256], g_attn[..., 320:384]), axis=-1),
-        )
-    ).reshape(
-        2, width // piece_rows, 2, half, 4 * local
-    )
-    s_attn = jnp.concatenate(
-        (
-            reduce_scatter(g_attn[:, :, 0], True),
-            reduce_scatter(g_attn[:, :, 1], False),
-        )
-    )
-
-    def widen(own_first, size):
-        if own_first.shape[0] != 2:
-            own_first = jnp.stack(
-                (
-                    jnp.concatenate((own_first[0:128], own_first[256:320])),
-                    jnp.concatenate((own_first[128:256], own_first[320:384])),
-                )
-            )
+
+    def widen(own_first):
         by_p = ordered(p, own_first[0], own_first[1])
         zero = jnp.zeros_like(by_p)
         return jnp.where(
             c == 0,
             jnp.stack((by_p, zero), axis=1),
             jnp.stack((zero, by_p), axis=1),
-        ).reshape(size)
+        ).reshape(-1)
 
     vectors = [
-        widen(g_query_bias, HEADS * HD),
-        widen(g_value_bias, HEADS * HD),
         g_out_bias,
         g_first_gain,
         g_first_shift,
-        widen(jnp.stack(g_up_bias), 4 * hidden_piece),
         g_down_bias,
         g_second_gain,
         g_second_shift,
+        widen(jnp.stack(g_up_bias)),
     ]
-    summed = sum_all(jnp.concatenate(vectors))
+    flat = jnp.concatenate(vectors)
+    flat = jnp.pad(flat, (0, -flat.shape[0] % 1024)).reshape(-1, 128)
+    grad_x, s_attn, s_feed, summed = backward(
+        gb, q_compact, d_attention, keys, values, keys_used, values_used, attention, rows_t, w_attn, select_b,
+        small, small_far, d_branch_all.reshape(2, blocks, 2 * cap, width), d_first.reshape(blocks, 2 * cap, width), flat,
+    )
+    grad_x = grad_x.reshape(block_count, quarter, width)
+    whole = summed[: flat.shape[0]].reshape(-1)
     ends, start = [], 0
     for vector in vectors:
-        ends.append(summed[start : start + vector.shape[0]])
+        ends.append(whole[start : start + vector.shape[0]])
         start += vector.shape[0]
-    (
+    v_out_bias, v_first_gain, v_first_shift, v_down_bias, v_second_gain, v_second_shift, v_up_bias = ends
+    last = summed[flat.shape[0] :].reshape(2, 2, 4, 128)
+    v_query_bias, v_value_bias = (
+        jnp.concatenate((last[0, i], last[1, i, :, :HD]), axis=-1).reshape(-1)
+        for i in range(2)
+    )
+
+    def columns_of(i, j, second):
+        at = 128 * j + HD * second
+        return jnp.concatenate((s_attn[:, 128 * i : 128 * (i + 1)], s_attn[:, at : at + HD]), axis=1)
+
+    return (
+        out_y,
+        grad_x,
+        columns_of(0, 3, 0),
         v_query_bias,
+        columns_of(1, 3, 1),
+        columns_of(2, 4, 0),
         v_value_bias,
+        columns_of(5, 4, 1).T,
         v_out_bias,
         v_first_gain,
         v_first_shift,
+        s_feed[0],
         v_up_bias,
-        v_down_bias,
-        v_second_gain,
-        v_second_shift,
-    ) = ends
-    return (
-        out_y,
-        grad_x,
-        s_attn[:, :local],
-        v_query_bias,
-        s_attn[:, local : 2 * local],
-        s_attn[:, 2 * local : 3 * local],
-        v_value_bias,
-        s_attn[:, 3 * local :].T,
-        v_out_bias,
-        v_first_gain,
-        v_first_shift,
-        s_up,
-        v_up_bias,
-        s_down,
+        s_feed[1].T,
         v_down_bias,
         v_second_gain,
         v_second_shift,

time: 440 us -> 354 us (0.80)
  Pallas kernels: 133 us -> 210 us
  starting transfers between devices: 43.4 us -> 1.5 us
  waiting for transfers between devices: 37.4 us -> 0.9 us
  local copies, waits for them, and re-layouts: 79.6 us -> 44.7 us
  matrix products: 89.6 us -> 62.6 us
  other arithmetic: 47.3 us -> 26.7 us
    pallas_call x2 -> x1, Pallas kernels: 23.2 us -> 99.3 us  [backward(): pl.pallas_call(functools.partial(back_kernel, True), out_shape=[out(2, bl...]
    ppermute x17 -> x0, starting transfers between devices: 29.7 us -> none  [shift(): lax.ppermute(block, axis, [(i, (i + distance) % n) for i in range(n)])]
    ppermute x21 -> x8, waiting for transfers between devices: 20.2 us -> 0.9 us  [flip(): return lax.ppermute(block, axis, [(i, i ^ bit) for i in range(n)])]
    ppermute x17 -> x0, waiting for transfers between devices: 17.2 us -> none  [shift(): lax.ppermute(block, axis, [(i, (i + distance) % n) for i in range(n)])]
    ppermute x21 -> x8, starting transfers between devices: 13.7 us -> 1.5 us  [flip(): return lax.ppermute(block, axis, [(i, i ^ bit) for i in range(n)])]
    dot_general x9 -> x6, matrix products: 53 us -> 41 us  [mm_t(): lax.dot_general(a, b, (((1,), (1,)), ((), ())), preferred_element_type=F32)]
    unnamed x184 -> x113, local copies, waits for them, and re-layouts: 19.2 us -> 7.75 us
    dot_general x8 -> x4, matrix products: 13.7 us -> 3.35 us  [t_mm(): lax.dot_general(a, b, (((0,), (0,)), ((), ())), preferred_element_type=F32)]
  transfers between devices with their start and end apart: 38 -> 8, of which waited for: 12 -> 2; matrix products, arithmetic and copies ran while one was open for 45% -> 12% of each run, Pallas kernels for 5% -> 0%
where the time goes in v3:
time: 354 us; the launch traced here: 348 us
  Pallas kernels  210 us (59%)
  matrix products  62.6 us (18%)
  local copies, waits for them, and re-layouts  44.7 us (13%)
  other arithmetic  26.7 us (8%)
    pallas_call x1, Pallas kernels, forward(): pl.pallas_call(functools.partial(forward_kernel, True), out_shape=shapes,...  111 us
    pallas_call x1, Pallas kernels, backward(): pl.pallas_call(functools.partial(back_kernel, True), out_shape=[out(2, bl...  99.3 us
    dot_general x6, matrix products, mm_t(): lax.dot_general(a, b, (((1,), (1,)), ((), ())), preferred_element_type=F32)  41 us
    dot_general x5, matrix products, mm(): return jnp.dot(a, b, preferred_element_type=F32)  11.1 us
    unnamed x113, local copies, waits for them, and re-layouts  7.75 us
  transfers between devices with their start and end apart: 8, of which 2 were waited for; matrix products, arithmetic and copies ran while one was open for 12% of the time, Pallas kernels for 0%

profile of v3, /device:TPU:0, one launch (start us, length us, event | category | flops | bytes accessed | tf_op | source)
XLA Modules:
  0.0 348.4 jit_solution(9538884959407280011)
XLA Ops:
  2.8 0.9 copy.39
  11.1 1.7 pad_maximum_fusion.10.refs_1_
  14.2 111.0 %shard_map.314 = (bf16[2,4,2,96,768]{4,3,2,1,0:T(8,128)(2,1)}, bf16[2,2,4,2,96,768]{5,4,3,2,1,0:T(8,128)(2,1)}, bf16[2,3,2,128,768]{4,3,2,1,0:T(8,128)(2,1)}, bf...) custom-call(bf16[96,768]{1,0:T(8,128)(2,1)} %concatenate.42.refs_0_,, ...), custom_call_target="tpu_custom_call" | custom-call | tf_op jit(solution)/shard_map/pallas_call | solution.py:454
  125.2 1.8 fusion.120
  128.5 0.8 copy-done.15
  130.5 1.0 fusion.124
  132.2 1.4 fusion.23
  133.8 1.5 copy.45
  135.3 1.3 slice_reduce_fusion
  136.7 1.4 fusion.123
  138.1 1.0 fusion.125
  140.7 18.2 %fusion.24 = f32[1536,768]{1,0:T(8,128)} fusion(f32[768]{0:T(1024)} %param.30, bf16[768,768]{1,0:T(8,128)(2,1)} %collective-permute-done.2, bf16[768,768]{1,0:T(8,128)(2,1)} %fusion.23, bf16[2,2,768,768]{3,2,1,0:T(8,128)(2,1)} %bitcast.185), kind=kOutput, calls=%fused_computation.54 | convolution fusion | flops 3706454016 | bytes 9441280 | tf_op jit(solution)/shard_map/dot_general | solution.py:57
  158.9 18.2 %convolution_add_fusion = f32[1536,768]{1,0:T(8,128)} fusion(f32[1536,768]{1,0:T(8,128)} %fusion.24, f32[768]{0:T(1024)} %slice_reduce_fusion, bf16[768,768]{1,0:T(8,128)(2,1)} %collective-permute-done.2, bf16[768,768]{1,0:T(8,128)(2,1)} %fusion.23, bf16[2,2,768,768]{3,2,1,0:T(8,128)(2,1)} %bitcast.186), kind=kOutput, calls=%fused_computation.39 | convolution fusion | flops 3707633664 | bytes 14159872 | tf_op jit(solution)/shard_map/dot_general | solution.py:57
  177.1 2.8 slice.336
  180.9 1.3 div.62
  182.2 1.3 rsqrt.45
  183.5 2.1 add_convert_fusion.1
  185.6 1.7 convolution_convert_fusion.5
  187.4 3.1 convolution_add_fusion.3
  190.5 2.9 convolution_add_fusion.2
  193.4 2.8 fusion.118
  196.2 1.4 copy-done.1
  197.6 1.7 fusion.126
  199.9 1.4 multiply_reduce_fusion.6
  203.2 2.8 multiply_reduce_fusion.2
  207.3 2.5 fusion.115
  211.6 0.9 dynamic-slice_bitcast_fusion
  212.8 0.9 fusion.113
  213.6 2.2 convert_reduce_fusion.1
  216.9 0.8 convolution_convert_fusion.3
  217.7 1.7 convert_reduce_fusion
  220.8 2.2 convolution_add_fusion.1
  223.3 0.9 convolution_convert_fusion.1
  224.3 0.9 convolution_convert_fusion
  225.5 0.8 convolution_convert_fusion.2
  226.4 2.6 maximum_maximum_fusion.refs_0_
  229.0 1.2 fusion.45
  230.2 1.1 pad_maximum_fusion.5
  231.8 1.0 convert_reduce_fusion.3
  234.4 0.9 pad_maximum_fusion.9
  235.3 1.2 convolution_convert_fusion.4
  236.5 99.3 %shard_map.315 = (bf16[2,3,128,768]{3,2,1,0:T(8,128)(2,1)}, f32[96,768]{1,0:T(8,128)}, f32[2,96,768]{2,1,0:T(8,128)}, f32[80,128]{1,0:T(8,128)}) custom-call(bf16[2,2,4,2,96,768]{5,4,3,2,1,0:T(8,128)(2,1)} %maximum_maximum_fusion.refs_0_, bf16[2,3,64,384]{3,2,1,0:T(8,128)(2,1)} %get-tuple-element.41.refs_1_, bf16[2,3,64,384]{3,2,1,0:T(8,128)(2,1)} %bitcast.203, ...), custom_call_target="tpu_custom_call" | custom-call | tf_op jit(solution)/shard_map/pallas_call | solution.py:866
  335.8 1.0 fusion.121
  336.8 1.0 fusion.122
  338.5 1.4 slice_bitcast_fusion.22
  339.9 1.3 slice_bitcast_fusion.21
  343.3 1.9 slice_bitcast_fusion.17
  347.1 1.0 copy.54
  (204 shorter events, 32.5 us)
Async XLA Ops:
  0.7 202.5 %copy-start = (bf16[6,128,768]{2,1,0:T(8,128)(2,1)S(1)}, bf16[6,128,768]{2,1,0:T(8,128)(2,1)}, u32[]{:S(2)}) copy-start(bf16[6,128,768]{2,1,0:T(8,128)(2,1)} %param.37) | copy-start | bytes 3538948
  127.2 2.1 copy-start.15
  127.5 1.9 copy-start.11
  127.5 2.7 collective-permute-start.1
  128.4 2.1 collective-permute-start
  133.6 7.1 %collective-permute-start.2 = (bf16[768,768]{1,0:T(8,128)(2,1)}, bf16[768,768]{1,0:T(8,128)(2,1)}, u32[]{:S(2)}, u32[]{:S(2)}) collective-permute-start(bf16[768,768]{1,0:T(8,128)(2,1)} %fusion.23), channel_id=1, source_target_pairs={{0,1},{1,0},{2,3},{3,2},{4,5},{5,4},{6,7},{7,6},{8,9},{9,8},{10,11... | collective-permute-start | bytes 3538952 | tf_op jit(solution)/shard_map/ppermute | solution.py:22
  138.1 2.6 copy-start.17
  139.1 1.6 copy-start.30
  177.1 3.2 copy-start.37
  179.9 13.5 %collective-permute-start.3 = (bf16[768,768]{1,0:T(8,128)(2,1)}, bf16[768,768]{1,0:T(8,128)(2,1)}, u32[]{:S(2)}, u32[]{:S(2)}) collective-permute-start(bf16[768,768]{1,0:T(8,128)(2,1)} %slice.336), channel_id=1, source_target_pairs={{0,1},{1,0},{2,3},{3,2},{4,5},{5,4},{6,7},{7,6},{8,9},{9,8},{10,11... | collective-permute-start | bytes 3538952 | tf_op jit(solution)/shard_map/ppermute | solution.py:22
  183.5 3.8 %copy-start.42 = (f32[768]{0:T(1024)S(1)}, f32[768]{0:T(1024)}, u32[]{:S(2)}) copy-start(f32[768]{0:T(1024)} %param.30) | copy-start | bytes 9220
  185.6 4.8 %copy-start.19 = (bf16[192,768]{1,0:T(8,128)(2,1)}, bf16[192,768]{1,0:T(8,128)(2,1)S(1)}, u32[]{:S(2)}) copy-start(bf16[192,768]{1,0:T(8,128)(2,1)S(1)} %get-tuple-element.100) | copy-start | bytes 884740
  185.6 4.8 %copy-start.43 = (f32[768]{0:T(1024)S(1)}, f32[768]{0:T(1024)}, u32[]{:S(2)}) copy-start(f32[768]{0:T(1024)} %slice_reduce_fusion) | copy-start | bytes 9220
  187.3 6.1 %copy-start.22 = (bf16[6,32,768]{2,1,0:T(8,128)(2,1)}, bf16[6,32,768]{2,1,0:T(8,128)(2,1)S(1)}, u32[]{:S(2)}) copy-start(bf16[6,32,768]{2,1,0:T(8,128)(2,1)S(1)} %convolution_convert_fusion.5) | copy-start | bytes 884740
  187.4 6.0 %copy-start.10 = (f32[1536,768]{1,0:T(8,128)S(1)}, f32[1536,768]{1,0:T(8,128)}, u32[]{:S(2)}) copy-start(f32[1536,768]{1,0:T(8,128)} %convolution_add_fusion) | copy-start | bytes 14155780
  190.5 3.0 copy-start.40
  193.4 4.2 %copy-start.18 = (bf16[1,3,2,32,128]{4,3,2,0,1:T(8,128)(2,1)S(1)}, bf16[1,3,2,32,128]{4,3,2,0,1:T(8,128)(2,1)}, u32[]{:S(2)}) copy-start(bf16[1,3,2,32,128]{4,3,2,0,1:T(8,128)(2,1)} %copy-done.17) | copy-start | bytes 147460
  196.2 7.0 %copy-start.28 = (f32[768]{0:T(1024)S(1)}, f32[768]{0:T(1024)}, u32[]{:S(2)}) copy-start(f32[768]{0:T(1024)} %param.33) | copy-start | bytes 9220
  199.3 11.3 %copy-start.2 = (f32[768,768]{1,0:T(8,128)S(1)}, f32[768,768]{1,0:T(8,128)}, u32[]{:S(2)}) copy-start(f32[768,768]{1,0:T(8,128)} %copy-done.1) | copy-start | bytes 7077892
  207.3 3.7 %copy-start.41 = (f32[768]{0:T(1024)S(1)}, f32[768]{0:T(1024)}, u32[]{:S(2)}) copy-start(f32[768]{0:T(1024)} %param.34) | copy-start | bytes 9220
  207.3 8.6 %slice-start = ((s8[4718592]{0:T(1024)(128)(4,1)}), s8[4194304]{0:T(1024)(128)(4,1)S(1)}, s32[]{:S(2)}) async-start(s8[4718592]{0:T(1024)(128)(4,1)} %bitcast.191), calls=%async_computation | async-start | bytes 8388608
  209.8 7.9 %copy-start.25 = (bf16[192,768]{1,0:T(8,128)(2,1)}, bf16[192,768]{1,0:T(8,128)(2,1)S(1)}, u32[]{:S(2)}) copy-start(bf16[192,768]{1,0:T(8,128)(2,1)S(1)} %get-tuple-element.98) | copy-start | bytes 884740
  209.8 3.8 %collective-permute-start.5 = (bf16[192,768]{1,0:T(8,128)(2,1)S(1)}, bf16[192,768]{1,0:T(8,128)(2,1)S(1)}, u32[]{:S(2)}, u32[]{:S(2)}) collective-permute-start(bf16[192,768]{1,0:T(8,128)(2,1)S(1)} %get-tuple-element.98), channel_id=1, source_target_pairs={{0,1},{1,0},{2,3},{3,2},{4,5},{5,4},{6,7},{7,6},{8,9},{9,8},{10,11... | collective-permute-start | bytes 884744 | tf_op jit(solution)/shard_map/ppermute | solution.py:22
  211.0 1.7 copy-start.3
  211.0 1.7 copy-start.6
  211.1 1.7 copy-start.32
  211.1 1.7 copy-start.33
  211.1 2.5 copy-start.48
  211.5 4.3 %copy-start.8 = (bf16[768,768]{1,0:T(8,128)(2,1)}, bf16[768,768]{1,0:T(8,128)(2,1)S(1)}, u32[]{:S(2)}) copy-start(bf16[768,768]{1,0:T(8,128)(2,1)S(1)} %add_convert_fusion) | copy-start | bytes 3538948
  211.5 4.3 %slice-start.1 = ((s8[4718592]{0:T(1024)(128)(4,1)}), s8[524288]{0:T(1024)(128)(4,1)S(1)}, s32[]{:S(2)}) async-start(s8[4718592]{0:T(1024)(128)(4,1)} %bitcast.191), calls=%async_computation.1 | async-start | bytes 1048576
  212.5 16.5 %collective-permute-start.4 = (bf16[3,128,768]{2,1,0:T(8,128)(2,1)}, bf16[3,128,768]{2,1,0:T(8,128)(2,1)}, u32[]{:S(2)}, u32[]{:S(2)}) collective-permute-start(bf16[3,128,768]{2,1,0:T(8,128)(2,1)} %dynamic-slice_bitcast_fusion), channel_id=1, source_target_pairs={{0,2},{1,3},{2,0},{3,1},{4,6},{5,7},{6,4},{7,5},{8,10},{9,11},{10,... | collective-permute-start | bytes 1769480 | tf_op jit(solution)/shard_map/ppermute | solution.py:22
  213.6 4.1 %copy-start.44 = (bf16[192,768]{1,0:T(8,128)(2,1)}, bf16[192,768]{1,0:T(8,128)(2,1)S(1)}, u32[]{:S(2)}) copy-start(bf16[192,768]{1,0:T(8,128)(2,1)S(1)} %collective-permute-done.5) | copy-start | bytes 884740
  215.9 1.8 copy-start.46
  220.8 2.5 copy-start.26
  220.8 2.5 copy-start.45
  220.8 2.5 copy-start.49
  223.1 8.3 %collective-permute-start.6 = (bf16[192,768]{1,0:T(8,128)(2,1)S(1)}, bf16[192,768]{1,0:T(8,128)(2,1)S(1)}, u32[]{:S(2)}, u32[]{:S(2)}) collective-permute-start(bf16[192,768]{1,0:T(8,128)(2,1)S(1)} %slice.337), channel_id=1, source_target_pairs={{0,1},{1,0},{2,3},{3,2},{4,5},{5,4},{6,7},{7,6},{8,9},{9,8},{10,11... | collective-permute-start | bytes 884744 | tf_op jit(solution)/shard_map/ppermute | solution.py:22
  226.4 2.6 copy-start.9
  228.9 2.4 copy-start.5
  228.9 2.4 copy-start.13
  230.2 1.6 copy-start.38
  231.4 1.7 copy-start.31
  231.4 1.8 copy-start.36
  231.4 1.8 copy-start.34
  231.4 1.8 copy-start.35
  231.8 3.5 %copy-start.12 = (bf16[768,384]{1,0:T(8,128)(2,1)S(1)}, bf16[768,384]{1,0:T(8,128)(2,1)}, u32[]{:S(2)}) copy-start(bf16[768,384]{1,0:T(8,128)(2,1)} %copy-done.11) | copy-start | bytes 1769476
  232.8 1.6 collective-permute-start.7
  335.8 11.3 %copy-start.14 = (bf16[2,3,128,768]{3,2,1,0:T(8,128)(2,1)S(1)}, bf16[2,3,128,768]{3,2,1,0:T(8,128)(2,1)}, u32[]{:S(2)}) copy-start(bf16[2,3,128,768]{3,2,1,0:T(8,128)(2,1)} %get-tuple-element.47) | copy-start | bytes 3538948
  (12 other events, 12.7 us)

commit v4 on v3

--- a/solution.py
+++ b/solution.py
@@ -74,6 +74,16 @@
         - jnp.mean(scaled, axis=-1, keepdims=True)
         - normed * jnp.mean(scaled * normed, axis=-1, keepdims=True)
     )
+
+
+def gaussian_parts(t):
+    k = 1.0 / (1.0 + (0.3275911 * 0.5**0.5) * jnp.abs(t))
+    bell = jnp.exp(-0.5 * t * t)
+    series = 0.5 * 1.061405429
+    for a in (-1.453152027, 1.421413741, -0.284496736, 0.254829592):
+        series = series * k + 0.5 * a
+    tail = series * k * bell
+    return jnp.where(t < 0.0, tail, 1.0 - tail), bell
 
 
 def gather(piece, x_first):
@@ -1068,7 +1078,7 @@
 
     def feed(i):
         pre = mm(hidden_all, w_up[i]) + b_up[i]
-        activated = jax.nn.gelu(pre, approximate=False).astype(BF16)
+        activated = (pre * gaussian_parts(pre)[0]).astype(BF16)
         return mm_t(activated, w_down[i])
 
     feed_term = feed(0) + feed(1)
@@ -1105,8 +1115,8 @@
     g_up, g_down, g_up_bias, d_hidden_term = [], [], [], 0.0
     for i in range(2):
         pre = mm(hidden_c_all, w_up[i]) + b_up[i]
-        cdf = 0.5 * (1.0 + lax.erf(pre * (0.5**0.5)))
-        density = jnp.exp(-0.5 * pre * pre) * (0.5 / jnp.pi) ** 0.5
+        cdf, bell = gaussian_parts(pre)
+        density = bell * (0.5 / jnp.pi) ** 0.5
         activated = (pre * cdf).astype(BF16)
         d_pre = (mm(d_feed_all, w_down[i]) * (cdf + pre * density)).astype(BF16)
         g_up_bias.append(jnp.sum(d_pre.astype(F32), axis=0))

time: 354 us -> 331 us (0.935)
  matrix products: 62.6 us -> 49.9 us
  local copies, waits for them, and re-layouts: 44.7 us -> 39 us
    dot_general x6, matrix products: 41 us -> 26.6 us  [mm_t(): lax.dot_general(a, b, (((1,), (1,)), ((), ())), preferred_element_type=F32)]
    unnamed x113 -> x127, local copies, waits for them, and re-layouts: 7.75 us -> 10.6 us
  transfers between devices with their start and end apart: 8 -> 8, of which waited for: 2 -> 1; matrix products, arithmetic and copies ran while one was open for 12% -> 12% of each run, Pallas kernels for 0% -> 0%
where the time goes in v4:
time: 331 us; the launch traced here: 326 us
  Pallas kernels  210 us (63%)
  matrix products  49.9 us (15%)
  local copies, waits for them, and re-layouts  39 us (12%)
  other arithmetic  23.2 us (7%)
    pallas_call x1, Pallas kernels, forward(): pl.pallas_call(functools.partial(forward_kernel, True), out_shape=shapes,...  111 us
    pallas_call x1, Pallas kernels, backward(): pl.pallas_call(functools.partial(back_kernel, True), out_shape=[out(2, bl...  98.7 us
    dot_general x6, matrix products, mm_t(): lax.dot_general(a, b, (((1,), (1,)), ((), ())), preferred_element_type=F32)  26.6 us
    dot_general x5, matrix products, mm(): return jnp.dot(a, b, preferred_element_type=F32)  12.4 us
    unnamed x127, local copies, waits for them, and re-layouts  10.6 us
  transfers between devices with their start and end apart: 8, of which 1 were waited for; matrix products, arithmetic and copies ran while one was open for 12% of the time, Pallas kernels for 0%

profile of v4, /device:TPU:0, one launch (start us, length us, event | category | flops | bytes accessed | tf_op | source)
XLA Modules:
  0.0 326.0 jit_solution(17834732775484288886)
XLA Ops:
  1.5 0.8 broadcast_in_dim.9.refs_5_
  2.9 0.9 copy.39
  6.7 1.7 pad_maximum_fusion.10.refs_1_
  9.9 111.0 %shard_map.314 = (bf16[2,4,2,96,768]{4,3,2,1,0:T(8,128)(2,1)}, bf16[2,2,4,2,96,768]{5,4,3,2,1,0:T(8,128)(2,1)}, bf16[2,3,2,128,768]{4,3,2,1,0:T(8,128)(2,1)}, bf...) custom-call(bf16[96,768]{1,0:T(8,128)(2,1)} %concatenate.42.refs_0_,, ...), custom_call_target="tpu_custom_call" | custom-call | tf_op jit(solution)/shard_map/pallas_call | solution.py:464
  120.8 1.8 fusion.96
  123.2 0.9 copy-done.9
  124.3 1.5 copy-done.17
  126.7 1.0 fusion.100
  128.4 1.4 fusion.11
  129.9 1.5 copy.45
  131.4 1.3 slice_reduce_fusion
  132.7 1.4 fusion.99
  134.2 1.0 fusion.101
  136.8 10.7 %fusion.12 = f32[1536,768]{1,0:T(8,128)} fusion(f32[768]{0:T(1024)} %param.30, bf16[768,768]{1,0:T(8,128)(2,1)} %collective-permute-done.2, bf16[768,768]{1,0:T(8,128)(2,1)} %fusion.11, bf16[2,2,768,768]{3,2,1,0:T(8,128)(2,1)} %bitcast.185), kind=kOutput, calls=%fused_computation.30 | convolution fusion | flops 3654549504 | bytes 9441280 | tf_op jit(solution)/shard_map/dot_general | solution.py:57
  147.5 11.2 %convolution_add_fusion = f32[1536,768]{1,0:T(8,128)} fusion(f32[1536,768]{1,0:T(8,128)} %fusion.12, f32[768]{0:T(1024)} %slice_reduce_fusion, bf16[768,768]{1,0:T(8,128)(2,1)} %collective-permute-done.2, bf16[768,768]{1,0:T(8,128)(2,1)} %fusion.11, bf16[2,2,768,768]{3,2,1,0:T(8,128)(2,1)} %bitcast.186), kind=kOutput, calls=%fused_computation.13 | convolution fusion | flops 3655729152 | bytes 14159872 | tf_op jit(solution)/shard_map/dot_general | solution.py:57
  158.7 2.8 slice.336
  162.6 1.3 div.76
  164.0 1.3 rsqrt.45
  165.3 2.1 add_convert_fusion.1
  167.4 1.7 convolution_convert_fusion.5
  169.1 3.1 convolution_add_fusion.3
  172.2 2.9 convolution_add_fusion.2
  175.2 2.8 fusion.94
  177.9 1.0 fusion.102
  180.9 3.0 multiply_reduce_fusion.2
  184.1 2.3 fusion.91
  188.0 1.0 copy-done.5
  189.3 0.8 fusion.89
  190.1 3.1 convert_reduce_fusion.1
  194.3 0.8 convolution_convert_fusion.3
  195.6 2.1 convert_reduce_fusion
  199.2 2.2 convolution_add_fusion.1
  202.0 1.3 convolution_convert_fusion.1
  203.3 1.4 convolution_convert_fusion
  204.8 0.8 convolution_convert_fusion.2
  205.6 2.4 maximum_maximum_fusion.refs_0_
  208.1 1.1 pad_maximum_fusion.5
  210.4 1.0 convert_reduce_fusion.3
  213.0 0.8 pad_maximum_fusion.9
  213.8 1.2 convolution_convert_fusion.4
  215.0 98.7 %shard_map.315 = (bf16[2,3,128,768]{3,2,1,0:T(8,128)(2,1)}, f32[96,768]{1,0:T(8,128)}, f32[2,96,768]{2,1,0:T(8,128)}, f32[80,128]{1,0:T(8,128)}) custom-call(bf16[2,2,4,2,96,768]{5,4,3,2,1,0:T(8,128)(2,1)} %maximum_maximum_fusion.refs_0_, bf16[2,3,64,384]{3,2,1,0:T(8,128)(2,1)} %get-tuple-element.41.refs_1_, bf16[2,3,64,384]{3,2,1,0:T(8,128)(2,1)} %bitcast.203, ...), custom_call_target="tpu_custom_call" | custom-call | tf_op jit(solution)/shard_map/pallas_call | solution.py:876
  313.7 1.0 fusion.97
  314.7 1.0 fusion.98
  315.7 0.8 slice.245
  316.5 1.4 slice_bitcast_fusion.22
  317.9 1.3 slice_bitcast_fusion.21
  321.3 0.8 slice_bitcast_fusion.17
  324.1 1.0 copy.54
  (224 shorter events, 25.5 us)
Async XLA Ops:
  0.7 180.2 %copy-start = (bf16[6,128,768]{2,1,0:T(8,128)(2,1)S(1)}, bf16[6,128,768]{2,1,0:T(8,128)(2,1)}, u32[]{:S(2)}) copy-start(bf16[6,128,768]{2,1,0:T(8,128)(2,1)} %param.37) | copy-start | bytes 3538948
  0.7 8.4 %slice-start.2 = ((bf16[96,192]{1,0:T(8,128)(2,1)}), bf16[96,128]{1,0:T(8,128)(2,1)S(1)}, s32[]{:S(2)}) async-start(bf16[96,192]{1,0:T(8,128)(2,1)} %param.20), calls=%async_computation.2 | async-start | bytes 49152 | tf_op jit(solution)/shard_map/slice | solution.py:980
  0.7 8.4 %slice-start.3 = ((bf16[96,192]{1,0:T(8,128)(2,1)}), bf16[96,64]{1,0:T(8,128)(2,1)S(1)}, s32[]{:S(2)}) async-start(bf16[96,192]{1,0:T(8,128)(2,1)} %param.20), calls=%async_computation.3 | async-start | bytes 49152 | tf_op jit(solution)/shard_map/slice | solution.py:983
  0.7 8.4 %slice-start.4 = ((bf16[96,192]{1,0:T(8,128)(2,1)}), bf16[96,128]{1,0:T(8,128)(2,1)S(1)}, s32[]{:S(2)}) async-start(bf16[96,192]{1,0:T(8,128)(2,1)} %param.22), calls=%async_computation.4 | async-start | bytes 49152 | tf_op jit(solution)/shard_map/slice | solution.py:981
  0.7 8.4 %slice-start.5 = ((bf16[96,192]{1,0:T(8,128)(2,1)}), bf16[96,64]{1,0:T(8,128)(2,1)S(1)}, s32[]{:S(2)}) async-start(bf16[96,192]{1,0:T(8,128)(2,1)} %param.22), calls=%async_computation.5 | async-start | bytes 49152 | tf_op jit(solution)/shard_map/slice | solution.py:984
  0.7 8.4 %slice-start.6 = ((bf16[96,192]{1,0:T(8,128)(2,1)}), bf16[96,128]{1,0:T(8,128)(2,1)S(1)}, s32[]{:S(2)}) async-start(bf16[96,192]{1,0:T(8,128)(2,1)} %param.23), calls=%async_computation.6 | async-start | bytes 49152 | tf_op jit(solution)/shard_map/slice | solution.py:982
  0.7 8.4 %slice-start.7 = ((bf16[96,192]{1,0:T(8,128)(2,1)}), bf16[96,64]{1,0:T(8,128)(2,1)S(1)}, s32[]{:S(2)}) async-start(bf16[96,192]{1,0:T(8,128)(2,1)} %param.23), calls=%async_computation.7 | async-start | bytes 49152 | tf_op jit(solution)/shard_map/slice | solution.py:985
  123.1 2.8 copy-start.13
  123.1 3.6 %collective-permute-start.1 = (bf16[768,384]{1,0:T(8,128)(2,1)S(1)}, bf16[768,384]{1,0:T(8,128)(2,1)S(1)}, u32[]{:S(2)}, u32[]{:S(2)}) collective-permute-start(bf16[768,384]{1,0:T(8,128)(2,1)S(1)} %pad_maximum_fusion.6), channel_id=1, source_target_pairs={{0,1},{1,0},{2,3},{3,2},{4,5},{5,4},{6,7},{7,6},{8,9},{9,8},{10,11... | collective-permute-start | bytes 1769480 | tf_op jit(solution)/shard_map/ppermute | solution.py:22
  124.1 1.7 copy-start.17
  124.3 2.4 collective-permute-start
  129.9 6.9 %collective-permute-start.2 = (bf16[768,768]{1,0:T(8,128)(2,1)}, bf16[768,768]{1,0:T(8,128)(2,1)}, u32[]{:S(2)}, u32[]{:S(2)}) collective-permute-start(bf16[768,768]{1,0:T(8,128)(2,1)} %fusion.11), channel_id=1, source_target_pairs={{0,1},{1,0},{2,3},{3,2},{4,5},{5,4},{6,7},{7,6},{8,9},{9,8},{10,11... | collective-permute-start | bytes 3538952 | tf_op jit(solution)/shard_map/ppermute | solution.py:22
  158.7 3.3 %copy-start.44 = (f32[6,32]{1,0:T(8,128)S(1)}, f32[6,32]{1,0:T(8,128)}, u32[]{:S(2)}) copy-start(f32[6,32]{1,0:T(8,128)} %multiply_reduce_fusion.7) | copy-start | bytes 2308
  161.5 13.6 %collective-permute-start.3 = (bf16[768,768]{1,0:T(8,128)(2,1)}, bf16[768,768]{1,0:T(8,128)(2,1)}, u32[]{:S(2)}, u32[]{:S(2)}) collective-permute-start(bf16[768,768]{1,0:T(8,128)(2,1)} %slice.336), channel_id=1, source_target_pairs={{0,1},{1,0},{2,3},{3,2},{4,5},{5,4},{6,7},{7,6},{8,9},{9,8},{10,11... | collective-permute-start | bytes 3538952 | tf_op jit(solution)/shard_map/ppermute | solution.py:22
  165.3 2.1 copy-start.30
  165.3 3.8 %copy-start.49 = (f32[768]{0:T(1024)S(1)}, f32[768]{0:T(1024)}, u32[]{:S(2)}) copy-start(f32[768]{0:T(1024)} %param.30) | copy-start | bytes 9220
  167.4 4.8 %copy-start.22 = (bf16[192,768]{1,0:T(8,128)(2,1)}, bf16[192,768]{1,0:T(8,128)(2,1)S(1)}, u32[]{:S(2)}) copy-start(bf16[192,768]{1,0:T(8,128)(2,1)S(1)} %get-tuple-element.100) | copy-start | bytes 884740
  167.4 4.8 %copy-start.50 = (f32[768]{0:T(1024)S(1)}, f32[768]{0:T(1024)}, u32[]{:S(2)}) copy-start(f32[768]{0:T(1024)} %slice_reduce_fusion) | copy-start | bytes 9220
  169.1 3.1 copy-start.25
  169.1 6.0 %copy-start.12 = (f32[1536,768]{1,0:T(8,128)S(1)}, f32[1536,768]{1,0:T(8,128)}, u32[]{:S(2)}) copy-start(f32[1536,768]{1,0:T(8,128)} %convolution_add_fusion) | copy-start | bytes 14155780
  172.2 2.9 copy-start.47
  175.1 2.8 copy-start.21
  177.9 3.0 copy-start.32
  180.9 5.5 %copy-start.3 = (f32[768,768]{1,0:T(8,128)S(1)}, f32[768,768]{1,0:T(8,128)}, u32[]{:S(2)}) copy-start(f32[768,768]{1,0:T(8,128)} %copy-done.2) | copy-start | bytes 7077892
  183.9 2.5 copy-start.43
  183.9 2.5 copy-start.36
  183.9 2.9 copy-start.38
  186.4 8.8 %copy-start.28 = (bf16[192,768]{1,0:T(8,128)(2,1)}, bf16[192,768]{1,0:T(8,128)(2,1)S(1)}, u32[]{:S(2)}) copy-start(bf16[192,768]{1,0:T(8,128)(2,1)S(1)} %get-tuple-element.98) | copy-start | bytes 884740
  186.4 3.8 %collective-permute-start.5 = (bf16[192,768]{1,0:T(8,128)(2,1)S(1)}, bf16[192,768]{1,0:T(8,128)(2,1)S(1)}, u32[]{:S(2)}, u32[]{:S(2)}) collective-permute-start(bf16[192,768]{1,0:T(8,128)(2,1)S(1)} %get-tuple-element.98), channel_id=1, source_target_pairs={{0,1},{1,0},{2,3},{3,2},{4,5},{5,4},{6,7},{7,6},{8,9},{9,8},{10,11... | collective-permute-start | bytes 884744 | tf_op jit(solution)/shard_map/ppermute | solution.py:22
  187.6 2.5 copy-start.10
  187.6 1.7 copy-start.8
  187.6 2.5 copy-start.55
  187.7 20.3 %collective-permute-start.4 = (bf16[3,128,768]{2,1,0:T(8,128)(2,1)S(1)}, bf16[3,128,768]{2,1,0:T(8,128)(2,1)S(1)}, u32[]{:S(2)}, u32[]{:S(2)}) collective-permute-start(bf16[3,128,768]{2,1,0:T(8,128)(2,1)S(1)} %dynamic-slice_bitcast_fusion), channel_id=1, source_target_pairs={{0,2},{1,3},{2,0},{3,1},{4,6},{5,7},{6,4},{7,5},{8,10},{9,11},{10,... | collective-permute-start | bytes 1769480 | tf_op jit(solution)/shard_map/ppermute | solution.py:22
  189.3 4.0 %slice-start = ((s8[4718592]{0:T(1024)(128)(4,1)}), s8[4194304]{0:T(1024)(128)(4,1)S(1)}, s32[]{:S(2)}) async-start(s8[4718592]{0:T(1024)(128)(4,1)} %bitcast.191), calls=%async_computation | async-start | bytes 8388608
  190.1 3.2 slice-start.1
  190.1 5.0 %copy-start.51 = (bf16[192,768]{1,0:T(8,128)(2,1)}, bf16[192,768]{1,0:T(8,128)(2,1)S(1)}, u32[]{:S(2)}) copy-start(bf16[192,768]{1,0:T(8,128)(2,1)S(1)} %collective-permute-done.5) | copy-start | bytes 884740
  199.1 2.8 copy-start.29
  199.1 2.8 copy-start.52
  199.2 2.8 copy-start.56
  201.4 1.8 copy-start.54
  201.5 7.7 %collective-permute-start.6 = (bf16[192,768]{1,0:T(8,128)(2,1)S(1)}, bf16[192,768]{1,0:T(8,128)(2,1)S(1)}, u32[]{:S(2)}, u32[]{:S(2)}) collective-permute-start(bf16[192,768]{1,0:T(8,128)(2,1)S(1)} %slice.337), channel_id=1, source_target_pairs={{0,1},{1,0},{2,3},{3,2},{4,5},{5,4},{6,7},{7,6},{8,9},{9,8},{10,11... | collective-permute-start | bytes 884744 | tf_op jit(solution)/shard_map/ppermute | solution.py:22
  205.6 2.4 copy-start.11
  208.1 1.7 copy-start.15
  211.4 2.4 copy-start.14
  211.4 1.6 collective-permute-start.7
  313.7 7.6 %copy-start.18 = (f32[2,96,768]{2,1,0:T(8,128)S(1)}, f32[2,96,768]{2,1,0:T(8,128)}, u32[]{:S(2)}) copy-start(f32[2,96,768]{2,1,0:T(8,128)} %get-tuple-element.50) | copy-start | bytes 1769476
  315.6 8.4 %copy-start.16 = (bf16[2,3,128,768]{3,2,1,0:T(8,128)(2,1)S(1)}, bf16[2,3,128,768]{3,2,1,0:T(8,128)(2,1)}, u32[]{:S(2)}) copy-start(bf16[2,3,128,768]{3,2,1,0:T(8,128)(2,1)} %get-tuple-element.47) | copy-start | bytes 3538948
  324.1 1.7 copy-start.1
  (25 other events, 29.2 us)

commit v5 on v4

--- a/solution.py
+++ b/solution.py
@@ -494,6 +494,309 @@
     w_attn = w_attn.reshape(2, width, -1)
     w_feed = w_feed.reshape(2, 2, width, -1)
     return (w_attn, w_feed, rows, *rest, far)
+
+
+OUT_BIAS, FIRST_GAIN, FIRST_SHIFT, DOWN_BIAS, SECOND_GAIN, SECOND_SHIFT = range(4, 10)
+
+
+def picked(chosen, rows):
+    high = rows.astype(BF16)
+    rest = (rows - high.astype(F32)).astype(BF16)
+    return mm(chosen, high) + mm(chosen, rest)
+
+
+def column_sum(rows):
+    return jnp.sum(rows, axis=0, keepdims=True)
+
+
+def middle_kernel(
+    wa_ref, wf_in, x_in, attn_ref, select_ref, picks_ref, grads_in, small_ref, far_ref,
+    y_ref, gb_ref, da_ref, db_ref, df_ref, vec_ref,
+    wf, xs, gs, wo, ao, hid, hl, hc, one_c, pre, act, feeds, ft_out, ft_in, rows_ref, ds, dfd, turned_h, turned_d,
+    d_act, d_pre, term, dt_out, dt_in, acc, local_sem, send_sem, recv_sem,
+):
+    blocks, half, width = hid.shape
+    quarter = half // 2
+    cap = df_ref.shape[1] // 2
+    own = blocks * 2 * cap
+    head = lax.axis_index("head")
+    member, pair = lax.rem(head, 2), lax.div(head, 2)
+    sibling_peer = {"head": 2 * pair + 1 - member}
+    y_peer = {"head": lax.rem(head + 2, 4)}
+    barrier = pltpu.get_barrier_semaphore()
+    for peer in (sibling_peer, y_peer):
+        pl.semaphore_signal(barrier, inc=1, device_id=peer, device_id_type=MESH)
+    sent = []
+
+    def remote(src, dst, peer, i):
+        return pltpu.make_async_remote_copy(
+            src_ref=src,
+            dst_ref=dst,
+            send_sem=send_sem.at[i],
+            recv_sem=recv_sem.at[i],
+            device_id=peer,
+            device_id_type=MESH,
+        )
+
+    def send(src, dst, peer):
+        copy = remote(src, dst, peer, 2 * blocks + len(sent))
+        copy.start()
+        sent.append(copy)
+        return copy
+
+    def local(src, dst, i):
+        copy = pltpu.make_async_copy(src, dst, local_sem.at[i])
+        copy.start()
+        return copy
+
+    def hidden_copy(b):
+        return remote(hl.at[0, b], hl.at[1, b], sibling_peer, b)
+
+    def feed_copy(b):
+        return remote(ft_out.at[b], ft_in.at[b], sibling_peer, blocks + b)
+
+    def vector(i):
+        return small_ref[i : i + 1, :]
+
+    up_biases = (small_ref, far_ref)
+
+    fill_x = local(x_in.at[0], xs, 0)
+    fill_w = local(wf_in, wf, 1)
+    fill_g = local(grads_in.at[pl.ds(blocks * pair, blocks)], gs, 2)
+    pl.semaphore_wait(barrier, 2)
+    other_rows = send(attn_ref.at[1], ao, sibling_peer)
+    for p in range(2):
+        wo[0, :, 128 * p : 128 * (p + 1)] = wa_ref[p, :, 640:768]
+    wo[0, :, 256:384] = highs_joined(
+        wa_ref[0, :, 512:640].astype(F32), wa_ref[1, :, 512:640].astype(F32)
+    ).astype(BF16)
+    other_weights = send(wo.at[0], wo.at[1], sibling_peer)
+
+    def branch_own(b, carry):
+        feeds[b] = mm_t(attn_ref[0, b], wo[0])
+        return carry
+
+    lax.fori_loop(0, blocks, branch_own, 0)
+    acc[...] = jnp.zeros_like(acc)
+    fill_x.wait()
+    other_rows.wait_recv()
+    other_weights.wait_recv()
+
+    def first_norm(b, carry):
+        rows = xs[b].reshape(half, width).astype(F32) + feeds[b] + mm_t(ao[b], wo[1]) + vector(OUT_BIAS)
+        hidden = norm_parts(rows)[0] * vector(FIRST_GAIN) + vector(FIRST_SHIFT)
+        low = hidden.astype(BF16)
+        hid[b] = hidden
+        hl[0, b] = low
+        hidden_copy(b).start()
+        for e in range(2):
+            at, run = slice(cap * e, cap * (e + 1)), slice(quarter * e, quarter * (e + 1))
+            chosen = select_ref[b, at, :]
+            one_c[b, at, :] = picked(chosen, rows[run])
+            hc[0, b, at, :] = mm(chosen, low[run]).astype(BF16)
+        return carry
+
+    lax.fori_loop(0, blocks, first_norm, 0)
+    other_listed = send(hc.at[0], hc.at[1], sibling_peer)
+    fill_w.wait()
+
+    def gelu_rows(i, carry):
+        at = pl.ds(pl.multiple_of(16 * i, 16), 16)
+        t = pre[at, :]
+        act[0, at, :] = (t * gaussian_parts(t)[0]).astype(BF16)
+        return carry
+
+    def feed(s, b):
+        out = 0.0
+        for p in range(2):
+            pre[0:half] = mm(hl[s, b], wf[p, 0]) + up_biases[p][3:4, :]
+            lax.fori_loop(0, half // 16, gelu_rows, 0, unroll=2)
+            out = out + mm_t(act[0, 0:half], wf[p, 1])
+        return out
+
+    def feed_other(b, carry):
+        hidden_copy(b).wait_recv()
+        ft_out[b] = feed(1, b).astype(BF16)
+        feed_copy(b).start()
+        return carry
+
+    lax.fori_loop(0, blocks, feed_other, 0)
+
+    def feed_own(b, carry):
+        feeds[b] = feed(0, b)
+        return carry
+
+    lax.fori_loop(0, blocks, feed_own, 0)
+    fill_g.wait()
+
+    def second_norm(b, carry):
+        feed_copy(b).wait_recv()
+        rows = hid[b] + feeds[b] + ft_in[b].astype(F32) + vector(DOWN_BIAS)
+        out = (norm_parts(rows)[0] * vector(SECOND_GAIN) + vector(SECOND_SHIFT)).astype(BF16)
+        listed = []
+        for e in range(2):
+            at, run = slice(cap * e, cap * (e + 1)), slice(quarter * e, quarter * (e + 1))
+            rows_ref[e, b] = out[run]
+            listed.append(picked(select_ref[b, at, :], rows[run]))
+        normed, inverse = norm_parts(jnp.concatenate(listed, axis=0))
+        grad_y = mm(picks_ref[b, 0 : 2 * cap, :], gs[b])
+        d_second = norm_back(grad_y, normed, inverse, vector(SECOND_GAIN))
+        d_feed = d_second.astype(BF16)
+        ds[b] = d_second
+        dfd[0, b] = d_feed
+        acc[3:4] += column_sum(d_feed.astype(F32))
+        acc[4:5] += column_sum(grad_y * normed)
+        acc[5:6] += column_sum(grad_y)
+        return carry
+
+    lax.fori_loop(0, blocks, second_norm, 0)
+    other_d = send(dfd.at[0], dfd.at[1], sibling_peer)
+    moved = send(rows_ref.at[1 - pair], y_ref.at[pair], y_peer)
+    kept = local(rows_ref.at[pair], y_ref.at[pair], 3)
+
+    other_listed.wait_recv()
+
+    def turn(ref, out):
+        flat = ref[...].reshape(2 * own, width)
+        for i in range(2 * own // 128):
+            out[:, 128 * i : 128 * (i + 1)] = flat[128 * i : 128 * (i + 1)].T
+
+    turn(hc, turned_h)
+    other_d.wait_recv()
+    turn(dfd, turned_d)
+
+    for p in range(2):
+        pre[...] = mm(hc[...].reshape(2 * own, width), wf[p, 0]) + up_biases[p][3:4, :]
+        d_act[...] = mm(dfd[...].reshape(2 * own, width), wf[p, 1])
+
+        def back_rows_of(i, total):
+            at = pl.ds(pl.multiple_of(16 * i, 16), 16)
+            t = pre[at, :]
+            cdf, bell = gaussian_parts(t)
+            act[p, at, :] = (t * cdf).astype(BF16)
+            d = (d_act[at, :] * (cdf + t * (bell * (0.5 / jnp.pi) ** 0.5))).astype(BF16)
+            d_pre[p, at, :] = d
+            d = d.astype(F32)
+            return total + (d[0:8] + d[8:16])
+
+        total = lax.fori_loop(0, 2 * own // 16, back_rows_of, jnp.zeros((8, width), F32))
+        acc[6 + p : 7 + p] = column_sum(total)
+        part = mm_t(d_pre[p], wf[p, 0])
+        if p == 0:
+            term[...] = part
+        else:
+            part = part + term[...]
+            dt_out[...] = part[own:].astype(BF16)
+            other_term = send(dt_out, dt_in, sibling_peer)
+            term[0:own] = part[:own]
+
+    gb_ref[0, 0] = mm(turned_h[...], d_pre[0]).astype(BF16)
+    other_term.wait_recv()
+
+    def first_back(b, carry):
+        at = pl.ds(pl.multiple_of(2 * cap * b, 2 * cap), 2 * cap)
+        d_hidden = ds[b] + term[at, :] + dt_in[at, :].astype(F32)
+        normed, inverse = norm_parts(one_c[b])
+        d_first = norm_back(d_hidden, normed, inverse, vector(FIRST_GAIN))
+        d_branch = d_first.astype(BF16)
+        df_ref[b] = d_first
+        db_ref[0, b] = d_branch
+        acc[0:1] += column_sum(d_branch.astype(F32))
+        acc[1:2] += column_sum(d_hidden * normed)
+        acc[2:3] += column_sum(d_hidden)
+        return carry
+
+    lax.fori_loop(0, blocks, first_back, 0)
+    other_branch = send(db_ref.at[0], db_ref.at[1], sibling_peer)
+    gb_ref[0, 1] = mm(turned_d[...], act[0]).astype(BF16)
+    gb_ref[1, 0] = mm(turned_h[...], d_pre[1]).astype(BF16)
+    gb_ref[1, 1] = mm(turned_d[...], act[1]).astype(BF16)
+    tiles = width // 128
+    vec_ref[...] = jnp.zeros_like(vec_ref)
+    for t in range(tiles):
+        lanes = slice(128 * t, 128 * (t + 1))
+        for i in range(6):
+            vec_ref[tiles * i + t : tiles * i + t + 1, :] = acc[i : i + 1, lanes]
+        for h in range(4):
+            mine = jnp.where(head == h, acc[6:7, lanes], 0.0)
+            other = jnp.where(lax.rem(head + 2, 4) == h, acc[7:8, lanes], 0.0)
+            at = tiles * (6 + h) + t
+            vec_ref[at : at + 1, :] = mine + other
+    other_branch.wait_recv()
+    for s in range(2):
+        da = mm(db_ref[s].reshape(own, width), wo[0])
+        da_ref[s] = da.astype(BF16).reshape(da_ref.shape[1:])
+    kept.wait()
+    moved.wait_recv()
+    for copy in sent:
+        copy.wait_send()
+    for b in range(blocks):
+        hidden_copy(b).wait_send()
+        feed_copy(b).wait_send()
+
+
+def middle(w_attn, w_feed, x_rows, attention, select, picks, out_grad, small, far):
+    _, blocks, block_half, lanes = attention.shape
+    width = w_attn.shape[1]
+    quarter = block_half // 2
+    listed = select.shape[1] // 2
+    own = blocks * listed
+
+    def out(*shape, dtype=BF16):
+        return jax.ShapeDtypeStruct(shape, dtype)
+
+    def room(*shape, dtype=BF16):
+        return pltpu.VMEM(shape, dtype)
+
+    in_specs = [vmem_spec()] * 9
+    for i in (1, 2, 6):
+        in_specs[i] = any_spec()
+    return pl.pallas_call(
+        middle_kernel,
+        out_shape=[
+            out(2, blocks, quarter, width),
+            out(*w_feed.shape),
+            out(2, blocks, listed, lanes),
+            out(2, blocks, listed, width),
+            out(blocks, listed, width, dtype=F32),
+            out(64, 128, dtype=F32),
+        ],
+        in_specs=in_specs,
+        out_specs=[vmem_spec()] * 6,
+        scratch_shapes=[
+            room(*w_feed.shape),
+            room(blocks, 2, quarter, width),
+            room(blocks, *out_grad.shape[1:]),
+            room(2, width, lanes),
+            room(blocks, block_half, lanes),
+            room(blocks, block_half, width, dtype=F32),
+            room(2, blocks, block_half, width),
+            room(2, blocks, listed, width),
+            room(blocks, listed, width, dtype=F32),
+            room(2 * own, width, dtype=F32),
+            room(2, 2 * own, width),
+            room(blocks, block_half, width, dtype=F32),
+            room(blocks, block_half, width),
+            room(blocks, block_half, width),
+            room(2, blocks, quarter, width),
+            room(blocks, listed, width, dtype=F32),
+            room(2, blocks, listed, width),
+            room(width, 2 * own),
+            room(width, 2 * own),
+            room(2 * own, width, dtype=F32),
+            room(2, 2 * own, width),
+            room(2 * own, width, dtype=F32),
+            room(own, width),
+            room(own, width),
+            room(8, width, dtype=F32),
+            pltpu.SemaphoreType.DMA((4,)),
+            pltpu.SemaphoreType.DMA((2 * blocks + 7,)),
+            pltpu.SemaphoreType.DMA((2 * blocks + 7,)),
+        ],
+        compiler_params=pltpu.CompilerParams(
+            collective_id=3, vmem_limit_bytes=60 * 2**20, has_side_effects=True
+        ),
+    )(w_attn, w_feed, x_rows, attention, select, picks, out_grad, small, far)
 
 
 def back_queries(b, qc_ref, g_ref, ku_ref, vu_ref, select_ref, o_ref, dt_ref, oc_ref, total_ref):
@@ -1001,173 +1304,35 @@
                 value_bias,
                 jnp.repeat(block_order.astype(F32), HD),
                 up_bias,
+                out_bias,
+                first_gain,
+                first_shift,
+                down_bias,
+                second_gain,
+                second_shift,
             )
         ]
-        + [jnp.zeros((hidden_piece,), F32)] * 4
+        + [jnp.zeros((hidden_piece,), F32)] * 6
     )
     listed = pick(masked_rows.reshape(2, blocks, slots), p)
     (
         w_attn, w_feed, x_rows, rows_t, attention, keys, values, keys_used, values_used, q_compact, picks_b, select_b, small_far,
     ) = forward(tokens, piece, jnp.stack((up_weight, down_weight.T)), small, listed, c, p)
 
-    def tiles(i, second, j):
-        second = HD * second
-
-        return jnp.concatenate(
-            (
-                w_attn[0][:, 128 * i : 128 * i + 128],
-                w_attn[1][:, 128 * i : 128 * i + 128],
-                w_attn[0][:, 128 * j + second : 128 * j + second + HD],
-                w_attn[1][:, 128 * j + second : 128 * j + second + HD],
-            ),
-            axis=1,
-        )
-
-    w_out_t = tiles(5, 1, 4)
-    w_out_other = sibling(w_out_t)
-    w_up, w_down = w_feed[:, 0], w_feed[:, 1]
-    b_up = jnp.stack((up_bias, small_far[3]))
-    x_flat = x_rows.reshape(-1, width)
-    own_count = x_flat.shape[0] // 2
-    attn_shape = (2, blocks, 2 * quarter, columns)
-    compact_shape = (2, blocks, 2 * cap, columns)
-    picks = jnp.transpose(picks_b.reshape(blocks, 2, 2, cap, slots), (1, 0, 2, 3, 4))
-    select = jnp.transpose(
-        select_b.reshape(blocks, 2, 2, cap, quarter), (1, 0, 2, 3, 4)
-    ).reshape(-1, cap, quarter)
-    runs_own = 2 * blocks
-
-    def compact(rows, which=slice(None), **kw):
-        source = select[which]
-        out = jnp.einsum(
-            "ukr,urw->ukw",
-            source.astype(rows.dtype),
-            rows.reshape(source.shape[0], quarter, -1),
-            preferred_element_type=F32,
-            **kw,
-        )
-        return out.reshape(-1, rows.shape[-1])
-
-    def spread(rows, which=slice(None), **kw):
-        source = select[which]
-        out = jnp.einsum(
-            "ukr,ukw->urw",
-            source.astype(rows.dtype),
-            rows.reshape(source.shape[0], cap, -1),
-            preferred_element_type=F32,
-            **kw,
-        )
-        return out.reshape(-1, rows.shape[-1])
-
-    own_runs, other_runs = slice(0, runs_own), slice(runs_own, None)
-    exact = {"precision": lax.Precision.HIGHEST}
-    grads_in = pick(out_grad.reshape(2, blocks, slots, width), p)
-    grad_y = jnp.einsum(
-        "beki,biw->bekw", picks[0], grads_in, preferred_element_type=F32
-    ).reshape(-1, width)
-
-    attn_other = sibling(attention[1]).reshape(own_count, columns)
-    branch = mm_t(attention[0].reshape(own_count, columns), w_out_t) + mm_t(
-        attn_other, w_out_other
-    )
-    sum_one = x_flat[:own_count].astype(F32) + branch + out_bias
-    hidden = norm_parts(sum_one)[0] * first_gain + first_shift
-    hidden_low = hidden.astype(BF16)
-    hidden_other = sibling(hidden_low)
-    hidden_all = jnp.concatenate((hidden_low, hidden_other))
-
-    def feed(i):
-        pre = mm(hidden_all, w_up[i]) + b_up[i]
-        activated = (pre * gaussian_parts(pre)[0]).astype(BF16)
-        return mm_t(activated, w_down[i])
-
-    feed_term = feed(0) + feed(1)
-    feed_out = (
-        feed_term[:own_count]
-        + sibling(feed_term[own_count:].astype(BF16)).astype(F32)
-        + down_bias
-    )
-    sum_two = hidden + feed_out
-    out_rows = (norm_parts(sum_two)[0] * second_gain + second_shift).astype(BF16)
-
-    def to_output(rows):
-        rows = rows.reshape(blocks, 2, quarter, width)
-        kept = pick(rows, p, 1)
-        moved = across(pick(rows, 1 - p, 1))
-        return ordered(p, kept, moved).reshape(block_count, quarter, width)
-
-    out_y = to_output(out_rows)
-
-    one_c = compact(sum_one, own_runs, **exact)
-    two_c = compact(sum_two, own_runs, **exact)
-    normed_two, inverse_two = norm_parts(two_c)
-    normed_one, inverse_one = norm_parts(one_c)
-    hidden_c = (normed_one * first_gain + first_shift).astype(BF16)
-    d_second = norm_back(grad_y, normed_two, inverse_two, second_gain)
-    g_second_gain = jnp.sum(grad_y * normed_two, axis=0)
-    g_second_shift = jnp.sum(grad_y, axis=0)
-    d_feed = d_second.astype(BF16)
-    g_down_bias = jnp.sum(d_feed.astype(F32), axis=0)
-    d_feed_all = jnp.concatenate((d_feed, sibling(d_feed)))
-    hidden_c_all = jnp.concatenate(
-        (hidden_c, compact(hidden_other, other_runs).astype(BF16))
-    )
-    g_up, g_down, g_up_bias, d_hidden_term = [], [], [], 0.0
-    for i in range(2):
-        pre = mm(hidden_c_all, w_up[i]) + b_up[i]
-        cdf, bell = gaussian_parts(pre)
-        density = bell * (0.5 / jnp.pi) ** 0.5
-        activated = (pre * cdf).astype(BF16)
-        d_pre = (mm(d_feed_all, w_down[i]) * (cdf + pre * density)).astype(BF16)
-        g_up_bias.append(jnp.sum(d_pre.astype(F32), axis=0))
-        g_up.append(t_mm(hidden_c_all, d_pre).astype(BF16))
-        g_down.append(t_mm(d_feed_all, activated).astype(BF16))
-        d_hidden_term = d_hidden_term + mm_t(d_pre, w_up[i])
-    compact_own = d_feed.shape[0]
-    d_hidden = (
-        d_second
-        + d_hidden_term[:compact_own]
-        + sibling(d_hidden_term[compact_own:].astype(BF16)).astype(F32)
-    )
-    gb = jnp.stack((jnp.stack(g_up), jnp.stack(g_down)), axis=1)
-    g_first_gain = jnp.sum(d_hidden * normed_one, axis=0)
-    g_first_shift = jnp.sum(d_hidden, axis=0)
-    d_first = norm_back(d_hidden, normed_one, inverse_one, first_gain)
-    d_branch = d_first.astype(BF16)
-    g_out_bias = jnp.sum(d_branch.astype(F32), axis=0)
-    d_branch_all = jnp.concatenate((d_branch, sibling(d_branch)))
-    d_attention = mm(d_branch_all, w_out_t).astype(BF16).reshape(compact_shape)
-
-    def widen(own_first):
-        by_p = ordered(p, own_first[0], own_first[1])
-        zero = jnp.zeros_like(by_p)
-        return jnp.where(
-            c == 0,
-            jnp.stack((by_p, zero), axis=1),
-            jnp.stack((zero, by_p), axis=1),
-        ).reshape(-1)
-
-    vectors = [
-        g_out_bias,
-        g_first_gain,
-        g_first_shift,
-        g_down_bias,
-        g_second_gain,
-        g_second_shift,
-        widen(jnp.stack(g_up_bias)),
-    ]
-    flat = jnp.concatenate(vectors)
-    flat = jnp.pad(flat, (0, -flat.shape[0] % 1024)).reshape(-1, 128)
+    out_y, gb, d_attention, d_branch_all, d_first, flat = middle(
+        w_attn, w_feed, x_rows, attention, select_b, picks_b, out_grad, small, small_far
+    )
+    out_y = out_y.reshape(block_count, quarter, width)
     grad_x, s_attn, s_feed, summed = backward(
         gb, q_compact, d_attention, keys, values, keys_used, values_used, attention, rows_t, w_attn, select_b,
-        small, small_far, d_branch_all.reshape(2, blocks, 2 * cap, width), d_first.reshape(blocks, 2 * cap, width), flat,
+        small, small_far, d_branch_all, d_first, flat,
     )
     grad_x = grad_x.reshape(block_count, quarter, width)
     whole = summed[: flat.shape[0]].reshape(-1)
     ends, start = [], 0
-    for vector in vectors:
-        ends.append(whole[start : start + vector.shape[0]])
-        start += vector.shape[0]
+    for size in [width] * 6 + [4 * hidden_piece]:
+        ends.append(whole[start : start + size])
+        start += size
     v_out_bias, v_first_gain, v_first_shift, v_down_bias, v_second_gain, v_second_shift, v_up_bias = ends
     last = summed[flat.shape[0] :].reshape(2, 2, 4, 128)
     v_query_bias, v_value_bias = (

time: 331 us -> 291 us (0.88); the launches traced: 326 us -> 290 us
  matrix products: 49.9 us -> 0 us
  Pallas kernels: 210 us -> 259 us
  other arithmetic: 23.2 us -> 2.8 us
  local copies, waits for them, and re-layouts: 39 us -> 26.8 us
    dot_general x19 -> x0, matrix products: 49.9 us -> none  [the longest x6 26.6 us: mm_t(): lax.dot_general(a, b, (((1,), (1,)), ((), ())), preferred_element_type=F32)]
    pallas_call x0 -> x1, Pallas kernels: none -> 49 us  [middle(): pl.pallas_call(middle_kernel, out_shape=[out(2, blocks, quarter, width),...]
    slice x12 -> x2, local copies, waits for them, and re-layouts: 10.5 us -> 2.71 us  [per_device(): ends.append(whole[start:start + size])]
    reduce_sum x8 -> x0, other arithmetic: 6.74 us -> none  [the longest x1 2.76 us: norm_parts(): centered = rows - jnp.mean(rows, axis=-1, keepdims=True)]
    convert_element_type x4 -> x0, other arithmetic: 6.29 us -> none  [the longest x1 2.31 us: per_device(): d_feed = d_second.astype(BF16)]
    unnamed x127 -> x14, local copies, waits for them, and re-layouts: 10.6 us -> 4.35 us
    another operation x6 -> x13, local copies, waits for them, and re-layouts: 1.34 us -> 6.13 us  [per_device(): jnp.stack([line(row, hidden_piece) for row in (query_bias, value_bias, jn...]
    another operation x4 -> x0, other arithmetic: 3.58 us -> none  [the longest x1 2.37 us: per_device(): gb = jnp.stack((jnp.stack(g_up), jnp.stack(g_down)), axis=1)]
  transfers between devices with their start and end apart: 8 -> 0, of which waited for: 1 -> 0; matrix products, arithmetic and copies ran while one was open for 12% -> 0% of each run, Pallas kernels for 0% -> 0%
where the time goes in v5:
time: 291 us; the launch traced here: 290 us
  Pallas kernels  259 us (89%)
  local copies, waits for them, and re-layouts  26.8 us (9%)
    pallas_call x1, Pallas kernels, forward(): pl.pallas_call(functools.partial(forward_kernel, True), out_shape=shapes,...  111 us
    pallas_call x1, Pallas kernels, backward(): pl.pallas_call(functools.partial(back_kernel, True), out_shape=[out(2, bl...  99.2 us
    pallas_call x1, Pallas kernels, middle(): pl.pallas_call(middle_kernel, out_shape=[out(2, blocks, quarter, width),...  49 us
    another operation x13, local copies, waits for them, and re-layouts, per_device(): jnp.stack([line(row, hidden_piece) for row in (query_bias, value_bias, jn...  6.13 us

profile of v5, /device:TPU:0, one launch (start us, length us, event | category | flops | bytes accessed | tf_op | source)
XLA Modules:
  0.0 289.7 jit_solution(10173072262602347751)
XLA Ops:
  0.7 0.0 copy-start.3
  0.7 0.0 copy-start.4
  0.7 0.7 convert_element_type.7
  1.4 0.1 broadcast_in_dim.9
  1.5 0.1 reshape.78
  1.6 0.7 stack.55
  2.3 0.7 stack.56
  3.0 0.7 stack.57
  3.6 0.7 stack.54
  4.3 0.7 stack.58
  5.0 0.7 stack.59
  5.7 0.7 stack.60
  6.4 0.7 pad.10
  7.1 0.7 pad.11
  7.8 0.7 reshape.79
  8.5 0.6 broadcast_in_dim.10.refs_4_
  9.1 1.3 stack.63.refs_3_.small_ref.refs_11_
  10.3 0.7 slice.122
  11.1 0.7 slice.119
  11.8 0.7 slice.123
  12.5 0.7 slice.120
  13.3 0.7 slice.124
  14.0 0.7 slice.121
  14.8 0.9 copy.38
  15.7 0.8 concatenate.21.refs_0_
  16.5 0.8 broadcast_in_dim.12.refs_5_
  17.2 0.0 copy-done.3
  17.3 0.0 copy-done.4
  17.3 0.7 pad_maximum_fusion.refs_1_
  18.0 111.1 %shard_map.314 = (bf16[2,4,2,96,768]{4,3,2,1,0:T(8,128)(2,1)}, bf16[2,2,4,2,96,768]{5,4,3,2,1,0:T(8,128)(2,1)}, bf16[2,3,2,128,768]{4,3,2,1,0:T(8,128)(2,1)}, bf...) custom-call(bf16[96,768]{1,0:T(8,128)(2,1)} %concatenate.21.refs_0_,, ...), custom_call_target="tpu_custom_call" | custom-call | tf_op jit(solution)/shard_map/pallas_call | solution.py:464
  129.1 49.0 %shard_map.315 = (bf16[2,3,128,768]{3,2,1,0:T(8,128)(2,1)}, bf16[2,2,768,768]{3,2,1,0:T(8,128)(2,1)}, bf16[2,3,64,384]{3,2,1,0:T(8,128)(2,1)}, bf16[2,3,64,768]{...) custom-call(bf16[2,768,768]{2,1,0:T(8,128)(2,1)} %bitcast.42, bf16[2,2,768,768]{3,2,1,0:T(8,128)(2,1)} %bitcast.46, ...), custom_call_target="tpu_custom_call" | custom-call | tf_op jit(solution)/shard_map/pallas_call | solution.py:754
  178.1 99.2 %shard_map.316 = (bf16[2,3,128,768]{3,2,1,0:T(8,128)(2,1)}, f32[96,768]{1,0:T(8,128)}, f32[2,96,768]{2,1,0:T(8,128)}, f32[80,128]{1,0:T(8,128)}) custom-call(bf16[2,2,4,2,96,768]{5,4,3,2,1,0:T(8,128)(2,1)} %bitcast.45, bf16[2,3,64,384]{3,2,1,0:T(8,128)(2,1)} %get-tuple-element.49.refs_1_, bf16[2,3,64,384]{3,2,1,0:T(8,128)(2,1)} %get-tuple-element.50.refs_2_, ...), custom_call_target="tpu_custom_call" | custom-call | tf_op jit(solution)/shard_map/pallas_call | solution.py:1179
  277.3 0.0 copy-start.2
  277.3 0.8 slice.129
  278.1 0.7 reshape.86
  278.7 0.7 reshape.87
  279.4 1.3 slice_bitcast_fusion.2
  280.7 1.4 slice_bitcast_fusion.3
  282.1 1.0 fusion.1
  283.1 0.9 fusion
  284.0 0.0 copy-start
  284.0 0.7 pad_maximum_fusion.3
  284.7 0.7 copy.40
  285.4 0.7 pad_maximum_fusion.1
  286.1 0.8 slice_bitcast_fusion
  287.0 1.0 copy.43
  288.0 0.7 copy-done.1
  288.7 1.0 copy.44
  (15 shorter events, 0.1 us)
Async XLA Ops:
  0.7 16.6 %copy-start.3 = (bf16[768,96]{0,1:T(8,128)(2,1)S(1)}, bf16[768,96]{0,1:T(8,128)(2,1)}, u32[]{:S(2)}) copy-start(bf16[768,96]{0,1:T(8,128)(2,1)} %param.31) | copy-start | bytes 442372
  0.7 16.6 %copy-start.4 = (bf16[96,768]{1,0:T(8,128)(2,1)S(1)}, bf16[96,768]{1,0:T(8,128)(2,1)}, u32[]{:S(2)}) copy-start(bf16[96,768]{1,0:T(8,128)(2,1)} %param.29) | copy-start | bytes 442372
  277.3 8.9 %copy-start.2 = (f32[2,96,768]{2,1,0:T(8,128)S(1)}, f32[2,96,768]{2,1,0:T(8,128)}, u32[]{:S(2)}) copy-start(f32[2,96,768]{2,1,0:T(8,128)} %get-tuple-element.62) | copy-start | bytes 1769476
  284.0 2.9 %copy-start = (bf16[2,3,128,768]{3,2,1,0:T(8,128)(2,1)S(1)}, bf16[2,3,128,768]{3,2,1,0:T(8,128)(2,1)}, u32[]{:S(2)}) copy-start(bf16[2,3,128,768]{3,2,1,0:T(8,128)(2,1)} %get-tuple-element.47) | copy-start | bytes 3538948
  287.0 1.7 copy-start.1

commit v6 on v5

--- a/solution.py
+++ b/solution.py
@@ -166,6 +166,11 @@
     )
 
 
+def heads_repeated(row):
+    head = lax.div(lax.broadcasted_iota(jnp.int32, (1, 256), 1), HD)
+    return sum(jnp.where(head == h, row[:, h : h + 1], 0.0) for h in range(3))
+
+
 def project(x, wa_ref, count):
     width = x.shape[1]
     tiles = []
@@ -222,11 +227,12 @@
         o_ref[:, b, :, lanes] = pair_lanes(outs).astype(BF16).reshape(2, rows // 2, 128)
 
 
-def forward_listed(b, member, row_ref, col_ref, q_ref, picks_ref, select_ref, qc_ref):
-    slots = row_ref.shape[-1]
+def forward_listed(b, member, pair, listed_ref, q_ref, picks_ref, select_ref, qc_ref):
+    slots = listed_ref.shape[-1]
     quarter = q_ref.shape[2] // 2
     cap = slots // 4
-    row, col = row_ref[b], col_ref[b]
+    row = listed_ref[pl.ds(q_ref.shape[1] * pair + b, 1), :]
+    col = jnp.broadcast_to(row.astype(F32), (slots, slots)).T[:, 0:1].astype(jnp.int32)
     bits = quarter.bit_length() - 1
     run_row = lax.shift_right_arithmetic(row, bits)
     run_col = lax.shift_right_arithmetic(col, bits)
@@ -254,16 +260,26 @@
             qc_ref[s, b, cap * e : cap * (e + 1), :] = mm(select[at : at + cap], rows).astype(BF16)
 
 
+def pack_piece(query_ref, key_ref, value_ref, out_ref, a_ref):
+    out = out_ref[...].T
+    query, key, value = query_ref[...], key_ref[...], value_ref[...]
+    for i, tile in enumerate((query, key, value)):
+        a_ref[:, 128 * i : 128 * (i + 1)] = tile[:, 0:128]
+    a_ref[:, 384:512] = jnp.concatenate((query[:, 128:192], key[:, 128:192]), axis=1)
+    a_ref[:, 512:640] = jnp.concatenate((value[:, 128:192], out[:, 128:192]), axis=1)
+    a_ref[:, 640:768] = out[:, 0:128]
+
+
 def forward_kernel(comm, *refs):
     if comm:
         (
-            a_ref, b_ref, t_ref, small_ref, row_ref, col_ref,
+            query_ref, key_ref, value_ref, out_ref, up_ref, down_ref, t_ref, small_ref, listed_ref,
             wa_ref, wb_ref, x_ref, xt_ref, o_ref, k_ref, v_ref, ku_ref, vu_ref, qc_ref, picks_ref, select_ref, far_ref,
-            xp_ref, q_ref, local_sem, send_sem, recv_sem,
+            a_ref, b_ref, xp_ref, q_ref, local_sem, send_sem, recv_sem,
         ) = refs
     else:
         (
-            wa_ref, x_ref, xp_ref, small_ref, far_ref, row_ref, col_ref,
+            wa_ref, x_ref, xp_ref, small_ref, far_ref, listed_ref,
             xt_ref, o_ref, k_ref, v_ref, ku_ref, vu_ref, qc_ref, picks_ref, select_ref,
             q_ref,
         ) = refs
@@ -272,7 +288,7 @@
     member, pair = lax.rem(head, 2), lax.div(head, 2)
 
     def listed(b, carry):
-        forward_listed(b, member, row_ref, col_ref, q_ref, picks_ref, select_ref, qc_ref)
+        forward_listed(b, member, pair, listed_ref, q_ref, picks_ref, select_ref, qc_ref)
         return carry
 
     def turned(i, carry):
@@ -284,8 +300,9 @@
 
     def bias_of():
         own, other = small_ref[...], far_ref[...]
-        rows = [head_tiles(own[i : i + 1], other[i : i + 1]) for i in range(3)]
-        return (rows[0], rows[1]), rows[2]
+        rows = [head_tiles(own[i : i + 1], other[i : i + 1]) for i in range(2)]
+        order = head_tiles(heads_repeated(own[2:3]), heads_repeated(other[2:3]))
+        return (rows[0], rows[1]), order
 
     if not comm:
         bias, swapped = bias_of()
@@ -301,9 +318,11 @@
         x_peer = {"dp": 2 * z + 1 - x}
         y_peer = {"head": lax.rem(head + 2, 4)}
         sibling_peer = {"head": 2 * pair + 1 - member}
-        z_peers = [{"dp": lax.rem(index + 2 * k, 8)} for k in (1, 2, 3)]
+        z_next = z + 1 - 2 * lax.rem(z, 2)
+        z_far = lax.rem(z + 2, 4)
+        next_peer, far_peer = {"dp": 2 * z_next + x}, {"dp": 2 * z_far + x}
         barrier = pltpu.get_barrier_semaphore()
-        for peer in [x_peer, y_peer, sibling_peer] + z_peers:
+        for peer in (x_peer, y_peer, sibling_peer, next_peer, far_peer):
             pl.semaphore_signal(barrier, inc=1, device_id=peer, device_id_type=MESH)
         counter = [0]
 
@@ -333,7 +352,7 @@
                 dst_ref=xp_ref.at[0, b],
                 send_sem=send_sem.at[15 + b],
                 recv_sem=recv_sem.at[15 + b],
-                device_id=z_peers[1],
+                device_id=far_peer,
                 device_id_type=MESH,
             )
 
@@ -354,31 +373,41 @@
             for s in range(2)
             for e in range(2)
         ]
+        pack_piece(query_ref, key_ref, value_ref, out_ref, a_ref)
         fill_a = local(a_ref, wa_ref.at[0, z, x], 4)
+        pl.semaphore_wait(barrier, 5)
+        a_next = send(a_ref, wa_ref.at[0, z, x], next_peer)
+        a_far = send(a_ref, wa_ref.at[0, z, x], far_peer)
+        far = send(small_ref, far_ref, y_peer)
+        b_ref[0] = up_ref[...]
+        b_ref[1] = down_ref[...]
         fill_b = local(b_ref, wb_ref.at[0, :, z, x], 5)
-        pl.semaphore_wait(barrier, 6)
-        a_z = [send(a_ref, wa_ref.at[0, z, x], peer) for peer in z_peers]
-        far = send(small_ref, far_ref, y_peer)
-        b_z = [send(b_ref, wb_ref.at[0, :, z, x], peer) for peer in z_peers]
+        b_far = send(b_ref, wb_ref.at[0, :, z, x], far_peer)
         for fill in fills:
             fill.wait()
-        for b in range(blocks):
-            far_copy(b).start()
         lax.fori_loop(0, 4 * blocks, turned, 0)
+        a_far.wait_recv()
+        a_pass = send(wa_ref.at[0, z_far, x], wa_ref.at[0, z_far, x], next_peer)
+        b_next = send(b_ref, wb_ref.at[0, :, z, x], next_peer)
+        far_copy(0).start()
         half = a_ref.shape[0] // 2
         up, low = pl.ds(0, half), pl.ds(half, half)
         fill_a.wait()
-        for copy in a_z:
-            copy.wait_recv()
+        a_next.wait_recv()
+        a_pass.wait_recv()
         a_x = send(wa_ref.at[0, :, x, up], wa_ref.at[0, :, x, up], x_peer)
         a_y = send(wa_ref.at[0, :, x, low], wa_ref.at[1, :, x, low], y_peer)
+        b_far.wait_recv()
+        b_pass = send(wb_ref.at[0, :, z_far, x], wb_ref.at[0, :, z_far, x], next_peer)
+        for b in range(1, blocks):
+            far_copy(b).start()
         a_x.wait_recv()
         a_xy = send(wa_ref.at[0, :, :, up], wa_ref.at[1, :, :, up], y_peer)
         a_y.wait_recv()
         a_yx = send(wa_ref.at[:, :, x, low], wa_ref.at[:, :, x, low], x_peer)
         fill_b.wait()
-        for copy in b_z:
-            copy.wait_recv()
+        b_next.wait_recv()
+        b_pass.wait_recv()
         b_x = send(wb_ref.at[0, 0, :, x], wb_ref.at[0, 0, :, x], x_peer)
         b_y = send(wb_ref.at[0, 1, :, x], wb_ref.at[1, 1, :, x], y_peer)
         far.wait_recv()
@@ -393,10 +422,7 @@
     lax.fori_loop(0, blocks, own_block, 0)
     lax.fori_loop(0, blocks, listed, 0)
     if comm:
-        b_x.wait_recv()
-        b_xy = send(wb_ref.at[0, 0], wb_ref.at[1, 0], y_peer)
-        b_y.wait_recv()
-        b_yx = send(wb_ref.at[:, 1, :, x], wb_ref.at[:, 1, :, x], x_peer)
+
         def attend_block(b, carry):
             far_copy(b).wait_recv()
             near = near_copy(b)
@@ -405,7 +431,12 @@
             forward_attend(b, xp_ref, wa_ref, bias, swapped, q_ref, k_ref, v_ref, ku_ref, vu_ref, o_ref)
             return carry
 
-        lax.fori_loop(0, blocks, attend_block, 0)
+        lax.fori_loop(0, 1, attend_block, 0)
+        b_x.wait_recv()
+        b_xy = send(wb_ref.at[0, 0], wb_ref.at[1, 0], y_peer)
+        b_y.wait_recv()
+        b_yx = send(wb_ref.at[:, 1, :, x], wb_ref.at[:, 1, :, x], x_peer)
+        lax.fori_loop(1, blocks, attend_block, 0)
         b_xy.wait_recv()
         b_yx.wait_recv()
         for copy in sent:
@@ -430,7 +461,7 @@
     return pl.BlockSpec(memory_space=pl.ANY)
 
 
-def forward(tokens, piece_a, piece_b, small, listed, member, pair):
+def forward(tokens, weights, small, listed, member, pair):
     n = lax.axis_size("dp")
     block_count, block_rows, width = tokens.shape
     blocks, quarter = block_count // 2, block_rows // 4
@@ -438,7 +469,8 @@
     cap = slots // 4
     lanes = 6 * HD
     tokens = tokens.reshape(block_count, 4, quarter, width)
-    row, col = listed[:, None, :], listed[:, :, None]
+    query, key, value, out_weight, up_weight, down_weight = weights
+    piece_rows, hidden = up_weight.shape
     rows_shape = (2, blocks, 2, quarter, width)
 
     def out(*shape, dtype=BF16):
@@ -453,8 +485,8 @@
     params = dict(vmem_limit_bytes=60 * 2**20, has_side_effects=True)
     if n == 8:
         shapes = [
-            out(2, 4, 2, *piece_a.shape),
-            out(2, 2, 4, 2, *piece_b.shape[1:]),
+            out(2, 4, 2, piece_rows, 12 * HD),
+            out(2, 2, 4, 2, piece_rows, hidden),
             out(*rows_shape),
             *tail,
             out(*small.shape, dtype=F32),
@@ -464,9 +496,11 @@
         results = pl.pallas_call(
             functools.partial(forward_kernel, True),
             out_shape=shapes,
-            in_specs=[vmem_spec(), vmem_spec(), any_spec()] + [vmem_spec()] * 3,
+            in_specs=[vmem_spec()] * 6 + [any_spec()] + [vmem_spec()] * 2,
             out_specs=specs,
             scratch_shapes=[
+                pltpu.VMEM((piece_rows, 12 * HD), BF16),
+                pltpu.VMEM((2, piece_rows, hidden), BF16),
                 pltpu.VMEM(rows_shape, BF16),
                 pltpu.VMEM(dense, BF16),
                 pltpu.SemaphoreType.DMA((6,)),
@@ -474,23 +508,31 @@
                 pltpu.SemaphoreType.DMA((15 + 2 * blocks,)),
             ],
             compiler_params=pltpu.CompilerParams(collective_id=1, **params),
-        )(piece_a, piece_b, tokens, small, row, col)
+        )(*weights, tokens, small, listed)
         w_attn, w_feed, rows, *rest, far = results
     else:
         mine = pick(tokens.reshape(2, blocks, 2, 2, quarter, width), pair)
         rows = jnp.stack((pick(mine, member, 2), pick(mine, 1 - member, 2)))
+        out_t = out_weight.T
+        first, last = slice(0, 2 * HD), slice(2 * HD, 3 * HD)
+        piece_a = jnp.concatenate(
+            [part[:, first] for part in (query, key, value)]
+            + [part[:, last] for part in (query, key, value, out_t)]
+            + [out_t[:, first]],
+            axis=1,
+        )
         w_attn = gather(piece_a, True)
-        w_feed = jnp.stack([gather(piece_b[i], True) for i in range(2)], axis=1)
+        w_feed = jnp.stack([gather(piece, True) for piece in (up_weight, down_weight)], axis=1)
         far = across(small)
         shapes = tail
         rest = pl.pallas_call(
             functools.partial(forward_kernel, False),
             out_shape=shapes,
-            in_specs=[vmem_spec()] * 7,
+            in_specs=[vmem_spec()] * 6,
             out_specs=[vmem_spec()] * len(shapes),
             scratch_shapes=[pltpu.VMEM(dense, BF16)],
             compiler_params=pltpu.CompilerParams(vmem_limit_bytes=60 * 2**20),
-        )(w_attn.reshape(2, width, -1), rows, partner(rows), small, far, row, col)
+        )(w_attn.reshape(2, width, -1), rows, partner(rows), small, far, listed)
     w_attn = w_attn.reshape(2, width, -1)
     w_feed = w_feed.reshape(2, 2, width, -1)
     return (w_attn, w_feed, rows, *rest, far)
@@ -510,8 +552,8 @@
 
 
 def middle_kernel(
-    wa_ref, wf_in, x_in, attn_ref, select_ref, picks_ref, grads_in, small_ref, far_ref,
-    y_ref, gb_ref, da_ref, db_ref, df_ref, vec_ref,
+    wa_ref, wf_in, x_in, attn_ref, select_ref, picks_ref, grads_in, small_ref, far_ref, qc_ref,
+    y_ref, gb_ref, da_ref, db_ref, df_ref, vec_ref, qf_ref,
     wf, xs, gs, wo, ao, hid, hl, hc, one_c, pre, act, feeds, ft_out, ft_in, rows_ref, ds, dfd, turned_h, turned_d,
     d_act, d_pre, term, dt_out, dt_in, acc, local_sem, send_sem, recv_sem,
 ):
@@ -523,8 +565,10 @@
     member, pair = lax.rem(head, 2), lax.div(head, 2)
     sibling_peer = {"head": 2 * pair + 1 - member}
     y_peer = {"head": lax.rem(head + 2, 4)}
+    devices = lax.axis_size("dp")
+    partner_peer = {"dp": lax.rem(lax.axis_index("dp") + devices // 2, devices)}
     barrier = pltpu.get_barrier_semaphore()
-    for peer in (sibling_peer, y_peer):
+    for peer in (sibling_peer, y_peer, partner_peer):
         pl.semaphore_signal(barrier, inc=1, device_id=peer, device_id_type=MESH)
     sent = []
 
@@ -563,7 +607,8 @@
     fill_x = local(x_in.at[0], xs, 0)
     fill_w = local(wf_in, wf, 1)
     fill_g = local(grads_in.at[pl.ds(blocks * pair, blocks)], gs, 2)
-    pl.semaphore_wait(barrier, 2)
+    pl.semaphore_wait(barrier, 3)
+    far_queries = send(qc_ref, qf_ref, partner_peer)
     other_rows = send(attn_ref.at[1], ao, sibling_peer)
     for p in range(2):
         wo[0, :, 128 * p : 128 * (p + 1)] = wa_ref[p, :, 640:768]
@@ -728,6 +773,7 @@
         da_ref[s] = da.astype(BF16).reshape(da_ref.shape[1:])
     kept.wait()
     moved.wait_recv()
+    far_queries.wait_recv()
     for copy in sent:
         copy.wait_send()
     for b in range(blocks):
@@ -735,7 +781,7 @@
         feed_copy(b).wait_send()
 
 
-def middle(w_attn, w_feed, x_rows, attention, select, picks, out_grad, small, far):
+def middle(w_attn, w_feed, x_rows, attention, select, picks, out_grad, small, far, q_compact):
     _, blocks, block_half, lanes = attention.shape
     width = w_attn.shape[1]
     quarter = block_half // 2
@@ -748,7 +794,7 @@
     def room(*shape, dtype=BF16):
         return pltpu.VMEM(shape, dtype)
 
-    in_specs = [vmem_spec()] * 9
+    in_specs = [vmem_spec()] * 10
     for i in (1, 2, 6):
         in_specs[i] = any_spec()
     return pl.pallas_call(
@@ -760,9 +806,10 @@
             out(2, blocks, listed, width),
             out(blocks, listed, width, dtype=F32),
             out(64, 128, dtype=F32),
+            out(*q_compact.shape),
         ],
         in_specs=in_specs,
-        out_specs=[vmem_spec()] * 6,
+        out_specs=[vmem_spec()] * 7,
         scratch_shapes=[
             room(*w_feed.shape),
             room(blocks, 2, quarter, width),
@@ -790,13 +837,13 @@
             room(own, width),
             room(8, width, dtype=F32),
             pltpu.SemaphoreType.DMA((4,)),
-            pltpu.SemaphoreType.DMA((2 * blocks + 7,)),
-            pltpu.SemaphoreType.DMA((2 * blocks + 7,)),
+            pltpu.SemaphoreType.DMA((2 * blocks + 8,)),
+            pltpu.SemaphoreType.DMA((2 * blocks + 8,)),
         ],
         compiler_params=pltpu.CompilerParams(
             collective_id=3, vmem_limit_bytes=60 * 2**20, has_side_effects=True
         ),
-    )(w_attn, w_feed, x_rows, attention, select, picks, out_grad, small, far)
+    )(w_attn, w_feed, x_rows, attention, select, picks, out_grad, small, far, q_compact)
 
 
 def back_queries(b, qc_ref, g_ref, ku_ref, vu_ref, select_ref, o_ref, dt_ref, oc_ref, total_ref):
@@ -932,13 +979,32 @@
     return first, second
 
 
+def store_vectors(total, refs):
+    at = 0
+    rows = total.shape[0] - 16
+    for ref in refs[:7]:
+        for t in range(ref.shape[0] // 128):
+            ref[128 * t : 128 * (t + 1)] = total[at]
+            at += 1
+    for i, ref in enumerate(refs[7:]):
+        for h in (0, 2):
+            line = rows + 4 * i + h
+            one, two = total[line : line + 1], total[line + 1 : line + 2]
+            one_last, two_last = total[line + 8 : line + 9], total[line + 9 : line + 10]
+            tiles = (one, halves_joined(one_last, two), highs_joined(two, pltpu.roll(two_last, HD, 1)))
+            for t, tile in enumerate(tiles):
+                at = 192 * h + 128 * t
+                ref[at : at + 128] = tile[0]
+
+
 def back_kernel(comm, *refs):
     if comm:
         (
-            gb_ref, qc_ref, g_ref, k_ref, v_ref, ku_ref, vu_ref, o_ref, xt_ref, wa_ref,
+            gb_ref, qf_ref, qc_ref, g_ref, k_ref, v_ref, ku_ref, vu_ref, o_ref, xt_ref, wa_ref,
             select_ref, small_ref, far_ref, db_ref, df_ref, vec_ref,
-            gx_ref, sa_ref, sb_ref, sum_ref,
-            dt_ref, oc_ref, ga_ref, total_ref, qf_ref, gf_ref, term_ref, near_ref, rows_ref,
+            gx_ref, gq_ref, gk_ref, gv_ref, go_ref, gu_ref, gd_ref,
+            v1_ref, v2_ref, v3_ref, v4_ref, v5_ref, v6_ref, v7_ref, v8_ref, v9_ref,
+            dt_ref, oc_ref, ga_ref, total_ref, gf_ref, term_ref, near_ref, rows_ref,
             b1_up, b1_low, b2, b3, a1_up, a1_low, a2, a3, vec1, vec4,
             local_sem, send_sem, recv_sem,
         ) = refs
@@ -952,7 +1018,7 @@
     blocks = k_ref.shape[1]
     head = lax.axis_index("head")
     member, pair = lax.rem(head, 2), lax.div(head, 2)
-    swapped = head_tiles(small_ref[2:3], far_ref[2:3])
+    swapped = head_tiles(heads_repeated(small_ref[2:3]), heads_repeated(far_ref[2:3]))
     total_ref[...] = jnp.zeros_like(total_ref)
 
     def queries(b, carry):
@@ -1015,12 +1081,10 @@
         return send(up_other, up_buffer, y_peer), send(low_other, low_buffer, x_peer)
 
     far_g = send(g_ref, gf_ref, z_peers[1])
-    far_q = send(qc_ref, qf_ref, z_peers[1])
     b_up = send(gb_ref.at[1, 0], b1_up, y_peer)
     b_low = send(gb_ref.at[:, 1, :, 1 - x], b1_low, x_peer)
     lax.fori_loop(0, blocks, queries, 0)
     far_g.wait_recv()
-    far_q.wait_recv()
     lax.fori_loop(0, blocks, keys, 0)
 
     vec_rows = vec_ref.shape[0]
@@ -1138,25 +1202,40 @@
         total = b2[t, z].astype(F32)
         for k in range(3):
             total = total + b3[k, t].astype(F32)
-        sb_ref[t] = total
+        if t == 0:
+            gu_ref[...] = total
+        else:
+            gd_ref[...] = total
     own_vec.wait()
     for copy in v_z:
         copy.wait_recv()
-    sum_ref[...] = (vec4[0] + vec4[1]) + (vec4[2] + vec4[3])
+    store_vectors(
+        (vec4[0] + vec4[1]) + (vec4[2] + vec4[3]),
+        (v1_ref, v2_ref, v3_ref, v4_ref, v5_ref, v6_ref, v7_ref, v8_ref, v9_ref),
+    )
     for copy in a_z:
         copy.wait_recv()
-    for t, part in enumerate((up, low)):
+    halves_of_a = []
+    for t in range(2):
         total = a2[t, z].astype(F32)
         for k in range(3):
             total = total + a3[k, t].astype(F32)
-        sa_ref[part] = total
+        halves_of_a.append(total)
+    total = jnp.concatenate(halves_of_a, axis=0)
+    last = total[:, 384:512], total[:, 512:640]
+    seconds = [pltpu.roll(tile, HD, 1) for tile in last]
+    for ref, i, tile in ((gq_ref, 0, last[0]), (gk_ref, 1, seconds[0]), (gv_ref, 2, last[1])):
+        ref[:, 0:128] = total[:, 128 * i : 128 * (i + 1)]
+        ref[:, 128:192] = tile[:, 0:HD]
+    go_ref[0:128, :] = total[:, 640:768].T
+    go_ref[128:192, :] = seconds[1].T[0:HD, :]
     kept.wait()
     moved.wait_recv()
     for copy in sent:
         copy.wait_send()
 
 
-def backward(gb, q_compact, d_attention, keys, values, keys_used, values_used, attention, rows_t, w_attn, select, small, far, d_branch, d_first, vectors):
+def backward(gb, q_far, q_compact, d_attention, keys, values, keys_used, values_used, attention, rows_t, w_attn, select, small, far, d_branch, d_first, vectors):
     n = lax.axis_size("dp")
     _, blocks, block_half, lanes = keys.shape
     width = rows_t.shape[0]
@@ -1164,6 +1243,7 @@
     piece = width // n
     slots = select.shape[1]
     vec_rows = vectors.shape[0] + 16
+    sizes = [width] * 6 + [4 * width] + [width] * 2
 
     def out(*shape, dtype=BF16):
         return jax.ShapeDtypeStruct(shape, dtype)
@@ -1180,17 +1260,20 @@
             functools.partial(back_kernel, True),
             out_shape=[
                 out(2, blocks, quarter, width),
+                out(piece, width // 4, dtype=F32),
+                out(piece, width // 4, dtype=F32),
+                out(piece, width // 4, dtype=F32),
+                out(width // 4, piece, dtype=F32),
                 out(piece, width, dtype=F32),
-                out(2, piece, width, dtype=F32),
-                out(vec_rows, 128, dtype=F32),
-            ],
-            in_specs=[vmem_spec()] * 16,
-            out_specs=[vmem_spec()] * 4,
+                out(piece, width, dtype=F32),
+            ]
+            + [out(size, dtype=F32) for size in sizes],
+            in_specs=[vmem_spec()] * 17,
+            out_specs=[vmem_spec()] * (7 + len(sizes)),
             scratch_shapes=scratch
             + [
                 pltpu.VMEM((2, 4, 2, piece, width), BF16),
                 pltpu.VMEM((8, lanes), F32),
-                pltpu.VMEM(compact, BF16),
                 pltpu.VMEM(compact, BF16),
                 pltpu.VMEM((blocks, block_half, width), BF16),
                 pltpu.VMEM((blocks, block_half, width), BF16),
@@ -1212,7 +1295,7 @@
             compiler_params=pltpu.CompilerParams(
                 collective_id=2, vmem_limit_bytes=62 * 2**20, has_side_effects=True
             ),
-        )(gb.reshape(2, 2, 4, 2, piece, width), *shared, d_first, vectors)
+        )(gb.reshape(2, 2, 4, 2, piece, width), q_far, *shared, d_first, vectors)
     ga, term, both = pl.pallas_call(
         functools.partial(back_kernel, False),
         out_shape=[
@@ -1224,7 +1307,7 @@
         out_specs=[vmem_spec()] * 3,
         scratch_shapes=scratch + [pltpu.VMEM((8, lanes), F32)],
         compiler_params=pltpu.CompilerParams(vmem_limit_bytes=62 * 2**20),
-    )(partner(q_compact), partner(d_attention), *shared)
+    )(q_far, partner(d_attention), *shared)
     pair = lax.axis_index("head") // 2
     cap = slots // 4
     chosen = select[:, : 2 * cap].reshape(blocks, 2, cap, quarter).astype(F32)
@@ -1240,7 +1323,51 @@
     pieces = (2, n, piece, width)
     s_attn = reduce_scatter(ga.reshape(pieces), True)
     s_feed = jnp.stack([reduce_scatter(gb[:, i].reshape(pieces), True) for i in range(2)])
-    return grad_x, s_attn, s_feed, lax.psum(jnp.concatenate((vectors, both)), ("dp", "head"))
+    summed = lax.psum(jnp.concatenate((vectors, both)), ("dp", "head"))
+    whole, ends, start = summed.reshape(-1), [], 0
+    for size in sizes[:7]:
+        ends.append(whole[start : start + size])
+        start += size
+    last = summed[vectors.shape[0] :].reshape(2, 2, 4, 128)
+    ends += [
+        jnp.concatenate((last[0, i], last[1, i, :, :HD]), axis=-1).reshape(-1) for i in range(2)
+    ]
+
+    def columns_of(i, j, second):
+        at = 128 * j + HD * second
+        return jnp.concatenate((s_attn[:, 128 * i : 128 * (i + 1)], s_attn[:, at : at + HD]), axis=1)
+
+    return (
+        grad_x,
+        columns_of(0, 3, 0),
+        columns_of(1, 3, 1),
+        columns_of(2, 4, 0),
+        columns_of(5, 4, 1).T,
+        s_feed[0],
+        s_feed[1],
+        *ends,
+    )
+
+
+def deliver_kernel(*refs):
+    count = (len(refs) - 1) // 2
+    copies = [
+        pltpu.make_async_copy(refs[i], refs[count + i], refs[-1].at[i]) for i in range(count)
+    ]
+    for copy in copies:
+        copy.start()
+    for copy in copies:
+        copy.wait()
+
+
+def deliver(arrays):
+    return pl.pallas_call(
+        deliver_kernel,
+        out_shape=[jax.ShapeDtypeStruct(array.shape, array.dtype) for array in arrays],
+        in_specs=[vmem_spec()] * len(arrays),
+        out_specs=[any_spec()] * len(arrays),
+        scratch_shapes=[pltpu.SemaphoreType.DMA((len(arrays),))],
+    )(*arrays)
 
 
 def per_device(
@@ -1266,99 +1393,68 @@
 ):
     block_count, block_rows, width = tokens.shape
     quarter = block_rows // 4
-    slots = masked_rows.shape[1]
-    cap = slots // 4
-    blocks = block_count // 2
-    piece_rows = query_weight.shape[0]
-    local = query_weight.shape[1]
-    columns = 2 * local
     hidden_piece = up_weight.shape[1]
     head = lax.axis_index("head")
     c, p = head % 2, head // 2
 
-    out_t = out_weight.T
-    first, last = slice(0, 2 * HD), slice(2 * HD, 3 * HD)
-    piece = jnp.concatenate(
-        (
-            query_weight[:, first],
-            key_weight[:, first],
-            value_weight[:, first],
-            query_weight[:, last],
-            key_weight[:, last],
-            value_weight[:, last],
-            out_t[:, last],
-            out_t[:, first],
-        ),
-        axis=1,
-    )
-    half = piece_rows // 2
-
-    def line(vector, size):
-        return jnp.pad(vector, (0, size - vector.shape[0]))
-
-    small = jnp.stack(
-        [
-            line(row, hidden_piece)
-            for row in (
-                query_bias,
-                value_bias,
-                jnp.repeat(block_order.astype(F32), HD),
-                up_bias,
-                out_bias,
-                first_gain,
-                first_shift,
-                down_bias,
-                second_gain,
-                second_shift,
-            )
-        ]
-        + [jnp.zeros((hidden_piece,), F32)] * 6
-    )
-    listed = pick(masked_rows.reshape(2, blocks, slots), p)
+    lines = (
+        query_bias,
+        value_bias,
+        block_order.astype(F32),
+        up_bias,
+        out_bias,
+        first_gain,
+        first_shift,
+        down_bias,
+        second_gain,
+        second_shift,
+    )
+    flat = []
+    for vector in lines:
+        flat += [vector, jnp.zeros((hidden_piece - vector.shape[0],), F32)]
+    flat.append(jnp.zeros((6 * hidden_piece,), F32))
+    small = jnp.concatenate(flat).reshape(16, hidden_piece)
     (
         w_attn, w_feed, x_rows, rows_t, attention, keys, values, keys_used, values_used, q_compact, picks_b, select_b, small_far,
-    ) = forward(tokens, piece, jnp.stack((up_weight, down_weight.T)), small, listed, c, p)
-
-    out_y, gb, d_attention, d_branch_all, d_first, flat = middle(
-        w_attn, w_feed, x_rows, attention, select_b, picks_b, out_grad, small, small_far
-    )
+    ) = forward(
+        tokens,
+        (query_weight, key_weight, value_weight, out_weight, up_weight, down_weight.T),
+        small,
+        masked_rows,
+        c,
+        p,
+    )
+
+    out_y, gb, d_attention, d_branch_all, d_first, flat, q_far = middle(
+        w_attn, w_feed, x_rows, attention, select_b, picks_b, out_grad, small, small_far, q_compact
+    )
+    grad_x, g_query, g_key, g_value, g_out, g_up, g_down, *ends = backward(
+        gb, q_far, q_compact, d_attention, keys, values, keys_used, values_used, attention, rows_t, w_attn, select_b,
+        small, small_far, d_branch_all, d_first, flat,
+    )
+    (
+        v_out_bias, v_first_gain, v_first_shift, v_down_bias, v_second_gain, v_second_shift, v_up_bias, v_query_bias, v_value_bias,
+        out_y, grad_x, g_query, g_key, g_value, g_out, g_up, g_down,
+    ) = deliver((*ends, out_y, grad_x, g_query, g_key, g_value, g_out, g_up, g_down))
+
     out_y = out_y.reshape(block_count, quarter, width)
-    grad_x, s_attn, s_feed, summed = backward(
-        gb, q_compact, d_attention, keys, values, keys_used, values_used, attention, rows_t, w_attn, select_b,
-        small, small_far, d_branch_all, d_first, flat,
-    )
     grad_x = grad_x.reshape(block_count, quarter, width)
-    whole = summed[: flat.shape[0]].reshape(-1)
-    ends, start = [], 0
-    for size in [width] * 6 + [4 * hidden_piece]:
-        ends.append(whole[start : start + size])
-        start += size
-    v_out_bias, v_first_gain, v_first_shift, v_down_bias, v_second_gain, v_second_shift, v_up_bias = ends
-    last = summed[flat.shape[0] :].reshape(2, 2, 4, 128)
-    v_query_bias, v_value_bias = (
-        jnp.concatenate((last[0, i], last[1, i, :, :HD]), axis=-1).reshape(-1)
-        for i in range(2)
-    )
-
-    def columns_of(i, j, second):
-        at = 128 * j + HD * second
-        return jnp.concatenate((s_attn[:, 128 * i : 128 * (i + 1)], s_attn[:, at : at + HD]), axis=1)
 
     return (
         out_y,
         grad_x,
-        columns_of(0, 3, 0),
+        g_query,
         v_query_bias,
-        columns_of(1, 3, 1),
-        columns_of(2, 4, 0),
+        g_key,
+        g_value,
         v_value_bias,
-        columns_of(5, 4, 1).T,
+        g_out,
         v_out_bias,
         v_first_gain,
         v_first_shift,
-        s_feed[0],
+        g_up,
         v_up_bias,
-        s_feed[1].T,
+        g_down.T,
         v_down_bias,
         v_second_gain,
         v_second_shift,

time: 291 us -> 245 us (0.84)
  local copies, waits for them, and re-layouts: 26.8 us -> 1.54 us
  Pallas kernels: 259 us -> 242 us
    pallas_call x1, Pallas kernels: 111 us -> 87.8 us  [forward(): pl.pallas_call(functools.partial(forward_kernel, True), out_shape=shapes,...]
    slice x13 -> x0, local copies, waits for them, and re-layouts: 9.82 us -> none  [the longest x2 2.71 us: per_device(): ends.append(whole[start:start + size])]
    another operation x13 -> x1, local copies, waits for them, and re-layouts: 6.13 us -> 0.01 us  [per_device(): jnp.stack([line(row, hidden_piece) for row in (query_bias, value_bias, jn...]
    pallas_call x1, Pallas kernels: 49 us -> 54.4 us  [middle(): pl.pallas_call(middle_kernel, out_shape=[out(2, blocks, quarter, width),...]
    unnamed x14 -> x0, local copies, waits for them, and re-layouts: 4.35 us -> none
    pallas_call x0 -> x1, Pallas kernels: none -> 3.87 us  [deliver(): pl.pallas_call(deliver_kernel, out_shape=[jax.ShapeDtypeStruct(array.shap...]
    pallas_call x1, Pallas kernels: 99.2 us -> 95.7 us  [backward(): pl.pallas_call(functools.partial(back_kernel, True), out_shape=[out(2, bl...]
where the time goes in v6:
time: 245 us
  Pallas kernels  242 us (99%)
    pallas_call x1, Pallas kernels, backward(): pl.pallas_call(functools.partial(back_kernel, True), out_shape=[out(2, bl...  95.7 us
    pallas_call x1, Pallas kernels, forward(): pl.pallas_call(functools.partial(forward_kernel, True), out_shape=shapes,...  87.8 us
    pallas_call x1, Pallas kernels, middle(): pl.pallas_call(middle_kernel, out_shape=[out(2, blocks, quarter, width),...  54.4 us

profile of v6, /device:TPU:0, one launch (start us, length us, event | category | flops | bytes accessed | tf_op | source)
XLA Modules:
  0.0 244.7 jit_solution(15485513982143249999)
XLA Ops:
  0.7 0.7 convert_element_type.3
  1.3 0.9 concatenate.3
  2.2 0.6 reshape.56.refs_7_.small_ref.refs_12_
  2.9 87.8 %shard_map.314 = (bf16[2,4,2,96,768]{4,3,2,1,0:T(8,128)(2,1)}, bf16[2,2,4,2,96,768]{5,4,3,2,1,0:T(8,128)(2,1)}, bf16[2,3,2,128,768]{4,3,2,1,0:T(8,128)(2,1)}, bf...) custom-call(bf16[96,192]{1,0:T(8,128)(2,1)} %refs_0_.1, ...), custom_call_target="tpu_custom_call" | custom-call | tf_op jit(solution)/shard_map/pallas_call | solution.py:496
  90.6 54.4 %shard_map.315 = (bf16[2,3,128,768]{3,2,1,0:T(8,128)(2,1)}, bf16[2,2,768,768]{3,2,1,0:T(8,128)(2,1)}, bf16[2,3,64,384]{3,2,1,0:T(8,128)(2,1)}, bf16[2,3,64,768]{...) custom-call(bf16[2,768,768]{2,1,0:T(8,128)(2,1)} %bitcast.8, ...), custom_call_target="tpu_custom_call" | custom-call | tf_op jit(solution)/shard_map/pallas_call | solution.py:800
  145.0 95.7 %shard_map.316 = (bf16[2,3,128,768]{3,2,1,0:T(8,128)(2,1)}, f32[96,192]{1,0:T(8,128)}, f32[96,192]{1,0:T(8,128)}, f32[96,192]{1,0:T(8,128)}, f32[192,96]{1,0:T(8...) custom-call(bf16[2,2,4,2,96,768]{5,4,3,2,1,0:T(8,128)(2,1)} %bitcast, ...), custom_call_target="tpu_custom_call" | custom-call | tf_op jit(solution)/shard_map/pallas_call | solution.py:1259
  240.7 3.9 %shard_map.317 = (f32[768]{0:T(1024)}, f32[768]{0:T(1024)}, f32[768]{0:T(1024)}, f32[768]{0:T(1024)}, f32[768]{0:T(1024)}, /*index=5*/f32[768]{0:T(1024)}, f32[3...) custom-call(f32[768]{0:T(1024)} %get-tuple-element.89.refs_0_, ...), custom_call_target="tpu_custom_call" | custom-call | tf_op jit(solution)/shard_map/pallas_call | solution.py:1364
  (3 shorter events, 0.0 us)

commit v7 on v6

--- a/solution.py
+++ b/solution.py
@@ -645,18 +645,14 @@
     other_listed = send(hc.at[0], hc.at[1], sibling_peer)
     fill_w.wait()
 
-    def gelu_rows(i, carry):
-        at = pl.ds(pl.multiple_of(16 * i, 16), 16)
-        t = pre[at, :]
-        act[0, at, :] = (t * gaussian_parts(t)[0]).astype(BF16)
-        return carry
-
     def feed(s, b):
         out = 0.0
         for p in range(2):
-            pre[0:half] = mm(hl[s, b], wf[p, 0]) + up_biases[p][3:4, :]
-            lax.fori_loop(0, half // 16, gelu_rows, 0, unroll=2)
-            out = out + mm_t(act[0, 0:half], wf[p, 1])
+            for i in range(3):
+                units = slice(width // 3 * i, width // 3 * (i + 1))
+                t = mm(hl[s, b], wf[p, 0, :, units]) + up_biases[p][3:4, units]
+                low = (t * gaussian_parts(t)[0]).astype(BF16)
+                out = out + mm_t(low, wf[p, 1, :, units])
         return out
 
     def feed_other(b, carry):

time: 245 us -> 242 us (0.988)
  Pallas kernels: 242 us -> 238 us
    pallas_call x1, Pallas kernels: 54.4 us -> 50.5 us  [middle(): pl.pallas_call(middle_kernel, out_shape=[out(2, blocks, quarter, width),...]
where the time goes in v7:
time: 242 us; the launch traced here: 241 us
  Pallas kernels  238 us (98%)
    pallas_call x1, Pallas kernels, backward(): pl.pallas_call(functools.partial(back_kernel, True), out_shape=[out(2, bl...  95.7 us
    pallas_call x1, Pallas kernels, forward(): pl.pallas_call(functools.partial(forward_kernel, True), out_shape=shapes,...  87.8 us
    pallas_call x1, Pallas kernels, middle(): pl.pallas_call(middle_kernel, out_shape=[out(2, blocks, quarter, width),...  50.5 us

profile of v7, /device:TPU:0, one launch (start us, length us, event | category | flops | bytes accessed | tf_op | source)
XLA Modules:
  0.0 240.8 jit_solution(14758511795132339857)
XLA Ops:
  0.7 0.7 convert_element_type.3
  1.3 0.9 concatenate.3
  2.2 0.6 reshape.56.refs_7_.small_ref.refs_12_
  2.9 87.8 %shard_map.314 = (bf16[2,4,2,96,768]{4,3,2,1,0:T(8,128)(2,1)}, bf16[2,2,4,2,96,768]{5,4,3,2,1,0:T(8,128)(2,1)}, bf16[2,3,2,128,768]{4,3,2,1,0:T(8,128)(2,1)}, bf...) custom-call(bf16[96,192]{1,0:T(8,128)(2,1)} %refs_0_.1, ...), custom_call_target="tpu_custom_call" | custom-call | tf_op jit(solution)/shard_map/pallas_call | solution.py:496
  90.6 50.5 %shard_map.315 = (bf16[2,3,128,768]{3,2,1,0:T(8,128)(2,1)}, bf16[2,2,768,768]{3,2,1,0:T(8,128)(2,1)}, bf16[2,3,64,384]{3,2,1,0:T(8,128)(2,1)}, bf16[2,3,64,768]{...) custom-call(bf16[2,768,768]{2,1,0:T(8,128)(2,1)} %bitcast.8, ...), custom_call_target="tpu_custom_call" | custom-call | tf_op jit(solution)/shard_map/pallas_call | solution.py:796
  141.1 95.7 %shard_map.316 = (bf16[2,3,128,768]{3,2,1,0:T(8,128)(2,1)}, f32[96,192]{1,0:T(8,128)}, f32[96,192]{1,0:T(8,128)}, f32[96,192]{1,0:T(8,128)}, f32[192,96]{1,0:T(8...) custom-call(bf16[2,2,4,2,96,768]{5,4,3,2,1,0:T(8,128)(2,1)} %bitcast, ...), custom_call_target="tpu_custom_call" | custom-call | tf_op jit(solution)/shard_map/pallas_call | solution.py:1255
  236.8 3.9 %shard_map.317 = (f32[768]{0:T(1024)}, f32[768]{0:T(1024)}, f32[768]{0:T(1024)}, f32[768]{0:T(1024)}, f32[768]{0:T(1024)}, /*index=5*/f32[768]{0:T(1024)}, f32[3...) custom-call(f32[768]{0:T(1024)} %get-tuple-element.89.refs_0_, ...), custom_call_target="tpu_custom_call" | custom-call | tf_op jit(solution)/shard_map/pallas_call | solution.py:1360
  (3 shorter events, 0.0 us)
